TPU v7x, 32 devices: a whole 2x2x4 slice. The times are simulated.
32 devices in a mesh: row: 4 (over y, x), col: 8 (over z, core).
Axes of the slice: x: 2, y: 2, z: 4, core: 2. Of those that a mesh axis runs over, the one named last changes fastest.
Arguments:
- features: bfloat16 [16384, 256], P(('row', 'col')), may hold values from -6 to 6
- weight: bfloat16 [256, 256], replicated, may hold values from -0.375 to 0.375
- bias_vector: float32 [256], replicated, may hold values from -3 to 3
- send_rows: int32 [4, 8, 8, 256], P('row', 'col'), may hold values from 0 to 511
- send_count: int32 [4, 8, 8], P('row', 'col'), may hold values from 1 to 256, as said below
- adjacency: bfloat16 [4, 8, 16, 16, 128, 128], P('row', 'col'), may hold values from 0 to 0.099609375
- source_tile: int32 [4, 8, 16, 16], P('row', 'col'), may hold values from 0 to 15, as said below
- tile_count: int32 [4, 8, 16], P('row', 'col'), may hold values from 1 to 16, as said below
- cotangent: bfloat16 [16384, 256], P(('row', 'col')), may hold values from -6 to 6
Outputs:
- output: bfloat16 [16384, 256], P(('row', 'col'))
- input_grad: bfloat16 [16384, 256], P(('row', 'col'))
- weight_grad: float32 [256, 256], replicated
- bias_grad: float32 [256], replicated
Inputs may be any that keep to these rules, and one draw needn't show every extreme that they name: `send_rows`: rows of one list may repeat. `send_count`: in every grid row some grid column receives 256 rows from every piece of that grid row. `source_tile`: the 16 slots of one target tile read distinct boundary tiles. `tile_count`: slots at or beyond the count are ignored.
All inputs are finite; a program needn't handle non-finite values.
Results may differ from a plain program's by a relative error of at most 0.0063.
Values may be sent and summed in bfloat16 or wider, within the bound.
No kernel may reach another device: no remote copies, remote signals or barrier semaphores. Data moves between devices by JAX's collectives and lax.ppermute only.
A program may use at most 192 MiB of HBM per device.

v0:
```python
import math

import jax
import jax.numpy as jnp
from jax import lax
from jax.sharding import PartitionSpec as P

TILE = 128
SLOTS = 16


def slice_tiles(tiles_here, source_index, slot_counts):
    return (tiles_here, source_index, slot_counts)


def forward_rows(source_rows, tiles_here, source_index, slot_counts, number):
    tiles_part, index_part, counts_part = slice_tiles(tiles_here, source_index, slot_counts)
    width = source_rows.shape[2]
    live_mask = jnp.arange(SLOTS)[None, :] < counts_part[:, None]
    masked = jnp.where(live_mask[:, :, None, None], tiles_part, jnp.zeros((), tiles_part.dtype))
    total = jnp.einsum(
        "tsab,tsbf->taf", masked, source_rows[index_part], preferred_element_type=jnp.float32
    )
    return total.reshape(number * TILE, width)


def per_device(
    features,
    weight,
    bias_vector,
    send_rows,
    send_count,
    adjacency,
    source_tile,
    tile_count,
    cotangent,
):
    list_rows = send_rows[0, 0]
    list_counts = send_count[0, 0]
    tiles_here = adjacency[0, 0]
    source_index = source_tile[0, 0]
    slot_counts = tile_count[0, 0]
    columns = list_rows.shape[0]
    capacity = list_rows.shape[1]
    node_dev = features.shape[0]
    target_tiles = tiles_here.shape[0]
    list_live = jnp.arange(capacity)[None, :] < list_counts[:, None]
    outgoing = jnp.where(list_live[:, :, None], features[list_rows], jnp.zeros((), features.dtype))
    received = lax.all_to_all(outgoing, "col", split_axis=0, concat_axis=0, tiled=True)
    source_rows = received.reshape(-1, TILE, received.shape[2])
    partial_sum = forward_rows(source_rows, tiles_here, source_index, slot_counts, target_tiles)
    summed = lax.psum_scatter(partial_sum, "row", scatter_dimension=0, tiled=True)
    aggregate = summed.astype(jnp.bfloat16)
    preact = jnp.dot(aggregate, weight, preferred_element_type=jnp.float32) + bias_vector
    output = jax.nn.silu(preact).astype(jnp.bfloat16)
    sigmoid_pre = jax.nn.sigmoid(preact)
    grad_pre = (
        cotangent.astype(jnp.float32) * sigmoid_pre * (1.0 + preact * (1.0 - sigmoid_pre))
    ).astype(jnp.bfloat16)
    weight_local = jnp.einsum("nf,ng->fg", aggregate, grad_pre, preferred_element_type=jnp.float32)
    bias_local = jnp.sum(grad_pre.astype(jnp.float32), axis=0)
    weight_sum, bias_sum = lax.psum((weight_local, bias_local), ("row", "col"))
    scale = 1.0 / math.sqrt(node_dev * lax.axis_size("row") * lax.axis_size("col"))
    weight_grad = weight_sum * scale
    bias_grad = bias_sum * scale
    back = jnp.einsum("ng,fg->nf", grad_pre, weight, preferred_element_type=jnp.float32).astype(
        jnp.bfloat16
    )
    width = back.shape[1]
    initial = jnp.zeros((columns * capacity // TILE, TILE, width), jnp.float32)
    shard_rows = lax.all_gather(back, "row", axis=0, tiled=True)
    number = shard_rows.shape[0] // TILE
    blocks = shard_rows.reshape(number, TILE, width)
    tiles_part, index_part, counts_part = slice_tiles(tiles_here, source_index, slot_counts)
    slot_limit = SLOTS

    def add_slot(slot_index, total):
        tile_block = lax.dynamic_index_in_dim(tiles_part, slot_index, 1, keepdims=False)
        live_mask = (slot_index < counts_part)[:, None, None]
        tile_block = jnp.where(live_mask, tile_block, jnp.zeros((), tile_block.dtype))
        contrib = jnp.einsum("tab,taf->tbf", tile_block, blocks, preferred_element_type=jnp.float32)
        target_index = lax.dynamic_index_in_dim(index_part, slot_index, 1, keepdims=False)
        return total.at[target_index].add(contrib)

    grads = lax.fori_loop(0, slot_limit, add_slot, initial)
    grads = grads.reshape(columns, capacity, width)
    arrived = lax.all_to_all(grads, "col", split_axis=0, concat_axis=0, tiled=True)
    block_width = arrived.shape[2]
    kept = jnp.where(list_live[:, :, None], arrived, jnp.zeros((), jnp.float32))
    input_grad = (
        jnp.zeros((node_dev, block_width), jnp.float32)
        .at[list_rows.reshape(-1)]
        .add(kept.reshape(-1, block_width))
        .astype(jnp.bfloat16)
    )
    return (output, input_grad, weight_grad, bias_grad)


def solution(mesh):
    in_specs = (
        P(("row", "col"), None),
        P(),
        P(),
        P("row", "col", None, None),
        P("row", "col", None),
        P("row", "col", None, None, None, None),
        P("row", "col", None, None),
        P("row", "col", None),
        P(("row", "col"), None),
    )
    out_specs = (P(("row", "col"), None), P(("row", "col"), None), P(), P())
    return jax.shard_map(
        per_device, mesh=mesh, in_specs=in_specs, out_specs=out_specs, check_vma=False
    )
```

profile of v0, /device:TPU:0, one launch (start us, length us, event | category | flops | bytes accessed | tf_op | source)
XLA Modules:
  0.0 404.8 jit_solution(13614778437504613898)
XLA Ops:
  8.7 7.5 %gather_fusion = bf16[2048,256]{1,0:T(8,128)(2,1)S(1)} fusion(bf16[512,256]{1,0:T(8,128)(2,1)S(1)} %copy-done, s32[2048]{0:T(1024)S(1)} %broadcast_clamp_fusion), kind=kCustom, calls=%fused_computation | custom fusion | bytes 2105344 | tf_op jit(solution)/shard_map/gather | solution.py:48
  17.5 6.3 %all-to-all-start = ((bf16[8,256,256]{2,1,0:T(8,128)(2,1)}), bf16[8,256,256]{2,1,0:T(8,128)(2,1)S(1)}, u32[]{:S(2)}, u32[]{:S(2)}) async-start(bf16[8,256,256]{2,1,0:T(8,128)(2,1)} %broadcast_select_fusion.1), calls=%async_computation | async-start | bytes 2097152 | tf_op jit(solution)/shard_map/all_to_all | solution.py:49
  24.0 12.3 %copy.16 = bf16[1,1,16,16,128,128]{4,5,2,3,1,0:T(8,128)(2,1)} copy(bf16[1,1,16,16,128,128]{5,4,3,2,1,0:T(8,128)(2,1)} %param.16) | data formatting | bytes 16777216 | tf_op args[5]
  36.3 14.1 %all-to-all-done = bf16[8,256,256]{2,1,0:T(8,128)(2,1)S(1)} async-done(((bf16[8,256,256]{2,1,0:T(8,128)(2,1)}), bf16[8,256,256]{2,1,0:T(8,128)(2,1)S(1)}, u32[]{:S(2)}, u32[]{:S(2)}) %all-to-all-start) | async-done | bytes 1048608 | tf_op jit(solution)/shard_map/all_to_all | solution.py:49
  50.4 9.7 %gather_fusion.1 = bf16[256,128,256]{2,1,0:T(8,128)(2,1)} fusion(bf16[16,128,256]{2,1,0:T(8,128)(2,1)S(1)} %bitcast.48, s32[1024]{0:T(1024)S(1)} %pad_clamp_fusion), kind=kCustom, calls=%fused_computation.1 | custom fusion | bytes 33555456 | tf_op jit(solution)/shard_map/gather | solution.py:22
  60.1 11.6 %fusion.7 = f32[16,128,256,1]{2,1,0,3:T(8,128)} fusion(bf16[16,16,128,256]{3,2,1,0:T(8,128)(2,1)} %bitcast.51, pred[16,16]{0,1:T(8,128)(4,1)S(1)} %iota_compare_fusion.1, bf16[1,1,16,16,128,128]{4,5,2,3,1,0:T(8,128)(2,1)} %copy.16), kind=kOutput, calls=%fused_computation.14 | convolution fusion | flops 2151677952 | bytes 27263232 | tf_op jit(solution)/shard_map/tsab,tsbf->taf/dot_general | solution.py:21
  71.8 34.2 %reduce-scatter.2.cloned.1.call-done = f32[512,256]{1,0:T(8,128)} async-done(((f32[2048,256]{1,0:T(8,128)}), f32[512,256]{1,0:T(8,128)}) %reduce-scatter.2.cloned.1.call-update) | async-done | bytes 524304 | tf_op jit(solution)/shard_map/reduce_scatter | solution.py:52
  106.0 2.2 convert_reduce_fusion
  109.9 26.7 %all-gather.2.cloned.1.call-done = bf16[2048,256]{1,0:T(8,128)(2,1)} async-done(((bf16[512,256]{1,0:T(8,128)(2,1)}), bf16[2048,256]{1,0:T(8,128)(2,1)}) %all-gather.2.cloned.1.call-update) | async-done | bytes 1048592 | tf_op jit(solution)/shard_map/all_gather | solution.py:71
  138.2 95.2 %while.13 = (s32[]{:T(128)}, f32[16,128,256]{2,1,0:T(8,128)}, s32[16,16]{0,1:T(8,128)S(1)}, s32[16]{0:T(128)S(1)}, bf16[16,16,128,128]{2,3,0,1:T(8,128)(2,1)}, /*index=5*/bf16[16,128,256]{2,1,0:T(8,128)(2,1)S(1)}, s32[]{:T(128)}) while((s32[]{:T(128)}, f32[16,128,256]{2,1,0:T(8,128)}, s32[16,16]{0,1:T(8,128)S(1)}, s32[16]{0:T(128)S(1)}, ...), condition=%wide.region_3.4_spmd, body=%wide.region_1.3_spmd.sunk | while | flops 135004224 | bytes 9962357 | solution.py:85
  139.8 4.3 %scatter_fusion = f32[16,128,256]{2,1,0:T(8,128)} fusion(f32[16,128,256]{2,1,0:T(8,128)} %get-tuple-element.174, s32[16]{0:T(128)S(1)} %fusion.29, f32[16,128,256]{2,1,0:T(8,128)S(1)} %fusion.30), kind=kCustom, calls=%fused_computation.2.clone.1 | custom fusion | flops 524288 | bytes 6291520 | tf_op jit(solution)/shard_map/while/body/eval_jaxpr/scatter-add | solution.py:83
  145.6 4.3 %scatter_fusion = f32[16,128,256]{2,1,0:T(8,128)} fusion(f32[16,128,256]{2,1,0:T(8,128)} %get-tuple-element.174, s32[16]{0:T(128)S(1)} %fusion.29, f32[16,128,256]{2,1,0:T(8,128)S(1)} %fusion.30), kind=kCustom, calls=%fused_computation.2.clone.1 | custom fusion | flops 524288 | bytes 6291520 | tf_op jit(solution)/shard_map/while/body/eval_jaxpr/scatter-add | solution.py:83
  151.5 4.4 %scatter_fusion = f32[16,128,256]{2,1,0:T(8,128)} fusion(f32[16,128,256]{2,1,0:T(8,128)} %get-tuple-element.174, s32[16]{0:T(128)S(1)} %fusion.29, f32[16,128,256]{2,1,0:T(8,128)S(1)} %fusion.30), kind=kCustom, calls=%fused_computation.2.clone.1 | custom fusion | flops 524288 | bytes 6291520 | tf_op jit(solution)/shard_map/while/body/eval_jaxpr/scatter-add | solution.py:83
  157.5 4.5 %scatter_fusion = f32[16,128,256]{2,1,0:T(8,128)} fusion(f32[16,128,256]{2,1,0:T(8,128)} %get-tuple-element.174, s32[16]{0:T(128)S(1)} %fusion.29, f32[16,128,256]{2,1,0:T(8,128)S(1)} %fusion.30), kind=kCustom, calls=%fused_computation.2.clone.1 | custom fusion | flops 524288 | bytes 6291520 | tf_op jit(solution)/shard_map/while/body/eval_jaxpr/scatter-add | solution.py:83
  163.5 4.5 %scatter_fusion = f32[16,128,256]{2,1,0:T(8,128)} fusion(f32[16,128,256]{2,1,0:T(8,128)} %get-tuple-element.174, s32[16]{0:T(128)S(1)} %fusion.29, f32[16,128,256]{2,1,0:T(8,128)S(1)} %fusion.30), kind=kCustom, calls=%fused_computation.2.clone.1 | custom fusion | flops 524288 | bytes 6291520 | tf_op jit(solution)/shard_map/while/body/eval_jaxpr/scatter-add | solution.py:83
  169.5 4.4 %scatter_fusion = f32[16,128,256]{2,1,0:T(8,128)} fusion(f32[16,128,256]{2,1,0:T(8,128)} %get-tuple-element.174, s32[16]{0:T(128)S(1)} %fusion.29, f32[16,128,256]{2,1,0:T(8,128)S(1)} %fusion.30), kind=kCustom, calls=%fused_computation.2.clone.1 | custom fusion | flops 524288 | bytes 6291520 | tf_op jit(solution)/shard_map/while/body/eval_jaxpr/scatter-add | solution.py:83
  175.5 4.5 %scatter_fusion = f32[16,128,256]{2,1,0:T(8,128)} fusion(f32[16,128,256]{2,1,0:T(8,128)} %get-tuple-element.174, s32[16]{0:T(128)S(1)} %fusion.29, f32[16,128,256]{2,1,0:T(8,128)S(1)} %fusion.30), kind=kCustom, calls=%fused_computation.2.clone.1 | custom fusion | flops 524288 | bytes 6291520 | tf_op jit(solution)/shard_map/while/body/eval_jaxpr/scatter-add | solution.py:83
  181.5 4.4 %scatter_fusion = f32[16,128,256]{2,1,0:T(8,128)} fusion(f32[16,128,256]{2,1,0:T(8,128)} %get-tuple-element.174, s32[16]{0:T(128)S(1)} %fusion.29, f32[16,128,256]{2,1,0:T(8,128)S(1)} %fusion.30), kind=kCustom, calls=%fused_computation.2.clone.1 | custom fusion | flops 524288 | bytes 6291520 | tf_op jit(solution)/shard_map/while/body/eval_jaxpr/scatter-add | solution.py:83
  187.5 4.4 %scatter_fusion = f32[16,128,256]{2,1,0:T(8,128)} fusion(f32[16,128,256]{2,1,0:T(8,128)} %get-tuple-element.174, s32[16]{0:T(128)S(1)} %fusion.29, f32[16,128,256]{2,1,0:T(8,128)S(1)} %fusion.30), kind=kCustom, calls=%fused_computation.2.clone.1 | custom fusion | flops 524288 | bytes 6291520 | tf_op jit(solution)/shard_map/while/body/eval_jaxpr/scatter-add | solution.py:83
  193.4 4.4 %scatter_fusion = f32[16,128,256]{2,1,0:T(8,128)} fusion(f32[16,128,256]{2,1,0:T(8,128)} %get-tuple-element.174, s32[16]{0:T(128)S(1)} %fusion.29, f32[16,128,256]{2,1,0:T(8,128)S(1)} %fusion.30), kind=kCustom, calls=%fused_computation.2.clone.1 | custom fusion | flops 524288 | bytes 6291520 | tf_op jit(solution)/shard_map/while/body/eval_jaxpr/scatter-add | solution.py:83
  199.3 4.5 %scatter_fusion = f32[16,128,256]{2,1,0:T(8,128)} fusion(f32[16,128,256]{2,1,0:T(8,128)} %get-tuple-element.174, s32[16]{0:T(128)S(1)} %fusion.29, f32[16,128,256]{2,1,0:T(8,128)S(1)} %fusion.30), kind=kCustom, calls=%fused_computation.2.clone.1 | custom fusion | flops 524288 | bytes 6291520 | tf_op jit(solution)/shard_map/while/body/eval_jaxpr/scatter-add | solution.py:83
  205.3 4.3 %scatter_fusion = f32[16,128,256]{2,1,0:T(8,128)} fusion(f32[16,128,256]{2,1,0:T(8,128)} %get-tuple-element.174, s32[16]{0:T(128)S(1)} %fusion.29, f32[16,128,256]{2,1,0:T(8,128)S(1)} %fusion.30), kind=kCustom, calls=%fused_computation.2.clone.1 | custom fusion | flops 524288 | bytes 6291520 | tf_op jit(solution)/shard_map/while/body/eval_jaxpr/scatter-add | solution.py:83
  211.2 4.4 %scatter_fusion = f32[16,128,256]{2,1,0:T(8,128)} fusion(f32[16,128,256]{2,1,0:T(8,128)} %get-tuple-element.174, s32[16]{0:T(128)S(1)} %fusion.29, f32[16,128,256]{2,1,0:T(8,128)S(1)} %fusion.30), kind=kCustom, calls=%fused_computation.2.clone.1 | custom fusion | flops 524288 | bytes 6291520 | tf_op jit(solution)/shard_map/while/body/eval_jaxpr/scatter-add | solution.py:83
  217.2 4.4 %scatter_fusion = f32[16,128,256]{2,1,0:T(8,128)} fusion(f32[16,128,256]{2,1,0:T(8,128)} %get-tuple-element.174, s32[16]{0:T(128)S(1)} %fusion.29, f32[16,128,256]{2,1,0:T(8,128)S(1)} %fusion.30), kind=kCustom, calls=%fused_computation.2.clone.1 | custom fusion | flops 524288 | bytes 6291520 | tf_op jit(solution)/shard_map/while/body/eval_jaxpr/scatter-add | solution.py:83
  223.1 4.4 %scatter_fusion = f32[16,128,256]{2,1,0:T(8,128)} fusion(f32[16,128,256]{2,1,0:T(8,128)} %get-tuple-element.174, s32[16]{0:T(128)S(1)} %fusion.29, f32[16,128,256]{2,1,0:T(8,128)S(1)} %fusion.30), kind=kCustom, calls=%fused_computation.2.clone.1 | custom fusion | flops 524288 | bytes 6291520 | tf_op jit(solution)/shard_map/while/body/eval_jaxpr/scatter-add | solution.py:83
  229.1 4.4 %scatter_fusion = f32[16,128,256]{2,1,0:T(8,128)} fusion(f32[16,128,256]{2,1,0:T(8,128)} %get-tuple-element.174, s32[16]{0:T(128)S(1)} %fusion.29, f32[16,128,256]{2,1,0:T(8,128)S(1)} %fusion.30), kind=kCustom, calls=%fused_computation.2.clone.1 | custom fusion | flops 524288 | bytes 6291520 | tf_op jit(solution)/shard_map/while/body/eval_jaxpr/scatter-add | solution.py:83
  233.5 4.6 %all-to-all-start.1 = ((f32[8,256,256]{2,1,0:T(8,128)}), f32[8,256,256]{2,1,0:T(8,128)S(1)}, u32[]{:S(2)}, u32[]{:S(2)}) async-start(f32[8,256,256]{2,1,0:T(8,128)} %bitcast.49), calls=%async_computation.2 | async-start | bytes 4194304 | tf_op jit(solution)/shard_map/all_to_all | solution.py:87
  239.1 68.6 %psum.15 = f32[256]{0:T(256)S(1)} all-reduce(f32[256]{0:T(256)S(1)} %get-tuple-element.126), channel_id=1, replica_groups=mesh['row'=4,'col'=8] {'row','col'}, use_global_device_ids=true, to_apply=%region_7.8 | all-reduce | flops 256 | bytes 2048 | tf_op jit(solution)/shard_map/psum | solution.py:62
  308.3 73.7 %all-reduce.2.cloned.1.call-done = f32[256,256]{1,0:T(8,128)} async-done(((f32[256,256]{1,0:T(8,128)}), f32[256,256]{1,0:T(8,128)}) %all-reduce.2.cloned.1.call-update) | async-done | bytes 262160 | tf_op jit(solution)/shard_map/psum | solution.py:62
  382.1 1.7 broadcast_multiply_fusion
  383.8 1.7 broadcast_select_fusion
  385.4 12.1 %scatter_custom_fusion.1 = f32[512,256]{1,0:T(8,128)S(1)} fusion(s32[2048]{0:T(1024)S(1)} %bitcast.59, f32[2048,256]{1,0:T(8,128)} %bitcast.55, f32[]{:T(128)} %constant.58.clone.1), kind=kCustom, calls=%fused_computation.27 | custom fusion | flops 524288 | bytes 524800 | tf_op jit(solution)/shard_map/scatter-add | solution.py:93
  (94 shorter events, 33.3 us)
Async XLA Ops:
  7.2 1.5 copy-start
  16.2 7.7 %copy-start.6 = (s32[1,1,16,16]{3,2,1,0:T(8,128)S(1)}, s32[1,1,16,16]{3,2,1,0:T(8,128)}, u32[]{:S(2)}) copy-start(s32[1,1,16,16]{3,2,1,0:T(8,128)} %param.17) | copy-start | bytes 3076
  17.5 32.9 %all-to-all-start = ((bf16[8,256,256]{2,1,0:T(8,128)(2,1)}), bf16[8,256,256]{2,1,0:T(8,128)(2,1)S(1)}, u32[]{:S(2)}, u32[]{:S(2)}) async-start(bf16[8,256,256]{2,1,0:T(8,128)(2,1)} %broadcast_select_fusion.1), calls=%async_computation | async-start | bytes 2097152 | tf_op jit(solution)/shard_map/all_to_all | solution.py:49
  23.8 82.2 %reduce-scatter.2.cloned.1.call-start = ((), (), s32[]{:S(2)}) async-start(), calls=%async_computation.3 | async-start | bytes 2621440 | tf_op jit(solution)/shard_map/reduce_scatter | solution.py:52
  24.0 12.4 %copy-start.8 = (s32[1,1,16]{2,1,0:T(1,128)S(1)}, s32[1,1,16]{2,1,0:T(1,128)}, u32[]{:S(2)}) copy-start(s32[1,1,16]{2,1,0:T(1,128)} %param.18) | copy-start | bytes 196
  71.7 34.3 %copy-start.5 = (bf16[256,256]{1,0:T(8,128)(2,1)S(1)}, bf16[256,256]{1,0:T(8,128)(2,1)}, u32[]{:S(2)}) copy-start(bf16[256,256]{1,0:T(8,128)(2,1)} %param.12) | copy-start | bytes 393220
  71.7 34.3 %copy-start.9 = (bf16[512,256]{1,0:T(8,128)(2,1)S(1)}, bf16[512,256]{1,0:T(8,128)(2,1)}, u32[]{:S(2)}) copy-start(bf16[512,256]{1,0:T(8,128)(2,1)} %param.19) | copy-start | bytes 786436
  71.7 34.3 %copy-start.10 = (f32[256]{0:T(256)S(1)}, f32[256]{0:T(256)}, u32[]{:S(2)}) copy-start(f32[256]{0:T(256)} %param.13) | copy-start | bytes 3076
  71.7 65.0 %all-gather.2.cloned.1.call-start = ((), (), s32[]{:S(2)}) async-start(), calls=%async_computation.4 | async-start | bytes 1310720 | tf_op jit(solution)/shard_map/all_gather | solution.py:71
  108.2 0.7 copy-start.2
  136.7 1.6 copy-start.1
  233.5 4.6 %copy-start.7 = (s32[1,1,8,256]{3,2,1,0:T(8,128)S(1)}, s32[1,1,8,256]{3,2,1,0:T(8,128)}, u32[]{:S(2)}) copy-start(s32[1,1,8,256]{3,2,1,0:T(8,128)} %param.14) | copy-start | bytes 24580
  233.5 4.6 %copy-start.3 = (bf16[512,256]{1,0:T(8,128)(2,1)S(1)}, bf16[512,256]{1,0:T(8,128)(2,1)}, u32[]{:S(2)}) copy-start(bf16[512,256]{1,0:T(8,128)(2,1)} %copy-done.2) | copy-start | bytes 786436
  233.5 4.7 %copy-start.4 = (f32[512,256]{1,0:T(8,128)S(1)}, f32[512,256]{1,0:T(8,128)}, u32[]{:S(2)}) copy-start(f32[512,256]{1,0:T(8,128)} %reduce-scatter.2.cloned.1.call-done) | copy-start | bytes 1572868
  233.5 150.3 %all-to-all-start.1 = ((f32[8,256,256]{2,1,0:T(8,128)}), f32[8,256,256]{2,1,0:T(8,128)S(1)}, u32[]{:S(2)}, u32[]{:S(2)}) async-start(f32[8,256,256]{2,1,0:T(8,128)} %bitcast.49), calls=%async_computation.2 | async-start | bytes 4194304 | tf_op jit(solution)/shard_map/all_to_all | solution.py:87
  238.0 144.1 %all-reduce.2.cloned.1.call-start = ((), (), s32[]{:S(2)}) async-start(), calls=%async_computation.5 | async-start | bytes 524288 | tf_op jit(solution)/shard_map/psum | solution.py:62
Sparse Core Ops, SparseCore 0:
  71.8 34.1 reduce-scatter.1
  110.0 26.6 all-gather.1
  245.8 136.1 all-reduce.1
where the time goes:
time: 407 us; the launch traced here: 405 us
  waiting for transfers between devices  149 us (37%)
  other arithmetic  90.2 us (22%)
  blocking collectives  68.6 us (17%)
  matrix products  40 us (10%)
  local copies, waits for them, and re-layouts  32 us (8%)
  between operations  13.9 us (3%)
  starting transfers between devices  11 us (3%)
    psum x1, waiting for transfers between devices, per_device(): weight_sum, bias_sum = lax.psum((weight_local, bias_local), ('row', 'col'))  73.7 us
    scatter-add x16, other arithmetic, add_slot(): return total.at[target_index].add(contrib)  70.3 us
    psum x1, blocking collectives, per_device(): weight_sum, bias_sum = lax.psum((weight_local, bias_local), ('row', 'col'))  68.6 us
    reduce_scatter x1, waiting for transfers between devices, per_device(): lax.psum_scatter(partial_sum, 'row', scatter_dimension=0, tiled=True)  34.2 us
    all_gather x1, waiting for transfers between devices, per_device(): shard_rows = lax.all_gather(back, 'row', axis=0, tiled=True)  26.7 us
    dot_general x16, matrix products, add_slot(): jnp.einsum('tab,taf->tbf', tile_block, blocks, preferred_element_type=jnp...  24.3 us
    all_to_all x1, waiting for transfers between devices, per_device(): lax.all_to_all(outgoing, 'col', split_axis=0, concat_axis=0, tiled=True)  14.1 us
    unnamed x26, local copies, waits for them, and re-layouts  13.2 us
  transfers between devices with their start and end apart: 5, of which 4 were waited for; matrix products, arithmetic and copies ran while one was open for 4% of the time, Pallas kernels for 0%

commit v1 on v0

v1 whole, which is shorter than its diff:
```python
import functools
import math

import jax
import jax.numpy as jnp
from jax import lax
from jax.experimental import pallas as pl
from jax.experimental.pallas import tpu as pltpu
from jax.sharding import PartitionSpec as P

TILE = 128
CHUNK = 128
VMEM_LIMIT = 40 * 1024 * 1024
BF16 = jnp.bfloat16
F32 = jnp.float32


def full_spec(shape):
    return pl.BlockSpec(shape, lambda *_: (0,) * len(shape))


def params(limit=VMEM_LIMIT):
    return pltpu.CompilerParams(vmem_limit_bytes=limit)


def xor_pairs(size, step):
    return [(i, i ^ step) for i in range(size)]


def z_pairs(pairs):
    return [(2 * a + core, 2 * b + core) for a, b in pairs for core in range(2)]


def densify_kernel(per_piece, src_ref, cnt_ref, pos_ref, adj_ref, out_ref):
    step = pl.program_id(0)
    tiles, slots = adj_ref.shape[0], adj_ref.shape[1]
    out_ref[...] = jnp.zeros_like(out_ref)
    here = pos_ref[1]
    for t in range(tiles):
        count = cnt_ref[step * tiles + t]
        for s in range(slots):

            @pl.when(s < count)
            def _(t=t, s=s):
                source = src_ref[step * tiles + t, s]
                slot = (source // per_piece) ^ here
                column = pl.multiple_of((slot * per_piece + source % per_piece) * TILE, TILE)
                out_ref[t * TILE : (t + 1) * TILE, pl.ds(column, TILE)] = adj_ref[t, s]


def densify(adjacency, source_tile, tile_count, pos, pieces, capacity):
    targets, slots = adjacency.shape[0], adjacency.shape[1]
    tiles = 4
    width = pieces * capacity
    return pl.pallas_call(
        functools.partial(densify_kernel, capacity // TILE),
        out_shape=jax.ShapeDtypeStruct((targets * TILE, width), BF16),
        grid_spec=pltpu.PrefetchScalarGridSpec(
            num_scalar_prefetch=3,
            grid=(targets // tiles,),
            in_specs=[pl.BlockSpec((tiles, slots, TILE, TILE), lambda i, *_: (i, 0, 0, 0))],
            out_specs=pl.BlockSpec((tiles * TILE, width), lambda i, *_: (i, 0)),
        ),
        compiler_params=params(),
        cost_estimate=pl.CostEstimate(
            flops=0, bytes_accessed=2 * targets * TILE * (width + slots * TILE), transcendentals=0
        ),
        name="densify",
    )(source_tile, tile_count, pos, adjacency)


def select_kernel(pos_ref, list_ref, pick_ref, put_ref):
    slot = pl.program_id(0)
    row = list_ref[pl.ds(slot ^ pos_ref[1], 1), :]
    nodes = put_ref.shape[1]
    hit = lax.broadcasted_iota(jnp.int32, (nodes, row.shape[1]), 0) == row
    put = jnp.where(hit, 1.0, 0.0).astype(BF16)
    put_ref[0] = put
    pick_ref[0] = put.T


def selectors(lists, pos, nodes):
    pieces, capacity = lists.shape
    return pl.pallas_call(
        select_kernel,
        out_shape=(
            jax.ShapeDtypeStruct((pieces, capacity, nodes), BF16),
            jax.ShapeDtypeStruct((pieces, nodes, capacity), BF16),
        ),
        grid_spec=pltpu.PrefetchScalarGridSpec(
            num_scalar_prefetch=1,
            grid=(pieces,),
            in_specs=[pl.BlockSpec((pieces, capacity), lambda i, *_: (0, 0))],
            out_specs=(
                pl.BlockSpec((1, capacity, nodes), lambda i, *_: (i, 0, 0)),
                pl.BlockSpec((1, nodes, capacity), lambda i, *_: (i, 0, 0)),
            ),
        ),
        compiler_params=params(),
        cost_estimate=pl.CostEstimate(
            flops=0, bytes_accessed=4 * pieces * capacity * nodes, transcendentals=0
        ),
        name="selectors",
    )(pos, lists)


def forward_kernel(groups, peers, pos_ref, pick_ref, dense_ref, *rest):
    total = sum(groups)
    sources, outs, gathered = rest[:total], rest[total : total + peers], rest[total + peers]
    step = pl.program_id(0)
    capacity = pick_ref.shape[1]

    @pl.when(step == 0)
    def _():
        at = 0
        for slot, count in enumerate(groups):
            piece = sources[at][...]
            for extra in range(1, count):
                piece = piece + sources[at + extra][...]
            at += count
            rows = jnp.dot(pick_ref[slot], piece, preferred_element_type=F32)
            gathered[slot * capacity : (slot + 1) * capacity, :] = rows.astype(BF16)

    result = jnp.dot(dense_ref[...], gathered[...], preferred_element_type=F32)
    for peer in range(peers):

        @pl.when(step == peer)
        def _(peer=peer):
            outs[peer][...] = result.astype(outs[peer].dtype)


def forward(dense, pick, groups, pos, peers):
    rows, width = dense.shape
    flat = [array for group in groups for array in group]
    nodes, chunk = flat[0].shape
    block = rows // peers
    return pl.pallas_call(
        functools.partial(forward_kernel, tuple(len(group) for group in groups), peers),
        out_shape=tuple(
            jax.ShapeDtypeStruct((block, chunk), F32 if peer == 0 else BF16)
            for peer in range(peers)
        ),
        grid_spec=pltpu.PrefetchScalarGridSpec(
            num_scalar_prefetch=1,
            grid=(peers,),
            in_specs=[
                full_spec(pick.shape),
                pl.BlockSpec((block, width), lambda i, pos_ref: (i ^ pos_ref[0], 0)),
            ]
            + [full_spec((nodes, chunk))] * len(flat),
            out_specs=tuple(full_spec((block, chunk)) for _ in range(peers)),
            scratch_shapes=[pltpu.VMEM((width, chunk), BF16)],
        ),
        compiler_params=params(),
        cost_estimate=pl.CostEstimate(
            flops=2 * rows * width * chunk, bytes_accessed=2 * rows * width, transcendentals=0
        ),
        name="forward_rows",
    )(pos, pick, dense, *flat)


def layer_kernel(chunks, peers, weight_ref, bias_ref, cot_ref, *rest):
    parts, outs = rest[: chunks * peers], rest[chunks * peers :]
    out_ref, agg_ref, grad_ref = outs[:3]
    columns = []
    for chunk in range(chunks):
        total = parts[chunk * peers][...].astype(F32)
        for peer in range(1, peers):
            total = total + parts[chunk * peers + peer][...].astype(F32)
        columns.append(total.astype(BF16))
    agg = jnp.concatenate(columns, axis=1) if chunks > 1 else columns[0]
    weight = weight_ref[...]
    preact = jnp.dot(agg, weight, preferred_element_type=F32) + bias_ref[...]
    sigma = 1.0 / (1.0 + jnp.exp(-preact))
    out_ref[...] = (preact * sigma).astype(BF16)
    grad = (cot_ref[...].astype(F32) * sigma * (1.0 + preact * (1.0 - sigma))).astype(BF16)
    agg_ref[...] = agg
    grad_ref[...] = grad
    back = lax.dot_general(
        weight, grad, (((1,), (1,)), ((), ())), preferred_element_type=F32
    ).astype(BF16)
    size = weight.shape[0] // chunks
    for chunk in range(chunks):
        outs[3 + chunk][...] = back[chunk * size : (chunk + 1) * size, :]


def layer(weight, bias_vector, cotangent, parts, chunks, peers):
    nodes, width = cotangent.shape
    size = width // chunks
    return pl.pallas_call(
        functools.partial(layer_kernel, chunks, peers),
        out_shape=(jax.ShapeDtypeStruct((nodes, width), BF16),) * 3
        + (jax.ShapeDtypeStruct((size, nodes), BF16),) * chunks,
        compiler_params=params(),
        cost_estimate=pl.CostEstimate(
            flops=4 * nodes * width * width,
            bytes_accessed=2 * nodes * width * 10,
            transcendentals=nodes * width,
        ),
        name="layer",
    )(weight, bias_vector.reshape(1, -1), cotangent, *parts)


def weights_kernel(agg_ref, grad_ref, top_ref, low_ref, bias_ref):
    grad = grad_ref[...]
    product = lax.dot_general(
        agg_ref[...], grad, (((0,), (0,)), ((), ())), preferred_element_type=F32
    )
    half = top_ref.shape[0]
    top_ref[...] = product[:half]
    low_ref[...] = product[half:]
    bias_ref[...] = jnp.sum(grad.astype(F32).reshape(-1, 8, grad.shape[1]), axis=0)


def weight_partials(agg, grad):
    nodes, width = agg.shape
    return pl.pallas_call(
        weights_kernel,
        out_shape=(
            jax.ShapeDtypeStruct((width // 2, width), F32),
            jax.ShapeDtypeStruct((width // 2, width), F32),
            jax.ShapeDtypeStruct((8, width), F32),
        ),
        compiler_params=params(),
        cost_estimate=pl.CostEstimate(
            flops=2 * nodes * width * width, bytes_accessed=6 * nodes * width, transcendentals=0
        ),
        name="weight_partials",
    )(agg, grad)


def backward_kernel(peers, slots, kept, pos_ref, put_ref, dense_ref, *rest):
    backs, outs, total = rest[:peers], rest[peers : peers + slots], rest[peers + slots]
    step = pl.program_id(0)
    capacity = put_ref.shape[2]
    for peer in range(peers):

        @pl.when(step == peer)
        def _(peer=peer):
            product = jnp.dot(backs[peer][...], dense_ref[...], preferred_element_type=F32)
            if peer == 0:
                total[...] = product
            else:
                total[...] += product

    @pl.when(step == peers - 1)
    def _():
        for slot in range(slots):
            rows = total[:, slot * capacity : (slot + 1) * capacity].astype(BF16)
            outs[slot][...] = lax.dot_general(
                put_ref[slot], rows, (((1,), (1,)), ((), ())), preferred_element_type=F32
            ).astype(outs[slot].dtype)


def backward(dense, put, backs, pos, kept):
    peers = len(backs)
    rows, width = dense.shape
    slots, nodes, _ = put.shape
    chunk = backs[0].shape[0]
    block = rows // peers
    return pl.pallas_call(
        functools.partial(backward_kernel, peers, slots, kept),
        out_shape=tuple(
            jax.ShapeDtypeStruct((nodes, chunk), F32 if slot in kept else BF16)
            for slot in range(slots)
        ),
        grid_spec=pltpu.PrefetchScalarGridSpec(
            num_scalar_prefetch=1,
            grid=(peers,),
            in_specs=[
                full_spec(put.shape),
                pl.BlockSpec((block, width), lambda i, pos_ref: (i ^ pos_ref[0], 0)),
            ]
            + [full_spec((chunk, block))] * peers,
            out_specs=tuple(full_spec((nodes, chunk)) for _ in range(slots)),
            scratch_shapes=[pltpu.VMEM((chunk, width), F32)],
        ),
        compiler_params=params(),
        cost_estimate=pl.CostEstimate(
            flops=2 * rows * width * chunk, bytes_accessed=2 * rows * width, transcendentals=0
        ),
        name="backward_rows",
    )(pos, put, dense, *backs)


def pair_sum_kernel(count, *refs):
    for i in range(count):
        total = refs[i][...].astype(F32) + refs[count + i][...].astype(F32)
        refs[2 * count + i][...] = total.astype(refs[2 * count + i].dtype)


def pair_sums(kept, received):
    count = len(kept)
    return pl.pallas_call(
        functools.partial(pair_sum_kernel, count),
        out_shape=tuple(
            jax.ShapeDtypeStruct(kept[i].shape, F32 if i == 0 else BF16) for i in range(count)
        ),
        compiler_params=params(),
        cost_estimate=pl.CostEstimate(
            flops=0, bytes_accessed=count * kept[0].size * 8, transcendentals=0
        ),
        name="pair_sums",
    )(*kept, *received)


def finish_kernel(chunks, each, *refs):
    out_ref = refs[-1]
    size = out_ref.shape[1] // chunks
    for chunk in range(chunks):
        total = refs[chunk * each][...].astype(F32)
        for term in range(1, each):
            total = total + refs[chunk * each + term][...].astype(F32)
        out_ref[:, chunk * size : (chunk + 1) * size] = total.astype(BF16)


def finish(terms):
    chunks, each = len(terms), len(terms[0])
    nodes, size = terms[0][0].shape
    return pl.pallas_call(
        functools.partial(finish_kernel, chunks, each),
        out_shape=jax.ShapeDtypeStruct((nodes, size * chunks), BF16),
        compiler_params=params(),
        cost_estimate=pl.CostEstimate(
            flops=0, bytes_accessed=chunks * nodes * size * 2 * each, transcendentals=0
        ),
        name="finish",
    )(*[array for group in terms for array in group])


LINE_SWAP1 = z_pairs([(0, 1), (1, 0), (2, 3), (3, 2)])
LINE_SWAP2 = z_pairs([(0, 2), (2, 0), (1, 3), (3, 1)])
LINE_MIDDLE = z_pairs([(1, 2), (2, 1)])
LINE_OUT = z_pairs([(2, 3), (1, 0)])
LINE_IN = z_pairs([(3, 2), (0, 1)])
CORE = xor_pairs(8, 1)


def spread(piece, columns):
    if columns != 8:
        return [[piece]] + [
            [lax.ppermute(piece, "col", xor_pairs(columns, step))] for step in range(1, columns)
        ]
    far = lax.ppermute(piece, "col", LINE_SWAP2)
    near = lax.ppermute(piece, "col", LINE_SWAP1)
    middle = lax.ppermute(piece, "col", LINE_MIDDLE)
    ends = lax.ppermute(far, "col", LINE_OUT)
    own = [[piece], [near], [far], [middle, ends]]
    other = [[lax.ppermute(a, "col", CORE) for a in group] for group in own]
    return [group for pair in zip(own, other) for group in pair]


def collect(pieces, columns):
    if columns != 8:
        return [pieces[0]] + [
            lax.ppermute(pieces[step], "col", xor_pairs(columns, step))
            for step in range(1, columns)
        ]
    received = [lax.ppermute(pieces[2 * z + 1], "col", CORE) for z in range(4)]
    own, near, far, last = pair_sums([pieces[2 * z] for z in range(4)], received)
    passed = lax.ppermute(last, "col", LINE_IN)
    middle = lax.ppermute(last, "col", LINE_MIDDLE)
    from_near = lax.ppermute(near, "col", LINE_SWAP1)
    far = (far.astype(F32) + passed.astype(F32)).astype(BF16)
    from_far = lax.ppermute(far, "col", LINE_SWAP2)
    return [own, middle, from_near, from_far]


def sum_everywhere(top, low, bias, rows, columns):
    core = lax.axis_index("col") % 2
    mine = jnp.where(core == 0, top, low)
    theirs = jnp.where(core == 0, low, top)
    mine = mine + lax.ppermute(theirs, "col", xor_pairs(columns, 1))
    bias = bias + lax.ppermute(bias, "col", xor_pairs(columns, 1))
    both = jnp.concatenate([mine, bias], axis=0)
    step = 2
    while step < columns:
        both = both + lax.ppermute(both, "col", xor_pairs(columns, step))
        step *= 2
    step = 1
    while step < rows:
        both = both + lax.ppermute(both, "row", xor_pairs(rows, step))
        step *= 2
    mine = both[: mine.shape[0]]
    theirs = lax.ppermute(mine, "col", xor_pairs(columns, 1))
    weight_sum = jnp.concatenate(
        [jnp.where(core == 0, mine, theirs), jnp.where(core == 0, theirs, mine)], axis=0
    )
    return weight_sum, jnp.sum(both[mine.shape[0] :], axis=0)


def per_device(
    features,
    weight,
    bias_vector,
    send_rows,
    send_count,
    adjacency,
    source_tile,
    tile_count,
    cotangent,
):
    rows, columns = lax.axis_size("row"), lax.axis_size("col")
    nodes, width = features.shape
    list_rows, list_counts = send_rows[0, 0], send_count[0, 0]
    capacity = list_rows.shape[1]
    chunks = width // CHUNK
    pos = jnp.stack([lax.axis_index("row"), lax.axis_index("col")]).astype(jnp.int32)

    slots = [
        spread(features[:, chunk * CHUNK : (chunk + 1) * CHUNK], columns)
        for chunk in range(chunks)
    ]
    live = jnp.arange(capacity)[None, :] < list_counts[:, None]
    lists = lax.all_to_all(
        jnp.where(live, list_rows, -1), "col", split_axis=0, concat_axis=0, tiled=True
    )
    dense = densify(adjacency[0, 0], source_tile[0, 0], tile_count[0, 0], pos, columns, capacity)
    pick, put = selectors(lists, pos, nodes)

    parts = []
    for chunk in range(chunks):
        blocks = forward(dense, pick, slots[chunk], pos, rows)
        parts.append(blocks[0])
        for step in range(1, rows):
            parts.append(lax.ppermute(blocks[step], "row", xor_pairs(rows, step)))

    results = layer(weight, bias_vector, cotangent, parts, chunks, rows)
    output, agg, grad_pre = results[:3]
    backs = [
        [back] + [lax.ppermute(back, "row", xor_pairs(rows, step)) for step in range(1, rows)]
        for back in results[3:]
    ]
    top, low, bias = weight_partials(agg, grad_pre)
    weight_sum, bias_sum = sum_everywhere(top, low, bias, rows, columns)
    scale = 1.0 / math.sqrt(nodes * rows * columns)

    kept = tuple(range(0, columns, 2)) if columns == 8 else (0,)
    terms = [
        collect(backward(dense, put, backs[chunk], pos, kept), columns)
        for chunk in range(chunks)
    ]
    return output, finish(terms), weight_sum * scale, bias_sum * scale


def solution(mesh):
    in_specs = (
        P(("row", "col"), None),
        P(),
        P(),
        P("row", "col", None, None),
        P("row", "col", None),
        P("row", "col", None, None, None, None),
        P("row", "col", None, None),
        P("row", "col", None),
        P(("row", "col"), None),
    )
    out_specs = (P(("row", "col"), None), P(("row", "col"), None), P(), P())
    return jax.shard_map(
        per_device, mesh=mesh, in_specs=in_specs, out_specs=out_specs, check_vma=False
    )
```

time: 407 us -> 142 us (0.35)
  waiting for transfers between devices: 149 us -> 30.9 us
  other arithmetic: 90.2 us -> 3.01 us
  blocking collectives: 68.6 us -> 0 us
  starting transfers between devices: 11 us -> 57.3 us
  matrix products: 40 us -> 0 us
  Pallas kernels: 0 us -> 28.4 us
  between operations: 13.9 us -> 1.06 us
  local copies, waits for them, and re-layouts: 32 us -> 20.5 us
    scatter-add x17 -> x0, other arithmetic: 82.4 us -> none  [the longest x16 70.3 us: add_slot(): return total.at[target_index].add(contrib)]
    psum x1 -> x0, waiting for transfers between devices: 73.7 us -> none  [per_device(): weight_sum, bias_sum = lax.psum((weight_local, bias_local), ('row', 'col'))]
    psum x1 -> x0, blocking collectives: 68.6 us -> none  [per_device(): weight_sum, bias_sum = lax.psum((weight_local, bias_local), ('row', 'col'))]
    ppermute x0 -> x53, starting transfers between devices: none -> 51.8 us  [the longest x6 7.46 us: per_device(): lax.ppermute(back, 'row', xor_pairs(rows, step))]
    dot_general x20 -> x0, matrix products: 40 us -> none  [the longest x16 24.3 us: add_slot(): jnp.einsum('tab,taf->tbf', tile_block, blocks, preferred_element_type=jnp...]
    reduce_scatter x1 -> x0, waiting for transfers between devices: 34.2 us -> none  [per_device(): lax.psum_scatter(partial_sum, 'row', scatter_dimension=0, tiled=True)]
    ppermute x0 -> x53, waiting for transfers between devices: none -> 30.9 us  [the longest x2 9.75 us: collect(): from_far = lax.ppermute(far, 'col', LINE_SWAP2)]
    pallas_call x0 -> x11, Pallas kernels: none -> 28.4 us  [the longest x2 10.8 us: forward(): pl.pallas_call(functools.partial(forward_kernel, tuple((len(group) for gr...]
  transfers between devices with their start and end apart: 5 -> 54, of which waited for: 4 -> 13; matrix products, arithmetic and copies ran while one was open for 4% -> 2% of each run, Pallas kernels for 0% -> 18%
where the time goes in v1:
time: 142 us; the launch traced here: 141 us
  starting transfers between devices  57.3 us (40%)
  waiting for transfers between devices  30.9 us (22%)
  Pallas kernels  28.4 us (20%)
  local copies, waits for them, and re-layouts  20.5 us (14%)
  other arithmetic  3.01 us (2%)
    unnamed x41, local copies, waits for them, and re-layouts  19.5 us
    pallas_call x2, Pallas kernels, forward(): pl.pallas_call(functools.partial(forward_kernel, tuple((len(group) for gr...  10.8 us
    ppermute x2, waiting for transfers between devices, collect(): from_far = lax.ppermute(far, 'col', LINE_SWAP2)  9.75 us
    ppermute x2, waiting for transfers between devices, spread(): far = lax.ppermute(piece, 'col', LINE_SWAP2)  8 us
    ppermute x6, starting transfers between devices, per_device(): lax.ppermute(back, 'row', xor_pairs(rows, step))  7.46 us
    ppermute x2, starting transfers between devices, spread(): far = lax.ppermute(piece, 'col', LINE_SWAP2)  7.32 us
    ppermute x6, starting transfers between devices, per_device(): parts.append(lax.ppermute(blocks[step], 'row', xor_pairs(rows, step)))  7.18 us
    ppermute x2, starting transfers between devices, collect(): passed = lax.ppermute(last, 'col', LINE_IN)  6.5 us
  transfers between devices with their start and end apart: 54, of which 13 were waited for; matrix products, arithmetic and copies ran while one was open for 2% of the time, Pallas kernels for 18%

profile of v1, /device:TPU:0, one launch (start us, length us, event | category | flops | bytes accessed | tf_op | source)
XLA Modules:
  0.0 141.1 jit_solution(4171636970786730197)
XLA Ops:
  1.6 4.1 %collective-permute-start.15 = (bf16[512,128]{1,0:T(8,128)(2,1)S(1)}, bf16[512,128]{1,0:T(8,128)(2,1)S(1)}, u32[]{:S(2)}, u32[]{:S(2)}) collective-permute-start(bf16[512,128]{1,0:T(8,128)(2,1)S(1)} %get-tuple-element.90.rest_0_), channel_id=1, source_target_pairs={{0,4},{1,5},{4,0},{5,1},{2,6},{3,7},{6,2},{7,3},{8,12},{9,13},{12,... | collective-permute-start | bytes 393224 | tf_op jit(solution)/shard_map/ppermute | solution.py:344
  5.7 1.6 %collective-permute-start.13 = (bf16[512,128]{1,0:T(8,128)(2,1)S(1)}, bf16[512,128]{1,0:T(8,128)(2,1)S(1)}, u32[]{:S(2)}, u32[]{:S(2)}) collective-permute-start(bf16[512,128]{1,0:T(8,128)(2,1)S(1)} %get-tuple-element.90.rest_0_), channel_id=1, source_target_pairs={{0,2},{1,3},{2,0},{3,1},{4,6},{5,7},{6,4},{7,5},{8,10},{9,11},{10,... | collective-permute-start | bytes 393224 | tf_op jit(solution)/shard_map/ppermute | solution.py:345
  8.0 3.2 %collective-permute-start.3 = (bf16[512,128]{1,0:T(8,128)(2,1)S(1)}, bf16[512,128]{1,0:T(8,128)(2,1)S(1)}, u32[]{:S(2)}, u32[]{:S(2)}) collective-permute-start(bf16[512,128]{1,0:T(8,128)(2,1)S(1)} %get-tuple-element.91.rest_0_), channel_id=1, source_target_pairs={{0,4},{1,5},{4,0},{5,1},{2,6},{3,7},{6,2},{7,3},{8,12},{9,13},{12,... | collective-permute-start | bytes 393224 | tf_op jit(solution)/shard_map/ppermute | solution.py:344
  11.3 1.6 %collective-permute-done.15.rest_4_ = bf16[512,128]{1,0:T(8,128)(2,1)S(1)} collective-permute-done((bf16[512,128]{1,0:T(8,128)(2,1)S(1)}, bf16[512,128]{1,0:T(8,128)(2,1)S(1)}, u32[]{:S(2)}, u32[]{:S(2)}) %collective-permute-start.15) | collective-permute-done | bytes 131104 | tf_op jit(solution)/shard_map/ppermute | solution.py:344
  14.9 6.4 %collective-permute-done.3.rest_4_ = bf16[512,128]{1,0:T(8,128)(2,1)S(1)} collective-permute-done((bf16[512,128]{1,0:T(8,128)(2,1)S(1)}, bf16[512,128]{1,0:T(8,128)(2,1)S(1)}, u32[]{:S(2)}, u32[]{:S(2)}) %collective-permute-start.3) | collective-permute-done | bytes 131104 | tf_op jit(solution)/shard_map/ppermute | solution.py:344
  25.1 5.5 %all-to-all-start = ((s32[8,1,256]{2,1,0:T(1,128)}), s32[8,1,256]{2,1,0:T(1,128)S(1)}, u32[]{:S(2)}, u32[]{:S(2)}) async-start(s32[8,1,256]{2,1,0:T(1,128)} %compare_select_fusion), calls=%async_computation | async-start | bytes 16384 | tf_op jit(solution)/shard_map/all_to_all | solution.py:415
  32.6 6.4 %densify.1.dense_ref = bf16[2048,2048]{1,0:T(8,128)(2,1)S(1)} custom-call(s32[16,16]{1,0:T(8,128)S(1)} %bitcast.12, s32[16]{0:T(128)S(1)} %bitcast.14, s32[2]{0:T(128)S(1)} %pad_add_fusion.pos_ref, bf16[16,16,128,128]{3,2,1,0:T(8,128)(2,1)} %bitcast.15), custom_call_target="tpu_custom_call" | custom-call | bytes 16777216 | tf_op jit(solution)/shard_map/densify/pallas_call | solution.py:55
  39.0 3.3 %copy-done = bf16[2048,2048]{1,0:T(8,128)(2,1)} copy-done((bf16[2048,2048]{1,0:T(8,128)(2,1)}, bf16[2048,2048]{1,0:T(8,128)(2,1)S(1)}, u32[]{:S(2)}) %copy-start) | copy-done | bytes 8388632
  45.4 1.6 %selectors.1 = (bf16[8,256,512]{2,1,0:T(8,128)(2,1)S(1)}, bf16[8,512,256]{2,1,0:T(8,128)(2,1)S(1)}) custom-call(s32[2]{0:T(128)S(1)} %pad_add_fusion.pos_ref, s32[8,256]{1,0:T(8,128)S(1)} %bitcast.11), custom_call_target="tpu_custom_call" | custom-call | bytes 4194304 | tf_op jit(solution)/shard_map/selectors/pallas_call | solution.py:84
  47.0 3.4 %copy-done.1 = bf16[2048,2048]{1,0:T(8,128)(2,1)S(1)} copy-done((bf16[2048,2048]{1,0:T(8,128)(2,1)S(1)}, bf16[2048,2048]{1,0:T(8,128)(2,1)}, u32[]{:S(2)}) %copy-start.1) | copy-done | bytes 8388632
  54.9 4.9 %forward_rows.3 = (f32[512,128]{1,0:T(8,128)S(1)}, bf16[512,128]{1,0:T(8,128)(2,1)S(1)}, bf16[512,128]{1,0:T(8,128)(2,1)}, bf16[512,128]{1,0:T(8,128)(2,1)}) custom-call(s32[2]{0:T(128)S(1)} %pad_add_fusion.pos_ref, bf16[8,256,512]{2,1,0:T(8,128)(2,1)S(1)} %get-tuple-element.46.pick_ref, bf16[2048,2048]{1,0:T(8,128)(2,1)S(1)} %copy-done.1, ...), custom_call_target="tpu_custom_call" | custom-call | flops 1073741824 | bytes 8388608 | tf_op jit(solution)/shard_map/forward_rows/pallas_call | solution.py:137
  59.8 1.9 %collective-permute-start.21 = (bf16[512,128]{1,0:T(8,128)(2,1)S(1)}, bf16[512,128]{1,0:T(8,128)(2,1)S(1)}, u32[]{:S(2)}, u32[]{:S(2)}) collective-permute-start(bf16[512,128]{1,0:T(8,128)(2,1)S(1)} %get-tuple-element.52), channel_id=1, source_target_pairs={{0,8},{8,0},{16,24},{24,16},{1,9},{9,1},{17,25},{25,17},{2,10},{10... | collective-permute-start | bytes 393224 | tf_op jit(solution)/shard_map/ppermute | solution.py:426
  63.5 6.0 %forward_rows.2 = (f32[512,128]{1,0:T(8,128)S(1)}, bf16[512,128]{1,0:T(8,128)(2,1)}, bf16[512,128]{1,0:T(8,128)(2,1)}, bf16[512,128]{1,0:T(8,128)(2,1)}) custom-call(s32[2]{0:T(128)S(1)} %pad_add_fusion.pos_ref, bf16[8,256,512]{2,1,0:T(8,128)(2,1)S(1)} %get-tuple-element.46.pick_ref, bf16[2048,2048]{1,0:T(8,128)(2,1)S(1)} %copy-done.1, ...), custom_call_target="tpu_custom_call" | custom-call | flops 1073741824 | bytes 8388608 | tf_op jit(solution)/shard_map/forward_rows/pallas_call | solution.py:137
  69.5 2.0 %collective-permute-start.10 = (bf16[512,128]{1,0:T(8,128)(2,1)}, bf16[512,128]{1,0:T(8,128)(2,1)S(1)}, u32[]{:S(2)}, u32[]{:S(2)}) collective-permute-start(bf16[512,128]{1,0:T(8,128)(2,1)} %get-tuple-element.49), channel_id=1, source_target_pairs={{0,16},{8,24},{16,0},{24,8},{1,17},{9,25},{17,1},{25,9},{2,18},{10... | collective-permute-start | bytes 393224 | tf_op jit(solution)/shard_map/ppermute | solution.py:426
  73.6 2.9 %collective-permute-done.10.rest_2_ = bf16[512,128]{1,0:T(8,128)(2,1)S(1)} collective-permute-done((bf16[512,128]{1,0:T(8,128)(2,1)}, bf16[512,128]{1,0:T(8,128)(2,1)S(1)}, u32[]{:S(2)}, u32[]{:S(2)}) %collective-permute-start.10) | collective-permute-done | bytes 131104 | tf_op jit(solution)/shard_map/ppermute | solution.py:426
  76.5 1.7 %collective-permute-done.11.rest_3_ = bf16[512,128]{1,0:T(8,128)(2,1)S(1)} collective-permute-done((bf16[512,128]{1,0:T(8,128)(2,1)}, bf16[512,128]{1,0:T(8,128)(2,1)S(1)}, u32[]{:S(2)}, u32[]{:S(2)}) %collective-permute-start.11) | collective-permute-done | bytes 131104 | tf_op jit(solution)/shard_map/ppermute | solution.py:426
  79.8 2.1 %layer.1 = (bf16[512,256]{1,0:T(8,128)(2,1)}, bf16[512,256]{1,0:T(8,128)(2,1)S(1)}, bf16[512,256]{1,0:T(8,128)(2,1)S(1)}, bf16[128,512]{1,0:T(8,128)(2,1)S(1)}, bf16[128,512]{1,0:T(8,128)(2,1)S(1)}) custom-call(bf16[256,256]{1,0:T(8,128)(2,1)S(1)} %copy-done.14, f32[1,256]{1,0:T(1,128)S(1)} %bitcast.13, bf16[512,256]{1,0:T(8,128)(2,1)S(1)} %copy-done.3, ...), custom_call_target="tpu_custom_call" | custom-call | flops 134217728 | bytes 2621440 | tf_op jit(solution)/shard_map/layer/pallas_call | solution.py:190
  89.1 1.7 %collective-permute-start.26 = (bf16[128,512]{1,0:T(8,128)(2,1)S(1)}, bf16[128,512]{1,0:T(8,128)(2,1)S(1)}, u32[]{:S(2)}, u32[]{:S(2)}) collective-permute-start(bf16[128,512]{1,0:T(8,128)(2,1)S(1)} %get-tuple-element.57.rest_0_), channel_id=1, source_target_pairs={{0,24},{8,16},{16,8},{24,0},{1,25},{9,17},{17,9},{25,1},{2,26},{10... | collective-permute-start | bytes 393224 | tf_op jit(solution)/shard_map/ppermute | solution.py:431
  92.0 2.2 %collective-permute-start.48 = (f32[136,256]{1,0:T(8,128)S(1)}, f32[136,256]{1,0:T(8,128)S(1)}, u32[]{:S(2)}, u32[]{:S(2)}) collective-permute-start(f32[136,256]{1,0:T(8,128)S(1)} %pad_maximum_fusion), channel_id=1, source_target_pairs={{0,2},{1,3},{2,0},{3,1},{4,6},{5,7},{6,4},{7,5},{8,10},{9,11},{10,... | collective-permute-start | bytes 417800 | tf_op jit(solution)/shard_map/ppermute | solution.py:378
  94.2 3.4 %copy-done.2 = bf16[2048,2048]{1,0:T(8,128)(2,1)S(1)} copy-done((bf16[2048,2048]{1,0:T(8,128)(2,1)S(1)}, bf16[2048,2048]{1,0:T(8,128)(2,1)}, u32[]{:S(2)}) %copy-start.2) | copy-done | bytes 8388632
  97.6 3.0 %backward_rows.3 = (f32[512,128]{1,0:T(8,128)S(1)}, bf16[512,128]{1,0:T(8,128)(2,1)S(1)}, f32[512,128]{1,0:T(8,128)S(1)}, bf16[512,128]{1,0:T(8,128)(2,1)S(1)}, ...) custom-call(s32[2]{0:T(128)S(1)} %pad_add_fusion.pos_ref, ...), custom_call_target="tpu_custom_call" | custom-call | flops 1073741824 | bytes 8388608 | tf_op jit(solution)/shard_map/backward_rows/pallas_call | solution.py:261
  101.8 3.1 %backward_rows.2 = (f32[512,128]{1,0:T(8,128)S(1)}, bf16[512,128]{1,0:T(8,128)(2,1)S(1)}, f32[512,128]{1,0:T(8,128)S(1)}, bf16[512,128]{1,0:T(8,128)(2,1)S(1)}, ...) custom-call(s32[2]{0:T(128)S(1)} %pad_add_fusion.pos_ref, ...), custom_call_target="tpu_custom_call" | custom-call | flops 1073741824 | bytes 8388608 | tf_op jit(solution)/shard_map/backward_rows/pallas_call | solution.py:261
  105.1 1.5 %collective-permute-start.49 = (f32[136,256]{1,0:T(8,128)S(1)}, f32[136,256]{1,0:T(8,128)S(1)}, u32[]{:S(2)}, u32[]{:S(2)}) collective-permute-start(f32[136,256]{1,0:T(8,128)S(1)} %fusion), channel_id=1, source_target_pairs={{0,4},{1,5},{2,6},{3,7},{4,0},{5,1},{6,2},{7,3},{8,12},{9,13},{10,... | collective-permute-start | bytes 417800 | tf_op jit(solution)/shard_map/ppermute | solution.py:378
  107.3 3.1 %collective-permute-start.44 = (bf16[512,128]{1,0:T(8,128)(2,1)S(1)}, bf16[512,128]{1,0:T(8,128)(2,1)S(1)}, u32[]{:S(2)}, u32[]{:S(2)}) collective-permute-start(bf16[512,128]{1,0:T(8,128)(2,1)S(1)} %get-tuple-element.80), channel_id=1, source_target_pairs={{6,4},{7,5},{0,2},{1,3},{14,12},{15,13},{8,10},{9,11},{22,20},{23,... | collective-permute-start | bytes 393224 | tf_op jit(solution)/shard_map/ppermute | solution.py:361
  111.3 3.4 %collective-permute-start.33 = (bf16[512,128]{1,0:T(8,128)(2,1)S(1)}, bf16[512,128]{1,0:T(8,128)(2,1)S(1)}, u32[]{:S(2)}, u32[]{:S(2)}) collective-permute-start(bf16[512,128]{1,0:T(8,128)(2,1)S(1)} %get-tuple-element.67), channel_id=1, source_target_pairs={{6,4},{7,5},{0,2},{1,3},{14,12},{15,13},{8,10},{9,11},{22,20},{23,... | collective-permute-start | bytes 393224 | tf_op jit(solution)/shard_map/ppermute | solution.py:361
  115.3 1.9 %collective-permute-start.43 = (bf16[512,128]{1,0:T(8,128)(2,1)S(1)}, bf16[512,128]{1,0:T(8,128)(2,1)S(1)}, u32[]{:S(2)}, u32[]{:S(2)}) collective-permute-start(bf16[512,128]{1,0:T(8,128)(2,1)S(1)} %get-tuple-element.81), channel_id=1, source_target_pairs={{0,2},{1,3},{2,0},{3,1},{4,6},{5,7},{6,4},{7,5},{8,10},{9,11},{10,... | collective-permute-start | bytes 393224 | tf_op jit(solution)/shard_map/ppermute | solution.py:363
  118.2 4.2 %collective-permute-done.50 = f32[136,256]{1,0:T(8,128)S(1)} collective-permute-done((f32[136,256]{1,0:T(8,128)S(1)}, f32[136,256]{1,0:T(8,128)S(1)}, u32[]{:S(2)}, u32[]{:S(2)}) %collective-permute-start.50) | collective-permute-done | bytes 139296 | tf_op jit(solution)/shard_map/ppermute | solution.py:382
  122.7 2.0 %collective-permute-start.51 = (f32[136,256]{1,0:T(8,128)S(1)}, f32[136,256]{1,0:T(8,128)S(1)}, u32[]{:S(2)}, u32[]{:S(2)}) collective-permute-start(f32[136,256]{1,0:T(8,128)S(1)} %add.35), channel_id=1, source_target_pairs={{0,16},{8,24},{16,0},{24,8},{1,17},{9,25},{17,1},{25,9},{2,18},{10... | collective-permute-start | bytes 417800 | tf_op jit(solution)/shard_map/ppermute | solution.py:382
  124.8 1.5 %collective-permute-start.45 = (bf16[512,128]{1,0:T(8,128)(2,1)S(1)}, bf16[512,128]{1,0:T(8,128)(2,1)S(1)}, u32[]{:S(2)}, u32[]{:S(2)}) collective-permute-start(bf16[512,128]{1,0:T(8,128)(2,1)S(1)} %add_convert_fusion), channel_id=1, source_target_pairs={{0,4},{1,5},{4,0},{5,1},{2,6},{3,7},{6,2},{7,3},{8,12},{9,13},{12,... | collective-permute-start | bytes 393224 | tf_op jit(solution)/shard_map/ppermute | solution.py:365
  126.3 1.5 %collective-permute-start.34 = (bf16[512,128]{1,0:T(8,128)(2,1)S(1)}, bf16[512,128]{1,0:T(8,128)(2,1)S(1)}, u32[]{:S(2)}, u32[]{:S(2)}) collective-permute-start(bf16[512,128]{1,0:T(8,128)(2,1)S(1)} %add_convert_fusion.1), channel_id=1, source_target_pairs={{0,4},{1,5},{4,0},{5,1},{2,6},{3,7},{6,2},{7,3},{8,12},{9,13},{12,... | collective-permute-start | bytes 393224 | tf_op jit(solution)/shard_map/ppermute | solution.py:365
  128.3 7.9 %collective-permute-done.45.refs_7_ = bf16[512,128]{1,0:T(8,128)(2,1)S(1)} collective-permute-done((bf16[512,128]{1,0:T(8,128)(2,1)S(1)}, bf16[512,128]{1,0:T(8,128)(2,1)S(1)}, u32[]{:S(2)}, u32[]{:S(2)}) %collective-permute-start.45) | collective-permute-done | bytes 131104 | tf_op jit(solution)/shard_map/ppermute | solution.py:365
  136.3 1.8 %collective-permute-done.34.refs_3_ = bf16[512,128]{1,0:T(8,128)(2,1)S(1)} collective-permute-done((bf16[512,128]{1,0:T(8,128)(2,1)S(1)}, bf16[512,128]{1,0:T(8,128)(2,1)S(1)}, u32[]{:S(2)}, u32[]{:S(2)}) %collective-permute-start.34) | collective-permute-done | bytes 131104 | tf_op jit(solution)/shard_map/ppermute | solution.py:365
  (146 shorter events, 39.2 us)
Async XLA Ops:
  1.6 11.2 %collective-permute-start.15 = (bf16[512,128]{1,0:T(8,128)(2,1)S(1)}, bf16[512,128]{1,0:T(8,128)(2,1)S(1)}, u32[]{:S(2)}, u32[]{:S(2)}) collective-permute-start(bf16[512,128]{1,0:T(8,128)(2,1)S(1)} %get-tuple-element.90.rest_0_), channel_id=1, source_target_pairs={{0,4},{1,5},{4,0},{5,1},{2,6},{3,7},{6,2},{7,3},{8,12},{9,13},{12,... | collective-permute-start | bytes 393224 | tf_op jit(solution)/shard_map/ppermute | solution.py:344
  8.0 13.3 %collective-permute-start.3 = (bf16[512,128]{1,0:T(8,128)(2,1)S(1)}, bf16[512,128]{1,0:T(8,128)(2,1)S(1)}, u32[]{:S(2)}, u32[]{:S(2)}) collective-permute-start(bf16[512,128]{1,0:T(8,128)(2,1)S(1)} %get-tuple-element.91.rest_0_), channel_id=1, source_target_pairs={{0,4},{1,5},{4,0},{5,1},{2,6},{3,7},{6,2},{7,3},{8,12},{9,13},{12,... | collective-permute-start | bytes 393224 | tf_op jit(solution)/shard_map/ppermute | solution.py:344
  12.9 9.0 %collective-permute-start.5 = (bf16[512,128]{1,0:T(8,128)(2,1)S(1)}, bf16[512,128]{1,0:T(8,128)(2,1)S(1)}, u32[]{:S(2)}, u32[]{:S(2)}) collective-permute-start(bf16[512,128]{1,0:T(8,128)(2,1)S(1)} %get-tuple-element.91.rest_0_), channel_id=1, source_target_pairs={{2,4},{3,5},{4,2},{5,3},{10,12},{11,13},{12,10},{13,11},{18,20},{1... | collective-permute-start | bytes 393224 | tf_op jit(solution)/shard_map/ppermute | solution.py:346
  13.5 10.2 %collective-permute-start.18 = (bf16[512,128]{1,0:T(8,128)(2,1)S(1)}, bf16[512,128]{1,0:T(8,128)(2,1)S(1)}, u32[]{:S(2)}, u32[]{:S(2)}) collective-permute-start(bf16[512,128]{1,0:T(8,128)(2,1)S(1)} %collective-permute-done.15.rest_4_), channel_id=1, source_target_pairs={{4,6},{5,7},{2,0},{3,1},{12,14},{13,15},{10,8},{11,9},{20,22},{21,... | collective-permute-start | bytes 393224 | tf_op jit(solution)/shard_map/ppermute | solution.py:347
  14.9 15.8 %collective-permute-start.16 = (bf16[512,128]{1,0:T(8,128)(2,1)S(1)}, bf16[512,128]{1,0:T(8,128)(2,1)S(1)}, u32[]{:S(2)}, u32[]{:S(2)}) collective-permute-start(bf16[512,128]{1,0:T(8,128)(2,1)S(1)} %collective-permute-done.15.rest_4_), channel_id=1, source_target_pairs={{0,1},{1,0},{2,3},{3,2},{4,5},{5,4},{6,7},{7,6},{8,9},{9,8},{10,11... | collective-permute-start | bytes 393224 | tf_op jit(solution)/shard_map/ppermute | solution.py:349
  21.3 21.0 %collective-permute-start.14 = (bf16[512,128]{1,0:T(8,128)(2,1)S(1)}, bf16[512,128]{1,0:T(8,128)(2,1)S(1)}, u32[]{:S(2)}, u32[]{:S(2)}) collective-permute-start(bf16[512,128]{1,0:T(8,128)(2,1)S(1)} %collective-permute-done.13.rest_2_), channel_id=1, source_target_pairs={{0,1},{1,0},{2,3},{3,2},{4,5},{5,4},{6,7},{7,6},{8,9},{9,8},{10,11... | collective-permute-start | bytes 393224 | tf_op jit(solution)/shard_map/ppermute | solution.py:349
  21.3 21.7 %collective-permute-start.19 = (bf16[512,128]{1,0:T(8,128)(2,1)S(1)}, bf16[512,128]{1,0:T(8,128)(2,1)S(1)}, u32[]{:S(2)}, u32[]{:S(2)}) collective-permute-start(bf16[512,128]{1,0:T(8,128)(2,1)S(1)} %collective-permute-done.17.rest_6_), channel_id=1, source_target_pairs={{0,1},{1,0},{2,3},{3,2},{4,5},{5,4},{6,7},{7,6},{8,9},{9,8},{10,11... | collective-permute-start | bytes 393224 | tf_op jit(solution)/shard_map/ppermute | solution.py:349
  21.9 22.3 %collective-permute-start.6 = (bf16[512,128]{1,0:T(8,128)(2,1)S(1)}, bf16[512,128]{1,0:T(8,128)(2,1)}, u32[]{:S(2)}, u32[]{:S(2)}) collective-permute-start(bf16[512,128]{1,0:T(8,128)(2,1)S(1)} %collective-permute-done.3.rest_4_), channel_id=1, source_target_pairs={{4,6},{5,7},{2,0},{3,1},{12,14},{13,15},{10,8},{11,9},{20,22},{21,... | collective-permute-start | bytes 393224 | tf_op jit(solution)/shard_map/ppermute | solution.py:347
  23.7 20.5 %collective-permute-start.20 = (bf16[512,128]{1,0:T(8,128)(2,1)S(1)}, bf16[512,128]{1,0:T(8,128)(2,1)S(1)}, u32[]{:S(2)}, u32[]{:S(2)}) collective-permute-start(bf16[512,128]{1,0:T(8,128)(2,1)S(1)} %collective-permute-done.18.rest_7_), channel_id=1, source_target_pairs={{0,1},{1,0},{2,3},{3,2},{4,5},{5,4},{6,7},{7,6},{8,9},{9,8},{10,11... | collective-permute-start | bytes 393224 | tf_op jit(solution)/shard_map/ppermute | solution.py:349
  25.1 17.2 %all-to-all-start = ((s32[8,1,256]{2,1,0:T(1,128)}), s32[8,1,256]{2,1,0:T(1,128)S(1)}, u32[]{:S(2)}, u32[]{:S(2)}) async-start(s32[8,1,256]{2,1,0:T(1,128)} %compare_select_fusion), calls=%async_computation | async-start | bytes 16384 | tf_op jit(solution)/shard_map/all_to_all | solution.py:415
  30.6 29.2 %collective-permute-start = (bf16[512,128]{1,0:T(8,128)(2,1)S(1)}, bf16[512,128]{1,0:T(8,128)(2,1)}, u32[]{:S(2)}, u32[]{:S(2)}) collective-permute-start(bf16[512,128]{1,0:T(8,128)(2,1)S(1)} %get-tuple-element.91.rest_0_), channel_id=1, source_target_pairs={{0,1},{1,0},{2,3},{3,2},{4,5},{5,4},{6,7},{7,6},{8,9},{9,8},{10,11... | collective-permute-start | bytes 393224 | tf_op jit(solution)/shard_map/ppermute | solution.py:349
  43.0 18.7 %collective-permute-start.4 = (bf16[512,128]{1,0:T(8,128)(2,1)S(1)}, bf16[512,128]{1,0:T(8,128)(2,1)S(1)}, u32[]{:S(2)}, u32[]{:S(2)}) collective-permute-start(bf16[512,128]{1,0:T(8,128)(2,1)S(1)} %collective-permute-done.3.rest_4_), channel_id=1, source_target_pairs={{0,1},{1,0},{2,3},{3,2},{4,5},{5,4},{6,7},{7,6},{8,9},{9,8},{10,11... | collective-permute-start | bytes 393224 | tf_op jit(solution)/shard_map/ppermute | solution.py:349
  43.7 18.9 %collective-permute-start.2 = (bf16[512,128]{1,0:T(8,128)(2,1)S(1)}, bf16[512,128]{1,0:T(8,128)(2,1)S(1)}, u32[]{:S(2)}, u32[]{:S(2)}) collective-permute-start(bf16[512,128]{1,0:T(8,128)(2,1)S(1)} %collective-permute-done.1.rest_2_), channel_id=1, source_target_pairs={{0,1},{1,0},{2,3},{3,2},{4,5},{5,4},{6,7},{7,6},{8,9},{9,8},{10,11... | collective-permute-start | bytes 393224 | tf_op jit(solution)/shard_map/ppermute | solution.py:349
  44.2 19.3 %collective-permute-start.7 = (bf16[512,128]{1,0:T(8,128)(2,1)S(1)}, bf16[512,128]{1,0:T(8,128)(2,1)S(1)}, u32[]{:S(2)}, u32[]{:S(2)}) collective-permute-start(bf16[512,128]{1,0:T(8,128)(2,1)S(1)} %collective-permute-done.5.rest_6_), channel_id=1, source_target_pairs={{0,1},{1,0},{2,3},{3,2},{4,5},{5,4},{6,7},{7,6},{8,9},{9,8},{10,11... | collective-permute-start | bytes 393224 | tf_op jit(solution)/shard_map/ppermute | solution.py:349
  44.9 18.7 %collective-permute-start.8 = (bf16[512,128]{1,0:T(8,128)(2,1)}, bf16[512,128]{1,0:T(8,128)(2,1)S(1)}, u32[]{:S(2)}, u32[]{:S(2)}) collective-permute-start(bf16[512,128]{1,0:T(8,128)(2,1)} %collective-permute-done.6.rest_7_), channel_id=1, source_target_pairs={{0,1},{1,0},{2,3},{3,2},{4,5},{5,4},{6,7},{7,6},{8,9},{9,8},{10,11... | collective-permute-start | bytes 393224 | tf_op jit(solution)/shard_map/ppermute | solution.py:349
  59.8 12.9 %collective-permute-start.21 = (bf16[512,128]{1,0:T(8,128)(2,1)S(1)}, bf16[512,128]{1,0:T(8,128)(2,1)S(1)}, u32[]{:S(2)}, u32[]{:S(2)}) collective-permute-start(bf16[512,128]{1,0:T(8,128)(2,1)S(1)} %get-tuple-element.52), channel_id=1, source_target_pairs={{0,8},{8,0},{16,24},{24,16},{1,9},{9,1},{17,25},{25,17},{2,10},{10... | collective-permute-start | bytes 393224 | tf_op jit(solution)/shard_map/ppermute | solution.py:426
  61.8 11.8 %collective-permute-start.22 = (bf16[512,128]{1,0:T(8,128)(2,1)}, bf16[512,128]{1,0:T(8,128)(2,1)}, u32[]{:S(2)}, u32[]{:S(2)}) collective-permute-start(bf16[512,128]{1,0:T(8,128)(2,1)} %get-tuple-element.53), channel_id=1, source_target_pairs={{0,16},{8,24},{16,0},{24,8},{1,17},{9,25},{17,1},{25,9},{2,18},{10... | collective-permute-start | bytes 393224 | tf_op jit(solution)/shard_map/ppermute | solution.py:426
  62.5 11.1 %collective-permute-start.23 = (bf16[512,128]{1,0:T(8,128)(2,1)}, bf16[512,128]{1,0:T(8,128)(2,1)}, u32[]{:S(2)}, u32[]{:S(2)}) collective-permute-start(bf16[512,128]{1,0:T(8,128)(2,1)} %get-tuple-element.54), channel_id=1, source_target_pairs={{0,24},{8,16},{16,8},{24,0},{1,25},{9,17},{17,9},{25,1},{2,26},{10... | collective-permute-start | bytes 393224 | tf_op jit(solution)/shard_map/ppermute | solution.py:426
  85.1 9.2 %collective-permute-start.37 = (bf16[128,512]{1,0:T(8,128)(2,1)S(1)}, bf16[128,512]{1,0:T(8,128)(2,1)S(1)}, u32[]{:S(2)}, u32[]{:S(2)}) collective-permute-start(bf16[128,512]{1,0:T(8,128)(2,1)S(1)} %get-tuple-element.70.rest_0_), channel_id=1, source_target_pairs={{0,24},{8,16},{16,8},{24,0},{1,25},{9,17},{17,9},{25,1},{2,26},{10... | collective-permute-start | bytes 393224 | tf_op jit(solution)/shard_map/ppermute | solution.py:431
  86.3 14.4 %collective-permute-start.24 = (bf16[128,512]{1,0:T(8,128)(2,1)S(1)}, bf16[128,512]{1,0:T(8,128)(2,1)S(1)}, u32[]{:S(2)}, u32[]{:S(2)}) collective-permute-start(bf16[128,512]{1,0:T(8,128)(2,1)S(1)} %get-tuple-element.57.rest_0_), channel_id=1, source_target_pairs={{0,8},{8,0},{16,24},{24,16},{1,9},{9,1},{17,25},{25,17},{2,10},{10... | collective-permute-start | bytes 393224 | tf_op jit(solution)/shard_map/ppermute | solution.py:431
  87.4 13.8 %collective-permute-start.25 = (bf16[128,512]{1,0:T(8,128)(2,1)S(1)}, bf16[128,512]{1,0:T(8,128)(2,1)S(1)}, u32[]{:S(2)}, u32[]{:S(2)}) collective-permute-start(bf16[128,512]{1,0:T(8,128)(2,1)S(1)} %get-tuple-element.57.rest_0_), channel_id=1, source_target_pairs={{0,16},{8,24},{16,0},{24,8},{1,17},{9,25},{17,1},{25,9},{2,18},{10... | collective-permute-start | bytes 393224 | tf_op jit(solution)/shard_map/ppermute | solution.py:431
  89.1 12.3 %collective-permute-start.26 = (bf16[128,512]{1,0:T(8,128)(2,1)S(1)}, bf16[128,512]{1,0:T(8,128)(2,1)S(1)}, u32[]{:S(2)}, u32[]{:S(2)}) collective-permute-start(bf16[128,512]{1,0:T(8,128)(2,1)S(1)} %get-tuple-element.57.rest_0_), channel_id=1, source_target_pairs={{0,24},{8,16},{16,8},{24,0},{1,25},{9,17},{17,9},{25,1},{2,26},{10... | collective-permute-start | bytes 393224 | tf_op jit(solution)/shard_map/ppermute | solution.py:431
  92.0 12.8 %collective-permute-start.48 = (f32[136,256]{1,0:T(8,128)S(1)}, f32[136,256]{1,0:T(8,128)S(1)}, u32[]{:S(2)}, u32[]{:S(2)}) collective-permute-start(f32[136,256]{1,0:T(8,128)S(1)} %pad_maximum_fusion), channel_id=1, source_target_pairs={{0,2},{1,3},{2,0},{3,1},{4,6},{5,7},{6,4},{7,5},{8,10},{9,11},{10,... | collective-permute-start | bytes 417800 | tf_op jit(solution)/shard_map/ppermute | solution.py:378
  105.1 10.2 %collective-permute-start.49 = (f32[136,256]{1,0:T(8,128)S(1)}, f32[136,256]{1,0:T(8,128)S(1)}, u32[]{:S(2)}, u32[]{:S(2)}) collective-permute-start(f32[136,256]{1,0:T(8,128)S(1)} %fusion), channel_id=1, source_target_pairs={{0,4},{1,5},{2,6},{3,7},{4,0},{5,1},{6,2},{7,3},{8,12},{9,13},{10,... | collective-permute-start | bytes 417800 | tf_op jit(solution)/shard_map/ppermute | solution.py:378
  107.3 9.9 %collective-permute-start.44 = (bf16[512,128]{1,0:T(8,128)(2,1)S(1)}, bf16[512,128]{1,0:T(8,128)(2,1)S(1)}, u32[]{:S(2)}, u32[]{:S(2)}) collective-permute-start(bf16[512,128]{1,0:T(8,128)(2,1)S(1)} %get-tuple-element.80), channel_id=1, source_target_pairs={{6,4},{7,5},{0,2},{1,3},{14,12},{15,13},{8,10},{9,11},{22,20},{23,... | collective-permute-start | bytes 393224 | tf_op jit(solution)/shard_map/ppermute | solution.py:361
  110.5 14.3 %collective-permute-start.42 = (bf16[512,128]{1,0:T(8,128)(2,1)S(1)}, bf16[512,128]{1,0:T(8,128)(2,1)S(1)}, u32[]{:S(2)}, u32[]{:S(2)}) collective-permute-start(bf16[512,128]{1,0:T(8,128)(2,1)S(1)} %get-tuple-element.80), channel_id=1, source_target_pairs={{2,4},{3,5},{4,2},{5,3},{10,12},{11,13},{12,10},{13,11},{18,20},{1... | collective-permute-start | bytes 393224 | tf_op jit(solution)/shard_map/ppermute | solution.py:362
  111.3 11.5 %collective-permute-start.33 = (bf16[512,128]{1,0:T(8,128)(2,1)S(1)}, bf16[512,128]{1,0:T(8,128)(2,1)S(1)}, u32[]{:S(2)}, u32[]{:S(2)}) collective-permute-start(bf16[512,128]{1,0:T(8,128)(2,1)S(1)} %get-tuple-element.67), channel_id=1, source_target_pairs={{6,4},{7,5},{0,2},{1,3},{14,12},{15,13},{8,10},{9,11},{22,20},{23,... | collective-permute-start | bytes 393224 | tf_op jit(solution)/shard_map/ppermute | solution.py:361
  114.7 13.2 %collective-permute-start.31 = (bf16[512,128]{1,0:T(8,128)(2,1)S(1)}, bf16[512,128]{1,0:T(8,128)(2,1)S(1)}, u32[]{:S(2)}, u32[]{:S(2)}) collective-permute-start(bf16[512,128]{1,0:T(8,128)(2,1)S(1)} %get-tuple-element.67), channel_id=1, source_target_pairs={{2,4},{3,5},{4,2},{5,3},{10,12},{11,13},{12,10},{13,11},{18,20},{1... | collective-permute-start | bytes 393224 | tf_op jit(solution)/shard_map/ppermute | solution.py:362
  115.3 11.0 %collective-permute-start.43 = (bf16[512,128]{1,0:T(8,128)(2,1)S(1)}, bf16[512,128]{1,0:T(8,128)(2,1)S(1)}, u32[]{:S(2)}, u32[]{:S(2)}) collective-permute-start(bf16[512,128]{1,0:T(8,128)(2,1)S(1)} %get-tuple-element.81), channel_id=1, source_target_pairs={{0,2},{1,3},{2,0},{3,1},{4,6},{5,7},{6,4},{7,5},{8,10},{9,11},{10,... | collective-permute-start | bytes 393224 | tf_op jit(solution)/shard_map/ppermute | solution.py:363
  122.7 16.2 %collective-permute-start.51 = (f32[136,256]{1,0:T(8,128)S(1)}, f32[136,256]{1,0:T(8,128)S(1)}, u32[]{:S(2)}, u32[]{:S(2)}) collective-permute-start(f32[136,256]{1,0:T(8,128)S(1)} %add.35), channel_id=1, source_target_pairs={{0,16},{8,24},{16,0},{24,8},{1,17},{9,25},{17,1},{25,9},{2,18},{10... | collective-permute-start | bytes 417800 | tf_op jit(solution)/shard_map/ppermute | solution.py:382
  124.8 11.4 %collective-permute-start.45 = (bf16[512,128]{1,0:T(8,128)(2,1)S(1)}, bf16[512,128]{1,0:T(8,128)(2,1)S(1)}, u32[]{:S(2)}, u32[]{:S(2)}) collective-permute-start(bf16[512,128]{1,0:T(8,128)(2,1)S(1)} %add_convert_fusion), channel_id=1, source_target_pairs={{0,4},{1,5},{4,0},{5,1},{2,6},{3,7},{6,2},{7,3},{8,12},{9,13},{12,... | collective-permute-start | bytes 393224 | tf_op jit(solution)/shard_map/ppermute | solution.py:365
  126.3 11.7 %collective-permute-start.34 = (bf16[512,128]{1,0:T(8,128)(2,1)S(1)}, bf16[512,128]{1,0:T(8,128)(2,1)S(1)}, u32[]{:S(2)}, u32[]{:S(2)}) collective-permute-start(bf16[512,128]{1,0:T(8,128)(2,1)S(1)} %add_convert_fusion.1), channel_id=1, source_target_pairs={{0,4},{1,5},{4,0},{5,1},{2,6},{3,7},{6,2},{7,3},{8,12},{9,13},{12,... | collective-permute-start | bytes 393224 | tf_op jit(solution)/shard_map/ppermute | solution.py:365
  (42 other events, 221.1 us)

commit v2 on v1

v2 whole, which is shorter than its diff:
```python
import functools
import math

import jax
import jax.numpy as jnp
from jax import lax
from jax.experimental import pallas as pl
from jax.experimental.pallas import tpu as pltpu
from jax.sharding import PartitionSpec as P

TILE = 128
VMEM_LIMIT = 16 * 1024 * 1024
BIG_LIMIT = 40 * 1024 * 1024
RESIDENT = 16 * 1024 * 1024
BF16 = jnp.bfloat16
F32 = jnp.float32


def full_spec(shape):
    return pl.BlockSpec(shape, lambda *_: (0,) * len(shape))


def params(limit=VMEM_LIMIT):
    return pltpu.CompilerParams(vmem_limit_bytes=limit)


def xor_pairs(size, step):
    return [(i, i ^ step) for i in range(size)]


def z_pairs(pairs):
    return [(2 * a + core, 2 * b + core) for a, b in pairs for core in range(2)]


def densify_kernel(per_piece, per_peer, src_ref, cnt_ref, pos_ref, adj_ref, out_ref, held, sems):
    targets, slots = adj_ref.shape[0], adj_ref.shape[1]
    here = pos_ref[1]
    whole = slots * TILE == out_ref.shape[1]
    copies = [
        pltpu.make_async_copy(adj_ref.at[t], held.at[t], sems.at[t]) for t in range(targets)
    ]
    for copy in copies:
        copy.start()
    for t, copy in enumerate(copies):
        place = ((t // per_peer) ^ pos_ref[0]) * per_peer + t % per_peer
        rows = pl.ds(pl.multiple_of(place * TILE, TILE), TILE)
        if not whole:
            out_ref[rows, :] = jnp.zeros((TILE, out_ref.shape[1]), out_ref.dtype)
        count = cnt_ref[t]
        copy.wait()
        for s in range(slots):
            source = src_ref[t, s]
            slot = (source // per_piece) ^ here
            column = pl.multiple_of((slot * per_piece + source % per_piece) * TILE, TILE)
            tile = held[t, s]
            out_ref[rows, pl.ds(column, TILE)] = jnp.where(s < count, tile, jnp.zeros_like(tile))


def densify(adjacency, source_tile, tile_count, pos, peers, pieces, capacity):
    targets = adjacency.shape[0]
    width = pieces * capacity
    smem = pl.BlockSpec(memory_space=pltpu.SMEM)
    return pl.pallas_call(
        functools.partial(densify_kernel, capacity // TILE, targets // peers),
        out_shape=jax.ShapeDtypeStruct((targets * TILE, width), BF16),
        in_specs=[smem, smem, smem, pl.BlockSpec(memory_space=pl.ANY)],
        out_specs=pl.BlockSpec(memory_space=pltpu.VMEM),
        scratch_shapes=[
            pltpu.VMEM(adjacency.shape, BF16),
            pltpu.SemaphoreType.DMA((targets,)),
        ],
        compiler_params=params(40 * 1024 * 1024),
        cost_estimate=pl.CostEstimate(
            flops=0, bytes_accessed=4 * targets * TILE * width, transcendentals=0
        ),
        name="densify",
    )(source_tile, tile_count, pos, adjacency)


def densify_blocks_kernel(per_piece, src_ref, cnt_ref, pos_ref, adj_ref, out_ref):
    step = pl.program_id(0)
    tiles, slots = adj_ref.shape[0], adj_ref.shape[1]
    out_ref[...] = jnp.zeros_like(out_ref)
    here = pos_ref[1]
    for t in range(tiles):
        count = cnt_ref[step * tiles + t]
        for s in range(slots):

            @pl.when(s < count)
            def _(t=t, s=s):
                source = src_ref[step * tiles + t, s]
                slot = (source // per_piece) ^ here
                column = pl.multiple_of((slot * per_piece + source % per_piece) * TILE, TILE)
                out_ref[t * TILE : (t + 1) * TILE, pl.ds(column, TILE)] = adj_ref[t, s]


def densify_blocks(adjacency, source_tile, tile_count, pos, pieces, capacity):
    targets, slots = adjacency.shape[0], adjacency.shape[1]
    tiles = 4
    width = pieces * capacity
    return pl.pallas_call(
        functools.partial(densify_blocks_kernel, capacity // TILE),
        out_shape=jax.ShapeDtypeStruct((targets * TILE, width), BF16),
        grid_spec=pltpu.PrefetchScalarGridSpec(
            num_scalar_prefetch=3,
            grid=(targets // tiles,),
            in_specs=[pl.BlockSpec((tiles, slots, TILE, TILE), lambda i, *_: (i, 0, 0, 0))],
            out_specs=pl.BlockSpec((tiles * TILE, width), lambda i, *_: (i, 0)),
        ),
        compiler_params=params(BIG_LIMIT),
        cost_estimate=pl.CostEstimate(
            flops=0, bytes_accessed=2 * targets * TILE * (width + slots * TILE), transcendentals=0
        ),
        name="densify",
    )(source_tile, tile_count, pos, adjacency)


def hits(row, nodes):
    node = lax.broadcasted_iota(jnp.int32, (nodes, row.shape[1]), 0).astype(F32)
    return jnp.where(node == row, 1.0, 0.0).astype(BF16)


def list_row(high, low):
    return high.astype(F32) * 256.0 + low.astype(F32)


def select_kernel(list_ref, pick_ref, put_ref):
    slots, nodes, _ = put_ref.shape
    for slot in range(slots):
        put = hits(list_ref[slot : slot + 1, :], nodes)
        put_ref[slot] = put
        pick_ref[slot] = put.T


def selectors(lists, nodes):
    pieces, capacity = lists.shape
    return pl.pallas_call(
        select_kernel,
        out_shape=(
            jax.ShapeDtypeStruct((pieces, capacity, nodes), BF16),
            jax.ShapeDtypeStruct((pieces, nodes, capacity), BF16),
        ),
        compiler_params=params(BIG_LIMIT),
        cost_estimate=pl.CostEstimate(
            flops=0, bytes_accessed=4 * pieces * capacity * nodes, transcendentals=0
        ),
        name="selectors",
    )(lists)


def gather_rows(sources, here, put_ref, at):
    nodes, capacity = put_ref.shape[1:]
    columns = (sources[0].shape[0] - nodes) // 2
    piece = sources[0][:nodes, :]
    tail = sources[0][nodes:, :].astype(F32)
    for extra in sources[1:]:
        piece = piece + extra[:nodes, :]
        tail = tail + extra[nodes:, :].astype(F32)
    table = list_row(tail[:columns], tail[columns:])
    mine = lax.broadcasted_iota(jnp.int32, table.shape, 0) == here
    put = hits(jnp.sum(jnp.where(mine, table, 0.0), axis=0, keepdims=True), nodes)
    put_ref[at] = put
    rows = lax.dot_general(put, piece, (((0,), (0,)), ((), ())), preferred_element_type=F32)
    return rows.astype(BF16)


def forward_part_kernel(groups, base, peers, last, pos_ref, dense_ref, *rest):
    total = sum(groups)
    sources, rest = rest[:total], rest[total:]
    if last:
        partial_ref, outs, put_ref, gathered = rest[0], rest[1 : 1 + peers], rest[1 + peers], rest[-1]
    else:
        partial_ref, put_ref, gathered = rest
    here = pos_ref[1]
    capacity = put_ref.shape[2]
    at = 0
    for slot, count in enumerate(groups):
        rows = gather_rows(sources[at : at + count], here, put_ref, slot)
        gathered[slot * capacity : (slot + 1) * capacity, :] = rows
        at += count
    columns = slice(base * capacity, (base + len(groups)) * capacity)
    if not last:
        partial_ref[...] = jnp.dot(
            dense_ref[:, columns], gathered[...], preferred_element_type=F32
        )
        return
    block = outs[0].shape[0]
    for peer in range(peers):
        here_rows = slice(peer * block, (peer + 1) * block)
        result = partial_ref[here_rows, :] + jnp.dot(
            dense_ref[here_rows, columns], gathered[...], preferred_element_type=F32
        )
        outs[peer][...] = result.astype(outs[peer].dtype)


def forward_part(dense, groups, base, pos, peers, nodes, capacity, before=None):
    rows = dense.shape[0]
    flat = [array for group in groups for array in group]
    width = flat[0].shape[1]
    last = before is not None
    put = jax.ShapeDtypeStruct((len(groups), nodes, capacity), BF16)
    if last:
        outs = tuple(
            jax.ShapeDtypeStruct((rows // peers, width), F32 if peer == 0 else BF16)
            for peer in range(peers)
        ) + (put,)
        flat = flat + [before]
    else:
        outs = (jax.ShapeDtypeStruct((rows, width), F32), put)
    depth = len(groups) * capacity
    return pl.pallas_call(
        functools.partial(
            forward_part_kernel, tuple(len(group) for group in groups), base, peers, last
        ),
        out_shape=outs,
        in_specs=[pl.BlockSpec(memory_space=pltpu.SMEM)]
        + [pl.BlockSpec(memory_space=pltpu.VMEM)] * (1 + len(flat)),
        scratch_shapes=[pltpu.VMEM((depth, width), BF16)],
        compiler_params=params(),
        cost_estimate=pl.CostEstimate(
            flops=2 * rows * depth * width, bytes_accessed=2 * rows * depth, transcendentals=0
        ),
        name="forward_late" if last else "forward_early",
    )(pos, dense, *flat)


def forward_blocks_kernel(groups, peers, pos_ref, pick_ref, dense_ref, *rest):
    total = sum(groups)
    sources, outs, gathered = rest[:total], rest[total : total + peers], rest[total + peers]
    step = pl.program_id(0)
    capacity = pick_ref.shape[1]

    @pl.when(step == 0)
    def _():
        at = 0
        for slot, count in enumerate(groups):
            piece = sources[at][...]
            for extra in range(1, count):
                piece = piece + sources[at + extra][...]
            at += count
            rows = jnp.dot(pick_ref[slot], piece, preferred_element_type=F32)
            gathered[slot * capacity : (slot + 1) * capacity, :] = rows.astype(BF16)

    result = jnp.dot(dense_ref[...], gathered[...], preferred_element_type=F32)
    for peer in range(peers):

        @pl.when(step == peer)
        def _(peer=peer):
            outs[peer][...] = result.astype(outs[peer].dtype)


def forward_blocks(dense, pick, groups, pos, peers):
    rows, width = dense.shape
    flat = [array for group in groups for array in group]
    nodes, chunk = flat[0].shape
    block = rows // peers
    return pl.pallas_call(
        functools.partial(forward_blocks_kernel, tuple(len(group) for group in groups), peers),
        out_shape=tuple(
            jax.ShapeDtypeStruct((block, chunk), F32 if peer == 0 else BF16)
            for peer in range(peers)
        ),
        grid_spec=pltpu.PrefetchScalarGridSpec(
            num_scalar_prefetch=1,
            grid=(peers,),
            in_specs=[
                full_spec(pick.shape),
                pl.BlockSpec((block, width), lambda i, pos_ref: (i ^ pos_ref[0], 0)),
            ]
            + [full_spec((nodes, chunk))] * len(flat),
            out_specs=tuple(full_spec((block, chunk)) for _ in range(peers)),
            scratch_shapes=[pltpu.VMEM((width, chunk), BF16)],
        ),
        compiler_params=params(BIG_LIMIT),
        cost_estimate=pl.CostEstimate(
            flops=2 * rows * width * chunk, bytes_accessed=2 * rows * width, transcendentals=0
        ),
        name="forward_rows",
    )(pos, pick, dense, *flat)


def layer_kernel(peers, weight_ref, bias_ref, cot_ref, *rest):
    parts, outs = rest[:peers], rest[peers:]
    out_ref, agg_ref, grad_ref = outs[:3]
    total = parts[0][...].astype(F32)
    for peer in range(1, peers):
        total = total + parts[peer][...].astype(F32)
    agg = total.astype(BF16)
    weight = weight_ref[...]
    preact = jnp.dot(agg, weight, preferred_element_type=F32) + bias_ref[...]
    sigma = 1.0 / (1.0 + jnp.exp(-preact))
    out_ref[...] = (preact * sigma).astype(BF16)
    grad = (cot_ref[...].astype(F32) * sigma * (1.0 + preact * (1.0 - sigma))).astype(BF16)
    agg_ref[...] = agg
    grad_ref[...] = grad
    outs[3][...] = lax.dot_general(
        grad, weight, (((1,), (1,)), ((), ())), preferred_element_type=F32
    ).astype(BF16)


def layer(weight, bias_vector, cotangent, parts):
    nodes, width = cotangent.shape
    return pl.pallas_call(
        functools.partial(layer_kernel, len(parts)),
        out_shape=(jax.ShapeDtypeStruct((nodes, width), BF16),) * 4,
        compiler_params=params(),
        cost_estimate=pl.CostEstimate(
            flops=4 * nodes * width * width,
            bytes_accessed=2 * nodes * width * 10,
            transcendentals=nodes * width,
        ),
        name="layer",
    )(weight, bias_vector.reshape(1, -1), cotangent, *parts)


def weights_kernel(scale, pos_ref, agg_ref, grad_ref, mine_ref, theirs_ref):
    grad = grad_ref[...]
    product = scale * lax.dot_general(
        agg_ref[...], grad, (((0,), (0,)), ((), ())), preferred_element_type=F32
    )
    bias = scale * jnp.sum(grad.astype(F32).reshape(-1, 8, grad.shape[1]), axis=0)
    half = product.shape[0] // 2
    core = pos_ref[1] % 2
    for keep, give, parity in ((mine_ref, theirs_ref, 0), (theirs_ref, mine_ref, 1)):

        @pl.when(core == parity)
        def _(keep=keep, give=give):
            keep[:half] = product[:half]
            give[:half] = product[half:]

    mine_ref[half:] = bias
    theirs_ref[half:] = bias


def weight_partials(agg, grad, pos, scale):
    nodes, width = agg.shape
    return pl.pallas_call(
        functools.partial(weights_kernel, scale),
        out_shape=(jax.ShapeDtypeStruct((width // 2 + 8, width), F32),) * 2,
        in_specs=[pl.BlockSpec(memory_space=pltpu.SMEM)]
        + [pl.BlockSpec(memory_space=pltpu.VMEM)] * 2,
        compiler_params=params(),
        cost_estimate=pl.CostEstimate(
            flops=2 * nodes * width * width, bytes_accessed=6 * nodes * width, transcendentals=0
        ),
        name="weight_partials",
    )(pos, agg, grad)


def assemble_kernel(pos_ref, mine_ref, theirs_ref, weight_ref, bias_ref):
    half = weight_ref.shape[0] // 2
    core = pos_ref[1] % 2
    mine = pl.multiple_of(core * half, half)
    theirs = pl.multiple_of((1 - core) * half, half)
    weight_ref[pl.ds(mine, half), :] = mine_ref[:half]
    weight_ref[pl.ds(theirs, half), :] = theirs_ref[:half]
    bias_ref[...] = jnp.sum(mine_ref[half:], axis=0, keepdims=True)


def assemble(mine, theirs, pos):
    width = mine.shape[1]
    weight, bias = pl.pallas_call(
        assemble_kernel,
        out_shape=(
            jax.ShapeDtypeStruct((width, width), F32),
            jax.ShapeDtypeStruct((1, width), F32),
        ),
        in_specs=[pl.BlockSpec(memory_space=pltpu.SMEM)]
        + [pl.BlockSpec(memory_space=pltpu.VMEM)] * 2,
        compiler_params=params(),
        cost_estimate=pl.CostEstimate(
            flops=0, bytes_accessed=16 * width * width, transcendentals=0
        ),
        name="assemble",
    )(pos, mine, theirs)
    return weight, bias.reshape(width)


def back_product(dense, back):
    return lax.dot_general(
        dense, back, (((0,), (0,)), ((), ())), preferred_element_type=F32
    )


def backward_early_kernel(dense_ref, back_ref, out_ref):
    out_ref[...] = back_product(dense_ref[: back_ref.shape[0], :], back_ref[...])


def backward_early(dense, back):
    width, size = dense.shape[1], back.shape[1]
    return pl.pallas_call(
        backward_early_kernel,
        out_shape=jax.ShapeDtypeStruct((width, size), F32),
        compiler_params=params(),
        cost_estimate=pl.CostEstimate(
            flops=2 * width * back.size, bytes_accessed=6 * width * size, transcendentals=0
        ),
        name="backward_early",
    )(dense, back)


def backward_late_kernel(base, slots, peers, dense_ref, put_ref, first_ref, *rest):
    backs, outs, (joined, rows) = rest[: peers - 1], rest[peers - 1 : -2], rest[-2:]
    capacity = put_ref.shape[2]
    block = backs[0].shape[0]
    for peer in range(1, peers):
        joined[(peer - 1) * block : peer * block, :] = backs[peer - 1][...]
    columns = slice(base * capacity, (base + slots) * capacity)
    rows[...] = (
        first_ref[columns, :] + back_product(dense_ref[block:, columns], joined[...])
    ).astype(BF16)
    for slot in range(slots):
        outs[slot][...] = jnp.dot(
            put_ref[slot],
            rows[slot * capacity : (slot + 1) * capacity, :],
            preferred_element_type=F32,
        ).astype(outs[slot].dtype)


def backward_late(dense, put, first, backs, base):
    slots, nodes, capacity = put.shape
    size = first.shape[1]
    return pl.pallas_call(
        functools.partial(backward_late_kernel, base, slots, len(backs) + 1),
        out_shape=tuple(
            jax.ShapeDtypeStruct((nodes, size), BF16 if slot % 2 else F32)
            for slot in range(slots)
        ),
        scratch_shapes=[
            pltpu.VMEM((len(backs) * backs[0].shape[0], size), BF16),
            pltpu.VMEM((slots * capacity, size), BF16),
        ],
        compiler_params=params(),
        cost_estimate=pl.CostEstimate(
            flops=2 * slots * capacity * size * dense.shape[0],
            bytes_accessed=2 * dense.shape[0] * slots * capacity,
            transcendentals=0,
        ),
        name="backward_late",
    )(dense, put, first, *backs)


def backward_blocks_kernel(peers, slots, pos_ref, put_ref, dense_ref, *rest):
    backs, outs, total = rest[:peers], rest[peers : peers + slots], rest[peers + slots]
    step = pl.program_id(0)
    capacity = put_ref.shape[2]
    for peer in range(peers):

        @pl.when(step == peer)
        def _(peer=peer):
            product = lax.dot_general(
                dense_ref[...], backs[peer][...], (((0,), (0,)), ((), ())), preferred_element_type=F32
            )
            if peer == 0:
                total[...] = product
            else:
                total[...] += product

    @pl.when(step == peers - 1)
    def _():
        for slot in range(slots):
            rows = total[slot * capacity : (slot + 1) * capacity, :].astype(BF16)
            outs[slot][...] = jnp.dot(put_ref[slot], rows, preferred_element_type=F32).astype(
                outs[slot].dtype
            )


def backward_blocks(dense, put, backs, pos, kept):
    peers = len(backs)
    rows, width = dense.shape
    slots, nodes, _ = put.shape
    chunk = backs[0].shape[1]
    block = rows // peers
    return pl.pallas_call(
        functools.partial(backward_blocks_kernel, peers, slots),
        out_shape=tuple(
            jax.ShapeDtypeStruct((nodes, chunk), F32 if slot in kept else BF16)
            for slot in range(slots)
        ),
        grid_spec=pltpu.PrefetchScalarGridSpec(
            num_scalar_prefetch=1,
            grid=(peers,),
            in_specs=[
                full_spec(put.shape),
                pl.BlockSpec((block, width), lambda i, pos_ref: (i ^ pos_ref[0], 0)),
            ]
            + [full_spec((block, chunk))] * peers,
            out_specs=tuple(full_spec((nodes, chunk)) for _ in range(slots)),
            scratch_shapes=[pltpu.VMEM((width, chunk), F32)],
        ),
        compiler_params=params(BIG_LIMIT),
        cost_estimate=pl.CostEstimate(
            flops=2 * rows * width * chunk, bytes_accessed=2 * rows * width, transcendentals=0
        ),
        name="backward_rows",
    )(pos, put, dense, *backs)


def pair_sum_kernel(count, *refs):
    for i in range(count):
        total = refs[i][...].astype(F32) + refs[count + i][...].astype(F32)
        refs[2 * count + i][...] = total.astype(refs[2 * count + i].dtype)


def pair_sums(kept, received, wide=-1):
    count = len(kept)
    return pl.pallas_call(
        functools.partial(pair_sum_kernel, count),
        out_shape=tuple(
            jax.ShapeDtypeStruct(kept[i].shape, F32 if i == wide else BF16) for i in range(count)
        ),
        compiler_params=params(),
        cost_estimate=pl.CostEstimate(
            flops=0, bytes_accessed=count * kept[0].size * 8, transcendentals=0
        ),
        name="pair_sums",
    )(*kept, *received)


def finish_kernel(chunks, each, *refs):
    out_ref = refs[-1]
    size = out_ref.shape[1] // chunks
    for chunk in range(chunks):
        total = refs[chunk * each][...].astype(F32)
        for term in range(1, each):
            total = total + refs[chunk * each + term][...].astype(F32)
        out_ref[:, chunk * size : (chunk + 1) * size] = total.astype(BF16)


def finish(terms):
    chunks, each = len(terms), len(terms[0])
    nodes, size = terms[0][0].shape
    return pl.pallas_call(
        functools.partial(finish_kernel, chunks, each),
        out_shape=jax.ShapeDtypeStruct((nodes, size * chunks), BF16),
        compiler_params=params(),
        cost_estimate=pl.CostEstimate(
            flops=0, bytes_accessed=chunks * nodes * size * 2 * each, transcendentals=0
        ),
        name="finish",
    )(*[array for group in terms for array in group])


LINE_SWAP1 = z_pairs([(0, 1), (1, 0), (2, 3), (3, 2)])
LINE_SWAP2 = z_pairs([(0, 2), (2, 0), (1, 3), (3, 1)])
LINE_MIDDLE = z_pairs([(1, 2), (2, 1)])
LINE_OUT = z_pairs([(2, 3), (1, 0)])
LINE_IN = z_pairs([(3, 2), (0, 1)])
CORE = xor_pairs(8, 1)


def after(value, *others):
    return lax.optimization_barrier((value,) + others)[0]


def exchange_add(value, axis, size, step):
    return value + lax.ppermute(value, axis, xor_pairs(size, step))


def with_lists(features, list_rows, list_counts):
    live = jnp.arange(list_rows.shape[1])[None, :] < list_counts[:, None]
    high = jnp.where(live, list_rows // 256, -1)
    low = jnp.where(live, list_rows % 256, 0)
    return jnp.concatenate([features, high.astype(BF16), low.astype(BF16)], axis=0)


def line_exchange(piece, dense_of, pos, nodes, capacity, rows):
    far = lax.ppermute(piece, "col", LINE_SWAP2)
    near = lax.ppermute(piece, "col", LINE_SWAP1)
    other = lax.ppermute(piece, "col", CORE)
    dense = dense_of()
    far, dense = lax.optimization_barrier((far, dense))
    ends = lax.ppermute(far, "col", LINE_OUT)
    middle = lax.ppermute(after(piece, far), "col", LINE_MIDDLE)
    early = [[piece], [other], [near], [lax.ppermute(near, "col", CORE)], [far]]
    early.append([lax.ppermute(far, "col", CORE)])
    partial, put_early = forward_part(dense, early, 0, pos, rows, nodes, capacity)
    partial, middle, ends = lax.optimization_barrier((partial, middle, ends))
    late = [[middle, ends], [lax.ppermute(middle, "col", CORE), lax.ppermute(ends, "col", CORE)]]
    *blocks, put_late = forward_part(dense, late, 6, pos, rows, nodes, capacity, partial)
    return dense, put_early, put_late, blocks


def row_exchange(own, arrays, rows):
    received = [
        lax.ppermute(arrays[step - 1], "row", xor_pairs(rows, step))
        for step in reversed(range(1, rows))
    ]
    return [own] + received[::-1]


def line_reduce(dense, put_early, put_late, back, backs, pos, sums, rows, columns):
    first = backward_early(dense, back)
    sums = exchange_add(sums, "col", columns, 2)
    sums = exchange_add(sums, "col", columns, 4)
    *backs, first, sums = lax.optimization_barrier((*backs, first, sums))
    keep3, give3 = backward_late(dense, put_late, first, backs, 6)
    got3 = lax.ppermute(give3, "col", CORE)
    sums = exchange_add(sums, "row", rows, 1)
    keep0, give0, keep1, give1, keep2, give2 = backward_late(dense, put_early, first, backs, 0)
    got3, give2, give1, give0, keep0, sums = lax.optimization_barrier(
        (got3, give2, give1, give0, keep0, sums)
    )
    step = 2
    while step < rows:
        sums = exchange_add(sums, "row", rows, step)
        step *= 2
    (last,) = pair_sums([keep3], [got3])
    passed = lax.ppermute(last, "col", LINE_IN)
    middle = lax.ppermute(last, "col", LINE_MIDDLE)
    got = [lax.ppermute(give, "col", CORE) for give in (give0, give1, give2)]
    own, near, far = pair_sums([keep0, keep1, keep2], got, 0)
    passed, middle, sums = lax.optimization_barrier((passed, middle, sums))
    far = (far.astype(F32) + passed.astype(F32)).astype(BF16)
    from_far = lax.ppermute(far, "col", LINE_SWAP2)
    from_near = lax.ppermute(after(near, far), "col", LINE_SWAP1)
    return [own, middle, from_near, from_far], sums


def per_device(
    features,
    weight,
    bias_vector,
    send_rows,
    send_count,
    adjacency,
    source_tile,
    tile_count,
    cotangent,
):
    rows, columns = lax.axis_size("row"), lax.axis_size("col")
    nodes, width = features.shape
    capacity = send_rows.shape[3]
    tiles, source, count = adjacency[0, 0], source_tile[0, 0], tile_count[0, 0]
    pos = jnp.stack([lax.axis_index("row"), lax.axis_index("col")]).astype(jnp.int32)
    piece = with_lists(features, send_rows[0, 0], send_count[0, 0])
    line = columns == 8 and 2 * tiles.shape[0] * TILE * columns * capacity <= RESIDENT

    if line:
        dense, put_early, put_late, blocks = line_exchange(
            piece,
            lambda: densify(tiles, source, count, pos, rows, columns, capacity),
            pos,
            nodes,
            capacity,
            rows,
        )
    else:
        dense = densify_blocks(tiles, source, count, pos, columns, capacity)
        pieces = [piece] + [
            lax.ppermute(piece, "col", xor_pairs(columns, step)) for step in range(1, columns)
        ]
        here = lax.axis_index("col")
        lists = jnp.stack(
            [
                list_row(
                    lax.dynamic_index_in_dim(a, nodes + here, 0, keepdims=False),
                    lax.dynamic_index_in_dim(a, nodes + columns + here, 0, keepdims=False),
                )
                for a in pieces
            ]
        )
        pick, put = selectors(lists, nodes)
        blocks = forward_blocks(dense, pick, [[a[:nodes]] for a in pieces], pos, rows)

    parts = row_exchange(blocks[0], blocks[1:], rows)
    output, agg, grad_pre, back = layer(weight, bias_vector, cotangent, parts)
    backs = row_exchange(back, [back] * (rows - 1), rows)
    scale = 1.0 / math.sqrt(nodes * rows * columns)
    mine, theirs = weight_partials(agg, grad_pre, pos, scale)
    sums = mine + lax.ppermute(theirs, "col", CORE if line else xor_pairs(columns, 1))

    if line:
        terms, sums = line_reduce(
            dense, put_early, put_late, back, backs[1:], pos, sums, rows, columns
        )
    else:
        scattered = backward_blocks(dense, put, backs, pos, (0,))
        terms = [scattered[0]] + [
            lax.ppermute(scattered[step], "col", xor_pairs(columns, step))
            for step in range(1, columns)
        ]
        step = 2
        while step < columns:
            sums = exchange_add(sums, "col", columns, step)
            step *= 2
        step = 1
        while step < rows:
            sums = exchange_add(sums, "row", rows, step)
            step *= 2
    weight_grad, bias_grad = assemble(
        sums, lax.ppermute(sums, "col", xor_pairs(columns, 1)), pos
    )
    terms[-2], weight_grad, bias_grad = lax.optimization_barrier(
        (terms[-2], weight_grad, bias_grad)
    )
    return output, finish([terms]), weight_grad, bias_grad


def solution(mesh):
    in_specs = (
        P(("row", "col"), None),
        P(),
        P(),
        P("row", "col", None, None),
        P("row", "col", None),
        P("row", "col", None, None, None, None),
        P("row", "col", None, None),
        P("row", "col", None),
        P(("row", "col"), None),
    )
    out_specs = (P(("row", "col"), None), P(("row", "col"), None), P(), P())
    return jax.shard_map(
        per_device, mesh=mesh, in_specs=in_specs, out_specs=out_specs, check_vma=False
    )
```

time: 142 us -> 105 us (0.74)
  starting transfers between devices: 57.3 us -> 30.7 us
  waiting for transfers between devices: 30.9 us -> 50.6 us
  local copies, waits for them, and re-layouts: 20.5 us -> 1.36 us
  Pallas kernels: 28.4 us -> 18.9 us
    ppermute x53 -> x29, starting transfers between devices: 51.8 us -> 30.7 us  [the longest x6 7.04 us: row_exchange(): lax.ppermute(arrays[step - 1], 'row', xor_pairs(rows, step))]
    ppermute x53 -> x29, waiting for transfers between devices: 30.9 us -> 50.6 us  [the longest x6 12.4 us: row_exchange(): lax.ppermute(arrays[step - 1], 'row', xor_pairs(rows, step))]
    unnamed x41 -> x10, local copies, waits for them, and re-layouts: 19.5 us -> 1.36 us
    pallas_call x8 -> x9, Pallas kernels: 27.4 us -> 17.9 us  [the longest x1 5.68 us: densify(): pl.pallas_call(functools.partial(densify_kernel, capacity // TILE, target...]
    all_to_all x1 -> x0, starting transfers between devices: 5.47 us -> none  [per_device(): lax.all_to_all(jnp.where(live, list_rows, -1), 'col', split_axis=0, conca...]
    select_n x3 -> x0, other arithmetic: 1.44 us -> none  [the longest x1 1.4 us: per_device(): jnp.where(live, list_rows, -1)]
  transfers between devices with their start and end apart: 54 -> 29, of which waited for: 13 -> 16; matrix products, arithmetic and copies ran while one was open for 2% -> 0% of each run, Pallas kernels for 18% -> 13%
where the time goes in v2:
time: 105 us; the launch traced here: 104 us
  waiting for transfers between devices  50.6 us (48%)
  starting transfers between devices  30.7 us (29%)
  Pallas kernels  18.9 us (18%)
  other arithmetic  2 us (2%)
  local copies, waits for them, and re-layouts  1.36 us (1%)
    ppermute x6, waiting for transfers between devices, row_exchange(): lax.ppermute(arrays[step - 1], 'row', xor_pairs(rows, step))  12.4 us
    ppermute x4, waiting for transfers between devices, exchange_add(): return value + lax.ppermute(value, axis, xor_pairs(size, step))  10.6 us
    ppermute x6, starting transfers between devices, row_exchange(): lax.ppermute(arrays[step - 1], 'row', xor_pairs(rows, step))  7.04 us
    ppermute x1, waiting for transfers between devices, line_exchange(): ends = lax.ppermute(far, 'col', LINE_OUT)  6.73 us
    ppermute x1, waiting for transfers between devices, line_reduce(): from_near = lax.ppermute(after(near, far), 'col', LINE_SWAP1)  6.7 us
    pallas_call x1, Pallas kernels, densify(): pl.pallas_call(functools.partial(densify_kernel, capacity // TILE, target...  5.68 us
    ppermute x4, starting transfers between devices, exchange_add(): return value + lax.ppermute(value, axis, xor_pairs(size, step))  4.9 us
    pallas_call x2, Pallas kernels, forward_part(): pl.pallas_call(functools.partial(forward_part_kernel, tuple((len(group) f...  4.52 us
  transfers between devices with their start and end apart: 29, of which 16 were waited for; matrix products, arithmetic and copies ran while one was open for 0% of the time, Pallas kernels for 13%

profile of v2, /device:TPU:0, one launch (start us, length us, event | category | flops | bytes accessed | tf_op | source)
XLA Modules:
  0.0 104.4 jit_solution(2722522159743286477)
XLA Ops:
  2.4 4.1 %collective-permute-start = (bf16[528,256]{1,0:T(8,128)(2,1)S(1)}, bf16[528,256]{1,0:T(8,128)(2,1)S(1)}, u32[]{:S(2)}, u32[]{:S(2)}) collective-permute-start(bf16[528,256]{1,0:T(8,128)(2,1)S(1)} %pad_maximum_fusion.rest_0_), channel_id=1, source_target_pairs={{0,4},{1,5},{4,0},{5,1},{2,6},{3,7},{6,2},{7,3},{8,12},{9,13},{12,... | collective-permute-start | bytes 811016 | tf_op jit(solution)/shard_map/ppermute | solution.py:568
  6.5 1.6 %collective-permute-start.2 = (bf16[528,256]{1,0:T(8,128)(2,1)S(1)}, bf16[528,256]{1,0:T(8,128)(2,1)S(1)}, u32[]{:S(2)}, u32[]{:S(2)}) collective-permute-start(bf16[528,256]{1,0:T(8,128)(2,1)S(1)} %pad_maximum_fusion.rest_0_), channel_id=1, source_target_pairs={{0,2},{1,3},{2,0},{3,1},{4,6},{5,7},{6,4},{7,5},{8,10},{9,11},{10,... | collective-permute-start | bytes 811016 | tf_op jit(solution)/shard_map/ppermute | solution.py:569
  9.5 5.7 %densify.1.dense_ref = bf16[2048,2048]{1,0:T(8,128)(2,1)S(1)} custom-call(s32[16,16]{1,0:T(8,128)S(1)} %bitcast.34, s32[16]{0:T(128)S(1)} %bitcast.36, s32[2]{0:T(128)S(1)} %pad_add_fusion.pos_ref, bf16[16,16,128,128]{3,2,1,0:T(8,128)(2,1)} %bitcast.37), custom_call_target="tpu_custom_call" | custom-call | bytes 16777216 | tf_op jit(solution)/shard_map/densify/pallas_call | solution.py:63
  15.2 3.7 %collective-permute-done.rest_4_ = bf16[528,256]{1,0:T(8,128)(2,1)S(1)} collective-permute-done((bf16[528,256]{1,0:T(8,128)(2,1)S(1)}, bf16[528,256]{1,0:T(8,128)(2,1)S(1)}, u32[]{:S(2)}, u32[]{:S(2)}) %collective-permute-start) | collective-permute-done | bytes 270368 | tf_op jit(solution)/shard_map/ppermute | solution.py:568
  20.0 1.3 %collective-permute-start.6 = (bf16[528,256]{1,0:T(8,128)(2,1)S(1)}, bf16[528,256]{1,0:T(8,128)(2,1)S(1)}, u32[]{:S(2)}, u32[]{:S(2)}) collective-permute-start(bf16[528,256]{1,0:T(8,128)(2,1)S(1)} %collective-permute-done.rest_4_), channel_id=1, source_target_pairs={{4,6},{5,7},{2,0},{3,1},{12,14},{13,15},{10,8},{11,9},{20,22},{21,... | collective-permute-start | bytes 811016 | tf_op jit(solution)/shard_map/ppermute | solution.py:573
  21.4 2.9 %forward_early.1 = (f32[2048,256]{1,0:T(8,128)S(1)}, bf16[6,512,256]{2,1,0:T(8,128)(2,1)S(1)}) custom-call(s32[2]{0:T(128)S(1)} %pad_add_fusion.pos_ref, bf16[2048,2048]{1,0:T(8,128)(2,1)S(1)} %densify.1.dense_ref, bf16[528,256]{1,0:T(8,128)(2,1)S(1)} %pad_maximum_fusion.rest_0_, bf16[528,256]{1,0:T(8,128)(2,1)S(1)} %collective-permute-done.1.rest_1_, ...), custom_call_target="tpu_custom_call" | custom-call | flops 1610612736 | bytes 6291456 | tf_op jit(solution)/shard_map/forward_early/pallas_call | solution.py:211
  24.3 6.7 %collective-permute-done.6.rest_1_ = bf16[528,256]{1,0:T(8,128)(2,1)S(1)} collective-permute-done((bf16[528,256]{1,0:T(8,128)(2,1)S(1)}, bf16[528,256]{1,0:T(8,128)(2,1)S(1)}, u32[]{:S(2)}, u32[]{:S(2)}) %collective-permute-start.6) | collective-permute-done | bytes 270368 | tf_op jit(solution)/shard_map/ppermute | solution.py:573
  33.0 1.6 %forward_late.1 = (f32[512,256]{1,0:T(8,128)S(1)}, bf16[512,256]{1,0:T(8,128)(2,1)S(1)}, bf16[512,256]{1,0:T(8,128)(2,1)S(1)}, bf16[512,256]{1,0:T(8,128)(2,1)S(1)}, bf16[2,512,256]{2,1,0:T(8,128)(2,1)S(1)}) custom-call(s32[2]{0:T(128)S(1)} %pad_add_fusion.pos_ref, bf16[2048,2048]{1,0:T(8,128)(2,1)S(1)} %densify.1.dense_ref, ...), custom_call_target="tpu_custom_call" | custom-call | flops 536870912 | bytes 2097152 | tf_op jit(solution)/shard_map/forward_late/pallas_call | solution.py:211
  34.6 1.6 %collective-permute-start.10 = (bf16[512,256]{1,0:T(8,128)(2,1)S(1)}, bf16[512,256]{1,0:T(8,128)(2,1)S(1)}, u32[]{:S(2)}, u32[]{:S(2)}) collective-permute-start(bf16[512,256]{1,0:T(8,128)(2,1)S(1)} %get-tuple-element.63), channel_id=1, source_target_pairs={{0,16},{8,24},{16,0},{24,8},{1,17},{9,25},{17,1},{25,9},{2,18},{10... | collective-permute-start | bytes 786440 | tf_op jit(solution)/shard_map/ppermute | solution.py:586
  36.2 1.4 %collective-permute-start.11 = (bf16[512,256]{1,0:T(8,128)(2,1)S(1)}, bf16[512,256]{1,0:T(8,128)(2,1)S(1)}, u32[]{:S(2)}, u32[]{:S(2)}) collective-permute-start(bf16[512,256]{1,0:T(8,128)(2,1)S(1)} %get-tuple-element.64), channel_id=1, source_target_pairs={{0,24},{8,16},{16,8},{24,0},{1,25},{9,17},{17,9},{25,1},{2,26},{10... | collective-permute-start | bytes 786440 | tf_op jit(solution)/shard_map/ppermute | solution.py:586
  38.1 10.5 %collective-permute-done.10.rest_2_ = bf16[512,256]{1,0:T(8,128)(2,1)S(1)} collective-permute-done((bf16[512,256]{1,0:T(8,128)(2,1)S(1)}, bf16[512,256]{1,0:T(8,128)(2,1)S(1)}, u32[]{:S(2)}, u32[]{:S(2)}) %collective-permute-start.10) | collective-permute-done | bytes 262176 | tf_op jit(solution)/shard_map/ppermute | solution.py:586
  48.6 1.2 %collective-permute-done.9.rest_1_ = bf16[512,256]{1,0:T(8,128)(2,1)S(1)} collective-permute-done((bf16[512,256]{1,0:T(8,128)(2,1)S(1)}, bf16[512,256]{1,0:T(8,128)(2,1)S(1)}, u32[]{:S(2)}, u32[]{:S(2)}) %collective-permute-start.9) | collective-permute-done | bytes 262176 | tf_op jit(solution)/shard_map/ppermute | solution.py:586
  49.9 1.1 %layer.1 = (bf16[512,256]{1,0:T(8,128)(2,1)}, bf16[512,256]{1,0:T(8,128)(2,1)S(1)}, bf16[512,256]{1,0:T(8,128)(2,1)S(1)}, bf16[512,256]{1,0:T(8,128)(2,1)S(1)}) custom-call(bf16[256,256]{1,0:T(8,128)(2,1)S(1)} %copy-done.1, f32[1,256]{1,0:T(1,128)S(1)} %bitcast.35, bf16[512,256]{1,0:T(8,128)(2,1)S(1)} %copy-done, f32[512,256]{1,0:T(8,128)S(1)} %get-tuple-element.61.rest_0_, ...), custom_call_target="tpu_custom_call" | custom-call | flops 134217728 | bytes 2621440 | tf_op jit(solution)/shard_map/layer/pallas_call | solution.py:303
  52.1 1.3 %collective-permute-done.15 = f32[136,256]{1,0:T(8,128)S(1)} collective-permute-done((f32[136,256]{1,0:T(8,128)S(1)}, f32[136,256]{1,0:T(8,128)S(1)}, u32[]{:S(2)}, u32[]{:S(2)}) %collective-permute-start.15) | collective-permute-done | bytes 139296 | tf_op jit(solution)/shard_map/ppermute | solution.py:671
  53.9 1.5 %collective-permute-start.12 = (bf16[512,256]{1,0:T(8,128)(2,1)S(1)}, bf16[512,256]{1,0:T(8,128)(2,1)S(1)}, u32[]{:S(2)}, u32[]{:S(2)}) collective-permute-start(bf16[512,256]{1,0:T(8,128)(2,1)S(1)} %get-tuple-element.67.back_ref), channel_id=1, source_target_pairs={{0,8},{8,0},{16,24},{24,16},{1,9},{9,1},{17,25},{25,17},{2,10},{10... | collective-permute-start | bytes 786440 | tf_op jit(solution)/shard_map/ppermute | solution.py:586
  55.4 1.5 %collective-permute-start.13 = (bf16[512,256]{1,0:T(8,128)(2,1)S(1)}, bf16[512,256]{1,0:T(8,128)(2,1)S(1)}, u32[]{:S(2)}, u32[]{:S(2)}) collective-permute-start(bf16[512,256]{1,0:T(8,128)(2,1)S(1)} %get-tuple-element.67.back_ref), channel_id=1, source_target_pairs={{0,16},{8,24},{16,0},{24,8},{1,17},{9,25},{17,1},{25,9},{2,18},{10... | collective-permute-start | bytes 786440 | tf_op jit(solution)/shard_map/ppermute | solution.py:586
  57.4 1.9 %collective-permute-done.16 = f32[136,256]{1,0:T(8,128)S(1)} collective-permute-done((f32[136,256]{1,0:T(8,128)S(1)}, f32[136,256]{1,0:T(8,128)S(1)}, u32[]{:S(2)}, u32[]{:S(2)}) %collective-permute-start.16) | collective-permute-done | bytes 139296 | tf_op jit(solution)/shard_map/ppermute | solution.py:557
  59.3 1.6 %collective-permute-start.17 = (f32[136,256]{1,0:T(8,128)S(1)}, f32[136,256]{1,0:T(8,128)S(1)}, u32[]{:S(2)}, u32[]{:S(2)}) collective-permute-start(f32[136,256]{1,0:T(8,128)S(1)} %add.27), channel_id=1, source_target_pairs={{0,4},{1,5},{2,6},{3,7},{4,0},{5,1},{6,2},{7,3},{8,12},{9,13},{10,... | collective-permute-start | bytes 417800 | tf_op jit(solution)/shard_map/ppermute | solution.py:557
  61.7 6.4 %collective-permute-done.17 = f32[136,256]{1,0:T(8,128)S(1)} collective-permute-done((f32[136,256]{1,0:T(8,128)S(1)}, f32[136,256]{1,0:T(8,128)S(1)}, u32[]{:S(2)}, u32[]{:S(2)}) %collective-permute-start.17) | collective-permute-done | bytes 139296 | tf_op jit(solution)/shard_map/ppermute | solution.py:557
  68.8 1.0 backward_late.2
  69.9 1.3 %collective-permute-start.19 = (f32[136,256]{1,0:T(8,128)S(1)}, f32[136,256]{1,0:T(8,128)S(1)}, u32[]{:S(2)}, u32[]{:S(2)}) collective-permute-start(f32[136,256]{1,0:T(8,128)S(1)} %add.28), channel_id=1, source_target_pairs={{0,8},{8,0},{16,24},{24,16},{1,9},{9,1},{17,25},{25,17},{2,10},{10... | collective-permute-start | bytes 417800 | tf_op jit(solution)/shard_map/ppermute | solution.py:557
  71.2 2.5 %backward_late.3 = (f32[512,256]{1,0:T(8,128)S(1)}, bf16[512,256]{1,0:T(8,128)(2,1)S(1)}, f32[512,256]{1,0:T(8,128)S(1)}, bf16[512,256]{1,0:T(8,128)(2,1)S(1)}, ...) custom-call(bf16[2048,2048]{1,0:T(8,128)(2,1)S(1)} %densify.1.dense_ref, ...), custom_call_target="tpu_custom_call" | custom-call | flops 1610612736 | bytes 6291456 | tf_op jit(solution)/shard_map/backward_late/pallas_call | solution.py:423
  73.7 2.3 %collective-permute-done.19 = f32[136,256]{1,0:T(8,128)S(1)} collective-permute-done((f32[136,256]{1,0:T(8,128)S(1)}, f32[136,256]{1,0:T(8,128)S(1)}, u32[]{:S(2)}, u32[]{:S(2)}) %collective-permute-start.19) | collective-permute-done | bytes 139296 | tf_op jit(solution)/shard_map/ppermute | solution.py:557
  76.0 1.6 %collective-permute-start.25 = (f32[136,256]{1,0:T(8,128)S(1)}, f32[136,256]{1,0:T(8,128)S(1)}, u32[]{:S(2)}, u32[]{:S(2)}) collective-permute-start(f32[136,256]{1,0:T(8,128)S(1)} %add.29), channel_id=1, source_target_pairs={{0,16},{8,24},{16,0},{24,8},{1,17},{9,25},{17,1},{25,9},{2,18},{10... | collective-permute-start | bytes 417800 | tf_op jit(solution)/shard_map/ppermute | solution.py:557
  77.7 3.6 %collective-permute-start.23 = (bf16[512,256]{1,0:T(8,128)(2,1)S(1)}, bf16[512,256]{1,0:T(8,128)(2,1)S(1)}, u32[]{:S(2)}, u32[]{:S(2)}) collective-permute-start(bf16[512,256]{1,0:T(8,128)(2,1)S(1)} %pair_sums.3), channel_id=1, source_target_pairs={{6,4},{7,5},{0,2},{1,3},{14,12},{15,13},{8,10},{9,11},{22,20},{23,... | collective-permute-start | bytes 786440 | tf_op jit(solution)/shard_map/ppermute | solution.py:609
  82.6 3.7 %collective-permute-done.23 = bf16[512,256]{1,0:T(8,128)(2,1)S(1)} collective-permute-done((bf16[512,256]{1,0:T(8,128)(2,1)S(1)}, bf16[512,256]{1,0:T(8,128)(2,1)S(1)}, u32[]{:S(2)}, u32[]{:S(2)}) %collective-permute-start.23) | collective-permute-done | bytes 262176 | tf_op jit(solution)/shard_map/ppermute | solution.py:609
  86.6 3.9 %collective-permute-start.26 = (bf16[512,256]{1,0:T(8,128)(2,1)S(1)}, bf16[512,256]{1,0:T(8,128)(2,1)S(1)}, u32[]{:S(2)}, u32[]{:S(2)}) collective-permute-start(bf16[512,256]{1,0:T(8,128)(2,1)S(1)} %get-tuple-element.97), channel_id=1, source_target_pairs={{0,2},{1,3},{2,0},{3,1},{4,6},{5,7},{6,4},{7,5},{8,10},{9,11},{10,... | collective-permute-start | bytes 786440 | tf_op jit(solution)/shard_map/ppermute | solution.py:616
  90.5 1.2 %collective-permute-start.28 = (bf16[512,256]{1,0:T(8,128)(2,1)S(1)}, bf16[512,256]{1,0:T(8,128)(2,1)S(1)}, u32[]{:S(2)}, u32[]{:S(2)}) collective-permute-start(bf16[512,256]{1,0:T(8,128)(2,1)S(1)} %add_convert_fusion), channel_id=1, source_target_pairs={{0,4},{1,5},{4,0},{5,1},{2,6},{3,7},{6,2},{7,3},{8,12},{9,13},{12,... | collective-permute-start | bytes 786440 | tf_op jit(solution)/shard_map/ppermute | solution.py:615
  91.8 1.4 %collective-permute-done.27.theirs_ref = f32[136,256]{1,0:T(8,128)S(1)} collective-permute-done((f32[136,256]{1,0:T(8,128)S(1)}, f32[136,256]{1,0:T(8,128)S(1)}, u32[]{:S(2)}, u32[]{:S(2)}) %collective-permute-start.27) | collective-permute-done | bytes 139296 | tf_op jit(solution)/shard_map/ppermute | solution.py:692
  93.1 1.3 %assemble.1 = (f32[256,256]{1,0:T(8,128)}, f32[1,256]{1,0:T(1,128)}) custom-call(s32[2]{0:T(128)S(1)} %pad_add_fusion.pos_ref, f32[136,256]{1,0:T(8,128)S(1)} %add.30.mine_ref, f32[136,256]{1,0:T(8,128)S(1)} %collective-permute-done.27.theirs_ref), custom_call_target="tpu_custom_call" | custom-call | bytes 1048576 | tf_op jit(solution)/shard_map/assemble/pallas_call | solution.py:362
  94.4 6.7 %collective-permute-done.26.refs_2_ = bf16[512,256]{1,0:T(8,128)(2,1)S(1)} collective-permute-done((bf16[512,256]{1,0:T(8,128)(2,1)S(1)}, bf16[512,256]{1,0:T(8,128)(2,1)S(1)}, u32[]{:S(2)}, u32[]{:S(2)}) %collective-permute-start.26) | collective-permute-done | bytes 262176 | tf_op jit(solution)/shard_map/ppermute | solution.py:616
  101.1 2.5 %collective-permute-done.28.refs_3_ = bf16[512,256]{1,0:T(8,128)(2,1)S(1)} collective-permute-done((bf16[512,256]{1,0:T(8,128)(2,1)S(1)}, bf16[512,256]{1,0:T(8,128)(2,1)S(1)}, u32[]{:S(2)}, u32[]{:S(2)}) %collective-permute-start.28) | collective-permute-done | bytes 262176 | tf_op jit(solution)/shard_map/ppermute | solution.py:615
  (57 shorter events, 12.9 us)
Async XLA Ops:
  2.4 16.5 %collective-permute-start = (bf16[528,256]{1,0:T(8,128)(2,1)S(1)}, bf16[528,256]{1,0:T(8,128)(2,1)S(1)}, u32[]{:S(2)}, u32[]{:S(2)}) collective-permute-start(bf16[528,256]{1,0:T(8,128)(2,1)S(1)} %pad_maximum_fusion.rest_0_), channel_id=1, source_target_pairs={{0,4},{1,5},{4,0},{5,1},{2,6},{3,7},{6,2},{7,3},{8,12},{9,13},{12,... | collective-permute-start | bytes 811016 | tf_op jit(solution)/shard_map/ppermute | solution.py:568
  6.5 12.6 %collective-permute-start.2 = (bf16[528,256]{1,0:T(8,128)(2,1)S(1)}, bf16[528,256]{1,0:T(8,128)(2,1)S(1)}, u32[]{:S(2)}, u32[]{:S(2)}) collective-permute-start(bf16[528,256]{1,0:T(8,128)(2,1)S(1)} %pad_maximum_fusion.rest_0_), channel_id=1, source_target_pairs={{0,2},{1,3},{2,0},{3,1},{4,6},{5,7},{6,4},{7,5},{8,10},{9,11},{10,... | collective-permute-start | bytes 811016 | tf_op jit(solution)/shard_map/ppermute | solution.py:569
  8.1 13.3 %collective-permute-start.1 = (bf16[528,256]{1,0:T(8,128)(2,1)S(1)}, bf16[528,256]{1,0:T(8,128)(2,1)S(1)}, u32[]{:S(2)}, u32[]{:S(2)}) collective-permute-start(bf16[528,256]{1,0:T(8,128)(2,1)S(1)} %pad_maximum_fusion.rest_0_), channel_id=1, source_target_pairs={{0,1},{1,0},{2,3},{3,2},{4,5},{5,4},{6,7},{7,6},{8,9},{9,8},{10,11... | collective-permute-start | bytes 811016 | tf_op jit(solution)/shard_map/ppermute | solution.py:570
  18.9 2.5 %collective-permute-start.4 = (bf16[528,256]{1,0:T(8,128)(2,1)S(1)}, bf16[528,256]{1,0:T(8,128)(2,1)S(1)}, u32[]{:S(2)}, u32[]{:S(2)}) collective-permute-start(bf16[528,256]{1,0:T(8,128)(2,1)S(1)} %collective-permute-done.rest_4_), channel_id=1, source_target_pairs={{0,1},{1,0},{2,3},{3,2},{4,5},{5,4},{6,7},{7,6},{8,9},{9,8},{10,11... | collective-permute-start | bytes 811016 | tf_op jit(solution)/shard_map/ppermute | solution.py:576
  19.0 2.3 %collective-permute-start.3 = (bf16[528,256]{1,0:T(8,128)(2,1)S(1)}, bf16[528,256]{1,0:T(8,128)(2,1)S(1)}, u32[]{:S(2)}, u32[]{:S(2)}) collective-permute-start(bf16[528,256]{1,0:T(8,128)(2,1)S(1)} %collective-permute-done.2.rest_2_), channel_id=1, source_target_pairs={{0,1},{1,0},{2,3},{3,2},{4,5},{5,4},{6,7},{7,6},{8,9},{9,8},{10,11... | collective-permute-start | bytes 811016 | tf_op jit(solution)/shard_map/ppermute | solution.py:575
  19.4 4.9 %collective-permute-start.5 = (bf16[528,256]{1,0:T(8,128)(2,1)S(1)}, bf16[528,256]{1,0:T(8,128)(2,1)S(1)}, u32[]{:S(2)}, u32[]{:S(2)}) collective-permute-start(bf16[528,256]{1,0:T(8,128)(2,1)S(1)} %pad_maximum_fusion.rest_0_), channel_id=1, source_target_pairs={{2,4},{3,5},{4,2},{5,3},{10,12},{11,13},{12,10},{13,11},{18,20},{1... | collective-permute-start | bytes 811016 | tf_op jit(solution)/shard_map/ppermute | solution.py:574
  20.0 11.0 %collective-permute-start.6 = (bf16[528,256]{1,0:T(8,128)(2,1)S(1)}, bf16[528,256]{1,0:T(8,128)(2,1)S(1)}, u32[]{:S(2)}, u32[]{:S(2)}) collective-permute-start(bf16[528,256]{1,0:T(8,128)(2,1)S(1)} %collective-permute-done.rest_4_), channel_id=1, source_target_pairs={{4,6},{5,7},{2,0},{3,1},{12,14},{13,15},{10,8},{11,9},{20,22},{21,... | collective-permute-start | bytes 811016 | tf_op jit(solution)/shard_map/ppermute | solution.py:573
  31.0 18.8 %copy-start = (bf16[512,256]{1,0:T(8,128)(2,1)S(1)}, bf16[512,256]{1,0:T(8,128)(2,1)}, u32[]{:S(2)}) copy-start(bf16[512,256]{1,0:T(8,128)(2,1)} %cot_ref.1) | copy-start | bytes 786436
  31.0 18.8 %copy-start.1 = (bf16[256,256]{1,0:T(8,128)(2,1)S(1)}, bf16[256,256]{1,0:T(8,128)(2,1)}, u32[]{:S(2)}) copy-start(bf16[256,256]{1,0:T(8,128)(2,1)} %weight_ref.1) | copy-start | bytes 393220
  31.0 18.8 %copy-start.3 = (f32[256]{0:T(256)S(1)}, f32[256]{0:T(256)}, u32[]{:S(2)}) copy-start(f32[256]{0:T(256)} %param.11) | copy-start | bytes 3076
  31.0 1.5 %collective-permute-start.7 = (bf16[528,256]{1,0:T(8,128)(2,1)S(1)}, bf16[528,256]{1,0:T(8,128)(2,1)S(1)}, u32[]{:S(2)}, u32[]{:S(2)}) collective-permute-start(bf16[528,256]{1,0:T(8,128)(2,1)S(1)} %collective-permute-done.5.rest_0_), channel_id=1, source_target_pairs={{0,1},{1,0},{2,3},{3,2},{4,5},{5,4},{6,7},{7,6},{8,9},{9,8},{10,11... | collective-permute-start | bytes 811016 | tf_op jit(solution)/shard_map/ppermute | solution.py:579
  31.1 1.9 %collective-permute-start.8 = (bf16[528,256]{1,0:T(8,128)(2,1)S(1)}, bf16[528,256]{1,0:T(8,128)(2,1)S(1)}, u32[]{:S(2)}, u32[]{:S(2)}) collective-permute-start(bf16[528,256]{1,0:T(8,128)(2,1)S(1)} %collective-permute-done.6.rest_1_), channel_id=1, source_target_pairs={{0,1},{1,0},{2,3},{3,2},{4,5},{5,4},{6,7},{7,6},{8,9},{9,8},{10,11... | collective-permute-start | bytes 811016 | tf_op jit(solution)/shard_map/ppermute | solution.py:579
  34.6 14.0 %collective-permute-start.10 = (bf16[512,256]{1,0:T(8,128)(2,1)S(1)}, bf16[512,256]{1,0:T(8,128)(2,1)S(1)}, u32[]{:S(2)}, u32[]{:S(2)}) collective-permute-start(bf16[512,256]{1,0:T(8,128)(2,1)S(1)} %get-tuple-element.63), channel_id=1, source_target_pairs={{0,16},{8,24},{16,0},{24,8},{1,17},{9,25},{17,1},{25,9},{2,18},{10... | collective-permute-start | bytes 786440 | tf_op jit(solution)/shard_map/ppermute | solution.py:586
  36.2 12.4 %collective-permute-start.11 = (bf16[512,256]{1,0:T(8,128)(2,1)S(1)}, bf16[512,256]{1,0:T(8,128)(2,1)S(1)}, u32[]{:S(2)}, u32[]{:S(2)}) collective-permute-start(bf16[512,256]{1,0:T(8,128)(2,1)S(1)} %get-tuple-element.64), channel_id=1, source_target_pairs={{0,24},{8,16},{16,8},{24,0},{1,25},{9,17},{17,9},{25,1},{2,26},{10... | collective-permute-start | bytes 786440 | tf_op jit(solution)/shard_map/ppermute | solution.py:586
  37.6 12.2 %collective-permute-start.9 = (bf16[512,256]{1,0:T(8,128)(2,1)S(1)}, bf16[512,256]{1,0:T(8,128)(2,1)S(1)}, u32[]{:S(2)}, u32[]{:S(2)}) collective-permute-start(bf16[512,256]{1,0:T(8,128)(2,1)S(1)} %get-tuple-element.62), channel_id=1, source_target_pairs={{0,8},{8,0},{16,24},{24,16},{1,9},{9,1},{17,25},{25,17},{2,10},{10... | collective-permute-start | bytes 786440 | tf_op jit(solution)/shard_map/ppermute | solution.py:586
  52.0 1.4 %collective-permute-start.15 = (f32[136,256]{1,0:T(8,128)S(1)}, f32[136,256]{1,0:T(8,128)S(1)}, u32[]{:S(2)}, u32[]{:S(2)}) collective-permute-start(f32[136,256]{1,0:T(8,128)S(1)} %get-tuple-element.71), channel_id=1, source_target_pairs={{0,1},{1,0},{2,3},{3,2},{4,5},{5,4},{6,7},{7,6},{8,9},{9,8},{10,11... | collective-permute-start | bytes 417800 | tf_op jit(solution)/shard_map/ppermute | solution.py:671
  53.5 5.8 %collective-permute-start.16 = (f32[136,256]{1,0:T(8,128)S(1)}, f32[136,256]{1,0:T(8,128)S(1)}, u32[]{:S(2)}, u32[]{:S(2)}) collective-permute-start(f32[136,256]{1,0:T(8,128)S(1)} %add.26), channel_id=1, source_target_pairs={{0,2},{1,3},{2,0},{3,1},{4,6},{5,7},{6,4},{7,5},{8,10},{9,11},{10,... | collective-permute-start | bytes 417800 | tf_op jit(solution)/shard_map/ppermute | solution.py:557
  53.9 14.3 %collective-permute-start.12 = (bf16[512,256]{1,0:T(8,128)(2,1)S(1)}, bf16[512,256]{1,0:T(8,128)(2,1)S(1)}, u32[]{:S(2)}, u32[]{:S(2)}) collective-permute-start(bf16[512,256]{1,0:T(8,128)(2,1)S(1)} %get-tuple-element.67.back_ref), channel_id=1, source_target_pairs={{0,8},{8,0},{16,24},{24,16},{1,9},{9,1},{17,25},{25,17},{2,10},{10... | collective-permute-start | bytes 786440 | tf_op jit(solution)/shard_map/ppermute | solution.py:586
  55.4 13.4 %collective-permute-start.13 = (bf16[512,256]{1,0:T(8,128)(2,1)S(1)}, bf16[512,256]{1,0:T(8,128)(2,1)S(1)}, u32[]{:S(2)}, u32[]{:S(2)}) collective-permute-start(bf16[512,256]{1,0:T(8,128)(2,1)S(1)} %get-tuple-element.67.back_ref), channel_id=1, source_target_pairs={{0,16},{8,24},{16,0},{24,8},{1,17},{9,25},{17,1},{25,9},{2,18},{10... | collective-permute-start | bytes 786440 | tf_op jit(solution)/shard_map/ppermute | solution.py:586
  56.9 11.9 %collective-permute-start.14 = (bf16[512,256]{1,0:T(8,128)(2,1)S(1)}, bf16[512,256]{1,0:T(8,128)(2,1)S(1)}, u32[]{:S(2)}, u32[]{:S(2)}) collective-permute-start(bf16[512,256]{1,0:T(8,128)(2,1)S(1)} %get-tuple-element.67.back_ref), channel_id=1, source_target_pairs={{0,24},{8,16},{16,8},{24,0},{1,25},{9,17},{17,9},{25,1},{2,26},{10... | collective-permute-start | bytes 786440 | tf_op jit(solution)/shard_map/ppermute | solution.py:586
  59.3 8.8 %collective-permute-start.17 = (f32[136,256]{1,0:T(8,128)S(1)}, f32[136,256]{1,0:T(8,128)S(1)}, u32[]{:S(2)}, u32[]{:S(2)}) collective-permute-start(f32[136,256]{1,0:T(8,128)S(1)} %add.27), channel_id=1, source_target_pairs={{0,4},{1,5},{2,6},{3,7},{4,0},{5,1},{6,2},{7,3},{8,12},{9,13},{10,... | collective-permute-start | bytes 417800 | tf_op jit(solution)/shard_map/ppermute | solution.py:557
  69.8 6.2 %collective-permute-start.18 = (bf16[512,256]{1,0:T(8,128)(2,1)S(1)}, bf16[512,256]{1,0:T(8,128)(2,1)S(1)}, u32[]{:S(2)}, u32[]{:S(2)}) collective-permute-start(bf16[512,256]{1,0:T(8,128)(2,1)S(1)} %get-tuple-element.76), channel_id=1, source_target_pairs={{0,1},{1,0},{2,3},{3,2},{4,5},{5,4},{6,7},{7,6},{8,9},{9,8},{10,11... | collective-permute-start | bytes 786440 | tf_op jit(solution)/shard_map/ppermute | solution.py:598
  69.9 6.1 %collective-permute-start.19 = (f32[136,256]{1,0:T(8,128)S(1)}, f32[136,256]{1,0:T(8,128)S(1)}, u32[]{:S(2)}, u32[]{:S(2)}) collective-permute-start(f32[136,256]{1,0:T(8,128)S(1)} %add.28), channel_id=1, source_target_pairs={{0,8},{8,0},{16,24},{24,16},{1,9},{9,1},{17,25},{25,17},{2,10},{10... | collective-permute-start | bytes 417800 | tf_op jit(solution)/shard_map/ppermute | solution.py:557
  76.0 6.5 %collective-permute-start.25 = (f32[136,256]{1,0:T(8,128)S(1)}, f32[136,256]{1,0:T(8,128)S(1)}, u32[]{:S(2)}, u32[]{:S(2)}) collective-permute-start(f32[136,256]{1,0:T(8,128)S(1)} %add.29), channel_id=1, source_target_pairs={{0,16},{8,24},{16,0},{24,8},{1,17},{9,25},{17,1},{25,9},{2,18},{10... | collective-permute-start | bytes 417800 | tf_op jit(solution)/shard_map/ppermute | solution.py:557
  77.7 8.7 %collective-permute-start.23 = (bf16[512,256]{1,0:T(8,128)(2,1)S(1)}, bf16[512,256]{1,0:T(8,128)(2,1)S(1)}, u32[]{:S(2)}, u32[]{:S(2)}) collective-permute-start(bf16[512,256]{1,0:T(8,128)(2,1)S(1)} %pair_sums.3), channel_id=1, source_target_pairs={{6,4},{7,5},{0,2},{1,3},{14,12},{15,13},{8,10},{9,11},{22,20},{23,... | collective-permute-start | bytes 786440 | tf_op jit(solution)/shard_map/ppermute | solution.py:609
  81.3 5.1 %collective-permute-start.24 = (bf16[512,256]{1,0:T(8,128)(2,1)S(1)}, bf16[512,256]{1,0:T(8,128)(2,1)S(1)}, u32[]{:S(2)}, u32[]{:S(2)}) collective-permute-start(bf16[512,256]{1,0:T(8,128)(2,1)S(1)} %pair_sums.3), channel_id=1, source_target_pairs={{2,4},{3,5},{4,2},{5,3},{10,12},{11,13},{12,10},{13,11},{18,20},{1... | collective-permute-start | bytes 786440 | tf_op jit(solution)/shard_map/ppermute | solution.py:610
  81.9 4.4 %collective-permute-start.20 = (bf16[512,256]{1,0:T(8,128)(2,1)S(1)}, bf16[512,256]{1,0:T(8,128)(2,1)S(1)}, u32[]{:S(2)}, u32[]{:S(2)}) collective-permute-start(bf16[512,256]{1,0:T(8,128)(2,1)S(1)} %get-tuple-element.86), channel_id=1, source_target_pairs={{0,1},{1,0},{2,3},{3,2},{4,5},{5,4},{6,7},{7,6},{8,9},{9,8},{10,11... | collective-permute-start | bytes 786440 | tf_op jit(solution)/shard_map/ppermute | solution.py:611
  82.0 4.3 %collective-permute-start.21 = (bf16[512,256]{1,0:T(8,128)(2,1)S(1)}, bf16[512,256]{1,0:T(8,128)(2,1)S(1)}, u32[]{:S(2)}, u32[]{:S(2)}) collective-permute-start(bf16[512,256]{1,0:T(8,128)(2,1)S(1)} %get-tuple-element.87), channel_id=1, source_target_pairs={{0,1},{1,0},{2,3},{3,2},{4,5},{5,4},{6,7},{7,6},{8,9},{9,8},{10,11... | collective-permute-start | bytes 786440 | tf_op jit(solution)/shard_map/ppermute | solution.py:611
  82.5 3.8 %collective-permute-start.22 = (bf16[512,256]{1,0:T(8,128)(2,1)S(1)}, bf16[512,256]{1,0:T(8,128)(2,1)S(1)}, u32[]{:S(2)}, u32[]{:S(2)}) collective-permute-start(bf16[512,256]{1,0:T(8,128)(2,1)S(1)} %get-tuple-element.88), channel_id=1, source_target_pairs={{0,1},{1,0},{2,3},{3,2},{4,5},{5,4},{6,7},{7,6},{8,9},{9,8},{10,11... | collective-permute-start | bytes 786440 | tf_op jit(solution)/shard_map/ppermute | solution.py:611
  86.6 14.5 %collective-permute-start.26 = (bf16[512,256]{1,0:T(8,128)(2,1)S(1)}, bf16[512,256]{1,0:T(8,128)(2,1)S(1)}, u32[]{:S(2)}, u32[]{:S(2)}) collective-permute-start(bf16[512,256]{1,0:T(8,128)(2,1)S(1)} %get-tuple-element.97), channel_id=1, source_target_pairs={{0,2},{1,3},{2,0},{3,1},{4,6},{5,7},{6,4},{7,5},{8,10},{9,11},{10,... | collective-permute-start | bytes 786440 | tf_op jit(solution)/shard_map/ppermute | solution.py:616
  90.5 13.1 %collective-permute-start.28 = (bf16[512,256]{1,0:T(8,128)(2,1)S(1)}, bf16[512,256]{1,0:T(8,128)(2,1)S(1)}, u32[]{:S(2)}, u32[]{:S(2)}) collective-permute-start(bf16[512,256]{1,0:T(8,128)(2,1)S(1)} %add_convert_fusion), channel_id=1, source_target_pairs={{0,4},{1,5},{4,0},{5,1},{2,6},{3,7},{6,2},{7,3},{8,12},{9,13},{12,... | collective-permute-start | bytes 786440 | tf_op jit(solution)/shard_map/ppermute | solution.py:615
  91.8 1.4 %collective-permute-start.27 = (f32[136,256]{1,0:T(8,128)S(1)}, f32[136,256]{1,0:T(8,128)S(1)}, u32[]{:S(2)}, u32[]{:S(2)}) collective-permute-start(f32[136,256]{1,0:T(8,128)S(1)} %add.30.mine_ref), channel_id=1, source_target_pairs={{0,1},{1,0},{2,3},{3,2},{4,5},{5,4},{6,7},{7,6},{8,9},{9,8},{10,11... | collective-permute-start | bytes 417800 | tf_op jit(solution)/shard_map/ppermute | solution.py:692
  (2 other events, 1.4 us)

commit v3 on v2

--- a/solution.py
+++ b/solution.py
@@ -596,23 +596,23 @@
     *backs, first, sums = lax.optimization_barrier((*backs, first, sums))
     keep3, give3 = backward_late(dense, put_late, first, backs, 6)
     got3 = lax.ppermute(give3, "col", CORE)
-    sums = exchange_add(sums, "row", rows, 1)
+    received = lax.ppermute(sums, "row", xor_pairs(rows, 1))
     keep0, give0, keep1, give1, keep2, give2 = backward_late(dense, put_early, first, backs, 0)
-    got3, give2, give1, give0, keep0, sums = lax.optimization_barrier(
-        (got3, give2, give1, give0, keep0, sums)
-    )
-    step = 2
-    while step < rows:
-        sums = exchange_add(sums, "row", rows, step)
-        step *= 2
+    got3, give2, give1, give0, keep0 = lax.optimization_barrier((got3, give2, give1, give0, keep0))
     (last,) = pair_sums([keep3], [got3])
     passed = lax.ppermute(last, "col", LINE_IN)
     middle = lax.ppermute(last, "col", LINE_MIDDLE)
     got = [lax.ppermute(give, "col", CORE) for give in (give0, give1, give2)]
     own, near, far = pair_sums([keep0, keep1, keep2], got, 0)
-    passed, middle, sums = lax.optimization_barrier((passed, middle, sums))
+    sums = sums + after(received, own)
+    step = 2
+    while step < rows:
+        sums = exchange_add(sums, "row", rows, step)
+        step *= 2
+    passed, middle = lax.optimization_barrier((passed, middle))
     far = (far.astype(F32) + passed.astype(F32)).astype(BF16)
     from_far = lax.ppermute(far, "col", LINE_SWAP2)
+    near, sums = lax.optimization_barrier((near, sums))
     from_near = lax.ppermute(after(near, far), "col", LINE_SWAP1)
     return [own, middle, from_near, from_far], sums
 
@@ -691,8 +691,8 @@
     weight_grad, bias_grad = assemble(
         sums, lax.ppermute(sums, "col", xor_pairs(columns, 1)), pos
     )
-    terms[-2], weight_grad, bias_grad = lax.optimization_barrier(
-        (terms[-2], weight_grad, bias_grad)
+    terms[-1], weight_grad, bias_grad = lax.optimization_barrier(
+        (terms[-1], weight_grad, bias_grad)
     )
     return output, finish([terms]), weight_grad, bias_grad
 

time: 105 us -> 101 us (0.962)
  waiting for transfers between devices: 50.6 us -> 46 us
    ppermute x1, waiting for transfers between devices: 6.7 us -> 0.32 us  [line_reduce(): from_near = lax.ppermute(after(near, far), 'col', LINE_SWAP1)]
    ppermute x0 -> x1, waiting for transfers between devices: none -> 4.01 us  [line_reduce(): received = lax.ppermute(sums, 'row', xor_pairs(rows, 1))]
    ppermute x1, waiting for transfers between devices: 3.71 us -> 0.01 us  [line_reduce(): passed = lax.ppermute(last, 'col', LINE_IN)]
    ppermute x1, waiting for transfers between devices: 2.47 us -> 5.96 us  [line_reduce(): from_far = lax.ppermute(far, 'col', LINE_SWAP2)]
    ppermute x4 -> x3, waiting for transfers between devices: 10.6 us -> 8.61 us  [exchange_add(): return value + lax.ppermute(value, axis, xor_pairs(size, step))]
    ppermute x1, starting transfers between devices: 1.25 us -> 3.14 us  [line_reduce(): from_far = lax.ppermute(far, 'col', LINE_SWAP2)]
    ppermute x1, starting transfers between devices: 3.93 us -> 2.5 us  [line_reduce(): from_near = lax.ppermute(after(near, far), 'col', LINE_SWAP1)]
    ppermute x4 -> x3, starting transfers between devices: 4.9 us -> 3.61 us  [exchange_add(): return value + lax.ppermute(value, axis, xor_pairs(size, step))]
where the time goes in v3:
time: 101 us
  waiting for transfers between devices  46 us (46%)
  starting transfers between devices  31.5 us (31%)
  Pallas kernels  18.9 us (19%)
  other arithmetic  1.98 us (2%)
  local copies, waits for them, and re-layouts  1.36 us (1%)
    ppermute x6, waiting for transfers between devices, row_exchange(): lax.ppermute(arrays[step - 1], 'row', xor_pairs(rows, step))  12.4 us
    ppermute x3, waiting for transfers between devices, exchange_add(): return value + lax.ppermute(value, axis, xor_pairs(size, step))  8.61 us
    ppermute x6, starting transfers between devices, row_exchange(): lax.ppermute(arrays[step - 1], 'row', xor_pairs(rows, step))  7.04 us
    ppermute x1, waiting for transfers between devices, line_exchange(): ends = lax.ppermute(far, 'col', LINE_OUT)  6.73 us
    ppermute x1, waiting for transfers between devices, line_reduce(): from_far = lax.ppermute(far, 'col', LINE_SWAP2)  5.96 us
    pallas_call x1, Pallas kernels, densify(): pl.pallas_call(functools.partial(densify_kernel, capacity // TILE, target...  5.66 us
    pallas_call x2, Pallas kernels, forward_part(): pl.pallas_call(functools.partial(forward_part_kernel, tuple((len(group) f...  4.52 us
    ppermute x1, starting transfers between devices, line_exchange(): far = lax.ppermute(piece, 'col', LINE_SWAP2)  4.1 us
  transfers between devices with their start and end apart: 29, of which 16 were waited for; matrix products, arithmetic and copies ran while one was open for 0% of the time, Pallas kernels for 13%

profile of v3, /device:TPU:0, one launch (start us, length us, event | category | flops | bytes accessed | tf_op | source)
XLA Modules:
  0.0 100.6 jit_solution(11608377176755999870)
XLA Ops:
  2.4 4.1 %collective-permute-start = (bf16[528,256]{1,0:T(8,128)(2,1)S(1)}, bf16[528,256]{1,0:T(8,128)(2,1)S(1)}, u32[]{:S(2)}, u32[]{:S(2)}) collective-permute-start(bf16[528,256]{1,0:T(8,128)(2,1)S(1)} %pad_maximum_fusion.rest_0_), channel_id=1, source_target_pairs={{0,4},{1,5},{4,0},{5,1},{2,6},{3,7},{6,2},{7,3},{8,12},{9,13},{12,... | collective-permute-start | bytes 811016 | tf_op jit(solution)/shard_map/ppermute | solution.py:568
  6.5 1.6 %collective-permute-start.2 = (bf16[528,256]{1,0:T(8,128)(2,1)S(1)}, bf16[528,256]{1,0:T(8,128)(2,1)S(1)}, u32[]{:S(2)}, u32[]{:S(2)}) collective-permute-start(bf16[528,256]{1,0:T(8,128)(2,1)S(1)} %pad_maximum_fusion.rest_0_), channel_id=1, source_target_pairs={{0,2},{1,3},{2,0},{3,1},{4,6},{5,7},{6,4},{7,5},{8,10},{9,11},{10,... | collective-permute-start | bytes 811016 | tf_op jit(solution)/shard_map/ppermute | solution.py:569
  9.5 5.7 %densify.1.dense_ref = bf16[2048,2048]{1,0:T(8,128)(2,1)S(1)} custom-call(s32[16,16]{1,0:T(8,128)S(1)} %bitcast.34, s32[16]{0:T(128)S(1)} %bitcast.36, s32[2]{0:T(128)S(1)} %pad_add_fusion.pos_ref, bf16[16,16,128,128]{3,2,1,0:T(8,128)(2,1)} %bitcast.37), custom_call_target="tpu_custom_call" | custom-call | bytes 16777216 | tf_op jit(solution)/shard_map/densify/pallas_call | solution.py:63
  15.2 3.7 %collective-permute-done.rest_4_ = bf16[528,256]{1,0:T(8,128)(2,1)S(1)} collective-permute-done((bf16[528,256]{1,0:T(8,128)(2,1)S(1)}, bf16[528,256]{1,0:T(8,128)(2,1)S(1)}, u32[]{:S(2)}, u32[]{:S(2)}) %collective-permute-start) | collective-permute-done | bytes 270368 | tf_op jit(solution)/shard_map/ppermute | solution.py:568
  20.0 1.3 %collective-permute-start.6 = (bf16[528,256]{1,0:T(8,128)(2,1)S(1)}, bf16[528,256]{1,0:T(8,128)(2,1)S(1)}, u32[]{:S(2)}, u32[]{:S(2)}) collective-permute-start(bf16[528,256]{1,0:T(8,128)(2,1)S(1)} %collective-permute-done.rest_4_), channel_id=1, source_target_pairs={{4,6},{5,7},{2,0},{3,1},{12,14},{13,15},{10,8},{11,9},{20,22},{21,... | collective-permute-start | bytes 811016 | tf_op jit(solution)/shard_map/ppermute | solution.py:573
  21.4 2.9 %forward_early.1 = (f32[2048,256]{1,0:T(8,128)S(1)}, bf16[6,512,256]{2,1,0:T(8,128)(2,1)S(1)}) custom-call(s32[2]{0:T(128)S(1)} %pad_add_fusion.pos_ref, bf16[2048,2048]{1,0:T(8,128)(2,1)S(1)} %densify.1.dense_ref, bf16[528,256]{1,0:T(8,128)(2,1)S(1)} %pad_maximum_fusion.rest_0_, bf16[528,256]{1,0:T(8,128)(2,1)S(1)} %collective-permute-done.1.rest_1_, ...), custom_call_target="tpu_custom_call" | custom-call | flops 1610612736 | bytes 6291456 | tf_op jit(solution)/shard_map/forward_early/pallas_call | solution.py:211
  24.3 6.7 %collective-permute-done.6.rest_1_ = bf16[528,256]{1,0:T(8,128)(2,1)S(1)} collective-permute-done((bf16[528,256]{1,0:T(8,128)(2,1)S(1)}, bf16[528,256]{1,0:T(8,128)(2,1)S(1)}, u32[]{:S(2)}, u32[]{:S(2)}) %collective-permute-start.6) | collective-permute-done | bytes 270368 | tf_op jit(solution)/shard_map/ppermute | solution.py:573
  31.6 1.0 %collective-permute-done.7.rest_2_ = bf16[528,256]{1,0:T(8,128)(2,1)S(1)} collective-permute-done((bf16[528,256]{1,0:T(8,128)(2,1)S(1)}, bf16[528,256]{1,0:T(8,128)(2,1)S(1)}, u32[]{:S(2)}, u32[]{:S(2)}) %collective-permute-start.7) | collective-permute-done | bytes 270368 | tf_op jit(solution)/shard_map/ppermute | solution.py:579
  33.0 1.6 %forward_late.1 = (f32[512,256]{1,0:T(8,128)S(1)}, bf16[512,256]{1,0:T(8,128)(2,1)S(1)}, bf16[512,256]{1,0:T(8,128)(2,1)S(1)}, bf16[512,256]{1,0:T(8,128)(2,1)S(1)}, bf16[2,512,256]{2,1,0:T(8,128)(2,1)S(1)}) custom-call(s32[2]{0:T(128)S(1)} %pad_add_fusion.pos_ref, bf16[2048,2048]{1,0:T(8,128)(2,1)S(1)} %densify.1.dense_ref, ...), custom_call_target="tpu_custom_call" | custom-call | flops 536870912 | bytes 2097152 | tf_op jit(solution)/shard_map/forward_late/pallas_call | solution.py:211
  34.6 1.6 %collective-permute-start.10 = (bf16[512,256]{1,0:T(8,128)(2,1)S(1)}, bf16[512,256]{1,0:T(8,128)(2,1)S(1)}, u32[]{:S(2)}, u32[]{:S(2)}) collective-permute-start(bf16[512,256]{1,0:T(8,128)(2,1)S(1)} %get-tuple-element.64), channel_id=1, source_target_pairs={{0,16},{8,24},{16,0},{24,8},{1,17},{9,25},{17,1},{25,9},{2,18},{10... | collective-permute-start | bytes 786440 | tf_op jit(solution)/shard_map/ppermute | solution.py:586
  36.2 1.4 %collective-permute-start.11 = (bf16[512,256]{1,0:T(8,128)(2,1)S(1)}, bf16[512,256]{1,0:T(8,128)(2,1)S(1)}, u32[]{:S(2)}, u32[]{:S(2)}) collective-permute-start(bf16[512,256]{1,0:T(8,128)(2,1)S(1)} %get-tuple-element.65), channel_id=1, source_target_pairs={{0,24},{8,16},{16,8},{24,0},{1,25},{9,17},{17,9},{25,1},{2,26},{10... | collective-permute-start | bytes 786440 | tf_op jit(solution)/shard_map/ppermute | solution.py:586
  38.1 10.5 %collective-permute-done.10.rest_2_ = bf16[512,256]{1,0:T(8,128)(2,1)S(1)} collective-permute-done((bf16[512,256]{1,0:T(8,128)(2,1)S(1)}, bf16[512,256]{1,0:T(8,128)(2,1)S(1)}, u32[]{:S(2)}, u32[]{:S(2)}) %collective-permute-start.10) | collective-permute-done | bytes 262176 | tf_op jit(solution)/shard_map/ppermute | solution.py:586
  48.6 1.2 %collective-permute-done.9.rest_1_ = bf16[512,256]{1,0:T(8,128)(2,1)S(1)} collective-permute-done((bf16[512,256]{1,0:T(8,128)(2,1)S(1)}, bf16[512,256]{1,0:T(8,128)(2,1)S(1)}, u32[]{:S(2)}, u32[]{:S(2)}) %collective-permute-start.9) | collective-permute-done | bytes 262176 | tf_op jit(solution)/shard_map/ppermute | solution.py:586
  49.9 1.1 %layer.1 = (bf16[512,256]{1,0:T(8,128)(2,1)}, bf16[512,256]{1,0:T(8,128)(2,1)S(1)}, bf16[512,256]{1,0:T(8,128)(2,1)S(1)}, bf16[512,256]{1,0:T(8,128)(2,1)S(1)}) custom-call(bf16[256,256]{1,0:T(8,128)(2,1)S(1)} %copy-done.1, f32[1,256]{1,0:T(1,128)S(1)} %bitcast.35, bf16[512,256]{1,0:T(8,128)(2,1)S(1)} %copy-done, f32[512,256]{1,0:T(8,128)S(1)} %get-tuple-element.62.rest_0_, ...), custom_call_target="tpu_custom_call" | custom-call | flops 134217728 | bytes 2621440 | tf_op jit(solution)/shard_map/layer/pallas_call | solution.py:303
  51.0 1.0 %weight_partials.1 = (f32[136,256]{1,0:T(8,128)S(1)}, f32[136,256]{1,0:T(8,128)S(1)}) custom-call(s32[2]{0:T(128)S(1)} %pad_add_fusion.pos_ref, bf16[512,256]{1,0:T(8,128)(2,1)S(1)} %get-tuple-element.69.agg_ref, bf16[512,256]{1,0:T(8,128)(2,1)S(1)} %get-tuple-element.70.grad_ref), custom_call_target="tpu_custom_call" | custom-call | flops 67108864 | bytes 786432 | tf_op jit(solution)/shard_map/weight_partials/pallas_call | solution.py:337
  52.1 1.3 %collective-permute-done.15 = f32[136,256]{1,0:T(8,128)S(1)} collective-permute-done((f32[136,256]{1,0:T(8,128)S(1)}, f32[136,256]{1,0:T(8,128)S(1)}, u32[]{:S(2)}, u32[]{:S(2)}) %collective-permute-start.15) | collective-permute-done | bytes 139296 | tf_op jit(solution)/shard_map/ppermute | solution.py:671
  53.9 1.5 %collective-permute-start.12 = (bf16[512,256]{1,0:T(8,128)(2,1)S(1)}, bf16[512,256]{1,0:T(8,128)(2,1)S(1)}, u32[]{:S(2)}, u32[]{:S(2)}) collective-permute-start(bf16[512,256]{1,0:T(8,128)(2,1)S(1)} %get-tuple-element.68.back_ref), channel_id=1, source_target_pairs={{0,8},{8,0},{16,24},{24,16},{1,9},{9,1},{17,25},{25,17},{2,10},{10... | collective-permute-start | bytes 786440 | tf_op jit(solution)/shard_map/ppermute | solution.py:586
  55.4 1.5 %collective-permute-start.13 = (bf16[512,256]{1,0:T(8,128)(2,1)S(1)}, bf16[512,256]{1,0:T(8,128)(2,1)S(1)}, u32[]{:S(2)}, u32[]{:S(2)}) collective-permute-start(bf16[512,256]{1,0:T(8,128)(2,1)S(1)} %get-tuple-element.68.back_ref), channel_id=1, source_target_pairs={{0,16},{8,24},{16,0},{24,8},{1,17},{9,25},{17,1},{25,9},{2,18},{10... | collective-permute-start | bytes 786440 | tf_op jit(solution)/shard_map/ppermute | solution.py:586
  57.4 1.9 %collective-permute-done.16 = f32[136,256]{1,0:T(8,128)S(1)} collective-permute-done((f32[136,256]{1,0:T(8,128)S(1)}, f32[136,256]{1,0:T(8,128)S(1)}, u32[]{:S(2)}, u32[]{:S(2)}) %collective-permute-start.16) | collective-permute-done | bytes 139296 | tf_op jit(solution)/shard_map/ppermute | solution.py:557
  59.3 1.6 %collective-permute-start.17 = (f32[136,256]{1,0:T(8,128)S(1)}, f32[136,256]{1,0:T(8,128)S(1)}, u32[]{:S(2)}, u32[]{:S(2)}) collective-permute-start(f32[136,256]{1,0:T(8,128)S(1)} %add.27), channel_id=1, source_target_pairs={{0,4},{1,5},{2,6},{3,7},{4,0},{5,1},{6,2},{7,3},{8,12},{9,13},{10,... | collective-permute-start | bytes 417800 | tf_op jit(solution)/shard_map/ppermute | solution.py:557
  61.7 6.4 %collective-permute-done.17 = f32[136,256]{1,0:T(8,128)S(1)} collective-permute-done((f32[136,256]{1,0:T(8,128)S(1)}, f32[136,256]{1,0:T(8,128)S(1)}, u32[]{:S(2)}, u32[]{:S(2)}) %collective-permute-start.17) | collective-permute-done | bytes 139296 | tf_op jit(solution)/shard_map/ppermute | solution.py:557
  68.8 1.0 %backward_late.2 = (f32[512,256]{1,0:T(8,128)S(1)}, bf16[512,256]{1,0:T(8,128)(2,1)S(1)}) custom-call(bf16[2048,2048]{1,0:T(8,128)(2,1)S(1)} %densify.1.dense_ref, bf16[2,512,256]{2,1,0:T(8,128)(2,1)S(1)} %get-tuple-element.67.put_ref, f32[2048,256]{1,0:T(8,128)S(1)} %backward_early.1.first_ref, bf16[512,256]{1,0:T(8,128)(2,1)S(1)} %collective-permute-done.12.rest_0_, ...), custom_call_target="tpu_custom_call" | custom-call | flops 536870912 | bytes 2097152 | tf_op jit(solution)/shard_map/backward_late/pallas_call | solution.py:423
  69.9 2.5 %backward_late.3 = (f32[512,256]{1,0:T(8,128)S(1)}, bf16[512,256]{1,0:T(8,128)(2,1)S(1)}, f32[512,256]{1,0:T(8,128)S(1)}, bf16[512,256]{1,0:T(8,128)(2,1)S(1)}, ...) custom-call(bf16[2048,2048]{1,0:T(8,128)(2,1)S(1)} %densify.1.dense_ref, ...), custom_call_target="tpu_custom_call" | custom-call | flops 1610612736 | bytes 6291456 | tf_op jit(solution)/shard_map/backward_late/pallas_call | solution.py:423
  73.5 3.6 %collective-permute-start.22 = (bf16[512,256]{1,0:T(8,128)(2,1)S(1)}, bf16[512,256]{1,0:T(8,128)(2,1)S(1)}, u32[]{:S(2)}, u32[]{:S(2)}) collective-permute-start(bf16[512,256]{1,0:T(8,128)(2,1)S(1)} %pair_sums.3), channel_id=1, source_target_pairs={{6,4},{7,5},{0,2},{1,3},{14,12},{15,13},{8,10},{9,11},{22,20},{23,... | collective-permute-start | bytes 786440 | tf_op jit(solution)/shard_map/ppermute | solution.py:603
  77.8 1.3 %collective-permute-start.24 = (f32[136,256]{1,0:T(8,128)S(1)}, f32[136,256]{1,0:T(8,128)S(1)}, u32[]{:S(2)}, u32[]{:S(2)}) collective-permute-start(f32[136,256]{1,0:T(8,128)S(1)} %add.28), channel_id=1, source_target_pairs={{0,8},{8,0},{16,24},{24,16},{1,9},{9,1},{17,25},{25,17},{2,10},{10... | collective-permute-start | bytes 417800 | tf_op jit(solution)/shard_map/ppermute | solution.py:599
  79.2 4.0 %collective-permute-done.24 = f32[136,256]{1,0:T(8,128)S(1)} collective-permute-done((f32[136,256]{1,0:T(8,128)S(1)}, f32[136,256]{1,0:T(8,128)S(1)}, u32[]{:S(2)}, u32[]{:S(2)}) %collective-permute-start.24) | collective-permute-done | bytes 139296 | tf_op jit(solution)/shard_map/ppermute | solution.py:599
  83.3 1.6 %collective-permute-start.25 = (f32[136,256]{1,0:T(8,128)S(1)}, f32[136,256]{1,0:T(8,128)S(1)}, u32[]{:S(2)}, u32[]{:S(2)}) collective-permute-start(f32[136,256]{1,0:T(8,128)S(1)} %add.29), channel_id=1, source_target_pairs={{0,16},{8,24},{16,0},{24,8},{1,17},{9,25},{17,1},{25,9},{2,18},{10... | collective-permute-start | bytes 417800 | tf_op jit(solution)/shard_map/ppermute | solution.py:557
  84.9 3.1 %collective-permute-start.27 = (bf16[512,256]{1,0:T(8,128)(2,1)S(1)}, bf16[512,256]{1,0:T(8,128)(2,1)S(1)}, u32[]{:S(2)}, u32[]{:S(2)}) collective-permute-start(bf16[512,256]{1,0:T(8,128)(2,1)S(1)} %add_convert_fusion), channel_id=1, source_target_pairs={{0,4},{1,5},{4,0},{5,1},{2,6},{3,7},{6,2},{7,3},{8,12},{9,13},{12,... | collective-permute-start | bytes 786440 | tf_op jit(solution)/shard_map/ppermute | solution.py:614
  88.4 2.5 %collective-permute-start.26 = (bf16[512,256]{1,0:T(8,128)(2,1)S(1)}, bf16[512,256]{1,0:T(8,128)(2,1)S(1)}, u32[]{:S(2)}, u32[]{:S(2)}) collective-permute-start(bf16[512,256]{1,0:T(8,128)(2,1)S(1)} %get-tuple-element.99), channel_id=1, source_target_pairs={{0,2},{1,3},{2,0},{3,1},{4,6},{5,7},{6,4},{7,5},{8,10},{9,11},{10,... | collective-permute-start | bytes 786440 | tf_op jit(solution)/shard_map/ppermute | solution.py:616
  90.9 1.4 %collective-permute-done.28.theirs_ref = f32[136,256]{1,0:T(8,128)S(1)} collective-permute-done((f32[136,256]{1,0:T(8,128)S(1)}, f32[136,256]{1,0:T(8,128)S(1)}, u32[]{:S(2)}, u32[]{:S(2)}) %collective-permute-start.28) | collective-permute-done | bytes 139296 | tf_op jit(solution)/shard_map/ppermute | solution.py:692
  92.3 1.3 %assemble.1 = (f32[256,256]{1,0:T(8,128)}, f32[1,256]{1,0:T(1,128)}) custom-call(s32[2]{0:T(128)S(1)} %pad_add_fusion.pos_ref, f32[136,256]{1,0:T(8,128)S(1)} %add.30.mine_ref, f32[136,256]{1,0:T(8,128)S(1)} %collective-permute-done.28.theirs_ref), custom_call_target="tpu_custom_call" | custom-call | bytes 1048576 | tf_op jit(solution)/shard_map/assemble/pallas_call | solution.py:362
  93.5 6.0 %collective-permute-done.27.refs_3_ = bf16[512,256]{1,0:T(8,128)(2,1)S(1)} collective-permute-done((bf16[512,256]{1,0:T(8,128)(2,1)S(1)}, bf16[512,256]{1,0:T(8,128)(2,1)S(1)}, u32[]{:S(2)}, u32[]{:S(2)}) %collective-permute-start.27) | collective-permute-done | bytes 262176 | tf_op jit(solution)/shard_map/ppermute | solution.py:614
  (57 shorter events, 11.9 us)
Async XLA Ops:
  2.4 16.5 %collective-permute-start = (bf16[528,256]{1,0:T(8,128)(2,1)S(1)}, bf16[528,256]{1,0:T(8,128)(2,1)S(1)}, u32[]{:S(2)}, u32[]{:S(2)}) collective-permute-start(bf16[528,256]{1,0:T(8,128)(2,1)S(1)} %pad_maximum_fusion.rest_0_), channel_id=1, source_target_pairs={{0,4},{1,5},{4,0},{5,1},{2,6},{3,7},{6,2},{7,3},{8,12},{9,13},{12,... | collective-permute-start | bytes 811016 | tf_op jit(solution)/shard_map/ppermute | solution.py:568
  6.5 12.6 %collective-permute-start.2 = (bf16[528,256]{1,0:T(8,128)(2,1)S(1)}, bf16[528,256]{1,0:T(8,128)(2,1)S(1)}, u32[]{:S(2)}, u32[]{:S(2)}) collective-permute-start(bf16[528,256]{1,0:T(8,128)(2,1)S(1)} %pad_maximum_fusion.rest_0_), channel_id=1, source_target_pairs={{0,2},{1,3},{2,0},{3,1},{4,6},{5,7},{6,4},{7,5},{8,10},{9,11},{10,... | collective-permute-start | bytes 811016 | tf_op jit(solution)/shard_map/ppermute | solution.py:569
  8.1 13.3 %collective-permute-start.1 = (bf16[528,256]{1,0:T(8,128)(2,1)S(1)}, bf16[528,256]{1,0:T(8,128)(2,1)S(1)}, u32[]{:S(2)}, u32[]{:S(2)}) collective-permute-start(bf16[528,256]{1,0:T(8,128)(2,1)S(1)} %pad_maximum_fusion.rest_0_), channel_id=1, source_target_pairs={{0,1},{1,0},{2,3},{3,2},{4,5},{5,4},{6,7},{7,6},{8,9},{9,8},{10,11... | collective-permute-start | bytes 811016 | tf_op jit(solution)/shard_map/ppermute | solution.py:570
  18.9 2.5 %collective-permute-start.4 = (bf16[528,256]{1,0:T(8,128)(2,1)S(1)}, bf16[528,256]{1,0:T(8,128)(2,1)S(1)}, u32[]{:S(2)}, u32[]{:S(2)}) collective-permute-start(bf16[528,256]{1,0:T(8,128)(2,1)S(1)} %collective-permute-done.rest_4_), channel_id=1, source_target_pairs={{0,1},{1,0},{2,3},{3,2},{4,5},{5,4},{6,7},{7,6},{8,9},{9,8},{10,11... | collective-permute-start | bytes 811016 | tf_op jit(solution)/shard_map/ppermute | solution.py:576
  19.0 2.3 %collective-permute-start.3 = (bf16[528,256]{1,0:T(8,128)(2,1)S(1)}, bf16[528,256]{1,0:T(8,128)(2,1)S(1)}, u32[]{:S(2)}, u32[]{:S(2)}) collective-permute-start(bf16[528,256]{1,0:T(8,128)(2,1)S(1)} %collective-permute-done.2.rest_2_), channel_id=1, source_target_pairs={{0,1},{1,0},{2,3},{3,2},{4,5},{5,4},{6,7},{7,6},{8,9},{9,8},{10,11... | collective-permute-start | bytes 811016 | tf_op jit(solution)/shard_map/ppermute | solution.py:575
  19.4 4.9 %collective-permute-start.5 = (bf16[528,256]{1,0:T(8,128)(2,1)S(1)}, bf16[528,256]{1,0:T(8,128)(2,1)S(1)}, u32[]{:S(2)}, u32[]{:S(2)}) collective-permute-start(bf16[528,256]{1,0:T(8,128)(2,1)S(1)} %pad_maximum_fusion.rest_0_), channel_id=1, source_target_pairs={{2,4},{3,5},{4,2},{5,3},{10,12},{11,13},{12,10},{13,11},{18,20},{1... | collective-permute-start | bytes 811016 | tf_op jit(solution)/shard_map/ppermute | solution.py:574
  20.0 11.0 %collective-permute-start.6 = (bf16[528,256]{1,0:T(8,128)(2,1)S(1)}, bf16[528,256]{1,0:T(8,128)(2,1)S(1)}, u32[]{:S(2)}, u32[]{:S(2)}) collective-permute-start(bf16[528,256]{1,0:T(8,128)(2,1)S(1)} %collective-permute-done.rest_4_), channel_id=1, source_target_pairs={{4,6},{5,7},{2,0},{3,1},{12,14},{13,15},{10,8},{11,9},{20,22},{21,... | collective-permute-start | bytes 811016 | tf_op jit(solution)/shard_map/ppermute | solution.py:573
  31.0 18.8 %copy-start = (bf16[512,256]{1,0:T(8,128)(2,1)S(1)}, bf16[512,256]{1,0:T(8,128)(2,1)}, u32[]{:S(2)}) copy-start(bf16[512,256]{1,0:T(8,128)(2,1)} %cot_ref.1) | copy-start | bytes 786436
  31.0 18.8 %copy-start.1 = (bf16[256,256]{1,0:T(8,128)(2,1)S(1)}, bf16[256,256]{1,0:T(8,128)(2,1)}, u32[]{:S(2)}) copy-start(bf16[256,256]{1,0:T(8,128)(2,1)} %weight_ref.1) | copy-start | bytes 393220
  31.0 18.8 %copy-start.3 = (f32[256]{0:T(256)S(1)}, f32[256]{0:T(256)}, u32[]{:S(2)}) copy-start(f32[256]{0:T(256)} %param.11) | copy-start | bytes 3076
  31.0 1.5 %collective-permute-start.7 = (bf16[528,256]{1,0:T(8,128)(2,1)S(1)}, bf16[528,256]{1,0:T(8,128)(2,1)S(1)}, u32[]{:S(2)}, u32[]{:S(2)}) collective-permute-start(bf16[528,256]{1,0:T(8,128)(2,1)S(1)} %collective-permute-done.5.rest_0_), channel_id=1, source_target_pairs={{0,1},{1,0},{2,3},{3,2},{4,5},{5,4},{6,7},{7,6},{8,9},{9,8},{10,11... | collective-permute-start | bytes 811016 | tf_op jit(solution)/shard_map/ppermute | solution.py:579
  31.1 1.9 %collective-permute-start.8 = (bf16[528,256]{1,0:T(8,128)(2,1)S(1)}, bf16[528,256]{1,0:T(8,128)(2,1)S(1)}, u32[]{:S(2)}, u32[]{:S(2)}) collective-permute-start(bf16[528,256]{1,0:T(8,128)(2,1)S(1)} %collective-permute-done.6.rest_1_), channel_id=1, source_target_pairs={{0,1},{1,0},{2,3},{3,2},{4,5},{5,4},{6,7},{7,6},{8,9},{9,8},{10,11... | collective-permute-start | bytes 811016 | tf_op jit(solution)/shard_map/ppermute | solution.py:579
  34.6 14.0 %collective-permute-start.10 = (bf16[512,256]{1,0:T(8,128)(2,1)S(1)}, bf16[512,256]{1,0:T(8,128)(2,1)S(1)}, u32[]{:S(2)}, u32[]{:S(2)}) collective-permute-start(bf16[512,256]{1,0:T(8,128)(2,1)S(1)} %get-tuple-element.64), channel_id=1, source_target_pairs={{0,16},{8,24},{16,0},{24,8},{1,17},{9,25},{17,1},{25,9},{2,18},{10... | collective-permute-start | bytes 786440 | tf_op jit(solution)/shard_map/ppermute | solution.py:586
  36.2 12.4 %collective-permute-start.11 = (bf16[512,256]{1,0:T(8,128)(2,1)S(1)}, bf16[512,256]{1,0:T(8,128)(2,1)S(1)}, u32[]{:S(2)}, u32[]{:S(2)}) collective-permute-start(bf16[512,256]{1,0:T(8,128)(2,1)S(1)} %get-tuple-element.65), channel_id=1, source_target_pairs={{0,24},{8,16},{16,8},{24,0},{1,25},{9,17},{17,9},{25,1},{2,26},{10... | collective-permute-start | bytes 786440 | tf_op jit(solution)/shard_map/ppermute | solution.py:586
  37.6 12.2 %collective-permute-start.9 = (bf16[512,256]{1,0:T(8,128)(2,1)S(1)}, bf16[512,256]{1,0:T(8,128)(2,1)S(1)}, u32[]{:S(2)}, u32[]{:S(2)}) collective-permute-start(bf16[512,256]{1,0:T(8,128)(2,1)S(1)} %get-tuple-element.63), channel_id=1, source_target_pairs={{0,8},{8,0},{16,24},{24,16},{1,9},{9,1},{17,25},{25,17},{2,10},{10... | collective-permute-start | bytes 786440 | tf_op jit(solution)/shard_map/ppermute | solution.py:586
  52.0 1.4 %collective-permute-start.15 = (f32[136,256]{1,0:T(8,128)S(1)}, f32[136,256]{1,0:T(8,128)S(1)}, u32[]{:S(2)}, u32[]{:S(2)}) collective-permute-start(f32[136,256]{1,0:T(8,128)S(1)} %get-tuple-element.72), channel_id=1, source_target_pairs={{0,1},{1,0},{2,3},{3,2},{4,5},{5,4},{6,7},{7,6},{8,9},{9,8},{10,11... | collective-permute-start | bytes 417800 | tf_op jit(solution)/shard_map/ppermute | solution.py:671
  53.5 5.8 %collective-permute-start.16 = (f32[136,256]{1,0:T(8,128)S(1)}, f32[136,256]{1,0:T(8,128)S(1)}, u32[]{:S(2)}, u32[]{:S(2)}) collective-permute-start(f32[136,256]{1,0:T(8,128)S(1)} %add.26), channel_id=1, source_target_pairs={{0,2},{1,3},{2,0},{3,1},{4,6},{5,7},{6,4},{7,5},{8,10},{9,11},{10,... | collective-permute-start | bytes 417800 | tf_op jit(solution)/shard_map/ppermute | solution.py:557
  53.9 14.3 %collective-permute-start.12 = (bf16[512,256]{1,0:T(8,128)(2,1)S(1)}, bf16[512,256]{1,0:T(8,128)(2,1)S(1)}, u32[]{:S(2)}, u32[]{:S(2)}) collective-permute-start(bf16[512,256]{1,0:T(8,128)(2,1)S(1)} %get-tuple-element.68.back_ref), channel_id=1, source_target_pairs={{0,8},{8,0},{16,24},{24,16},{1,9},{9,1},{17,25},{25,17},{2,10},{10... | collective-permute-start | bytes 786440 | tf_op jit(solution)/shard_map/ppermute | solution.py:586
  55.4 13.4 %collective-permute-start.13 = (bf16[512,256]{1,0:T(8,128)(2,1)S(1)}, bf16[512,256]{1,0:T(8,128)(2,1)S(1)}, u32[]{:S(2)}, u32[]{:S(2)}) collective-permute-start(bf16[512,256]{1,0:T(8,128)(2,1)S(1)} %get-tuple-element.68.back_ref), channel_id=1, source_target_pairs={{0,16},{8,24},{16,0},{24,8},{1,17},{9,25},{17,1},{25,9},{2,18},{10... | collective-permute-start | bytes 786440 | tf_op jit(solution)/shard_map/ppermute | solution.py:586
  56.9 11.9 %collective-permute-start.14 = (bf16[512,256]{1,0:T(8,128)(2,1)S(1)}, bf16[512,256]{1,0:T(8,128)(2,1)S(1)}, u32[]{:S(2)}, u32[]{:S(2)}) collective-permute-start(bf16[512,256]{1,0:T(8,128)(2,1)S(1)} %get-tuple-element.68.back_ref), channel_id=1, source_target_pairs={{0,24},{8,16},{16,8},{24,0},{1,25},{9,17},{17,9},{25,1},{2,26},{10... | collective-permute-start | bytes 786440 | tf_op jit(solution)/shard_map/ppermute | solution.py:586
  59.3 8.8 %collective-permute-start.17 = (f32[136,256]{1,0:T(8,128)S(1)}, f32[136,256]{1,0:T(8,128)S(1)}, u32[]{:S(2)}, u32[]{:S(2)}) collective-permute-start(f32[136,256]{1,0:T(8,128)S(1)} %add.27), channel_id=1, source_target_pairs={{0,4},{1,5},{2,6},{3,7},{4,0},{5,1},{6,2},{7,3},{8,12},{9,13},{10,... | collective-permute-start | bytes 417800 | tf_op jit(solution)/shard_map/ppermute | solution.py:557
  69.8 2.5 %collective-permute-start.18 = (bf16[512,256]{1,0:T(8,128)(2,1)S(1)}, bf16[512,256]{1,0:T(8,128)(2,1)S(1)}, u32[]{:S(2)}, u32[]{:S(2)}) collective-permute-start(bf16[512,256]{1,0:T(8,128)(2,1)S(1)} %get-tuple-element.77), channel_id=1, source_target_pairs={{0,1},{1,0},{2,3},{3,2},{4,5},{5,4},{6,7},{7,6},{8,9},{9,8},{10,11... | collective-permute-start | bytes 786440 | tf_op jit(solution)/shard_map/ppermute | solution.py:598
  72.4 5.4 %collective-permute-start.19 = (bf16[512,256]{1,0:T(8,128)(2,1)S(1)}, bf16[512,256]{1,0:T(8,128)(2,1)S(1)}, u32[]{:S(2)}, u32[]{:S(2)}) collective-permute-start(bf16[512,256]{1,0:T(8,128)(2,1)S(1)} %get-tuple-element.86), channel_id=1, source_target_pairs={{0,1},{1,0},{2,3},{3,2},{4,5},{5,4},{6,7},{7,6},{8,9},{9,8},{10,11... | collective-permute-start | bytes 786440 | tf_op jit(solution)/shard_map/ppermute | solution.py:605
  72.9 6.1 %collective-permute-start.20 = (bf16[512,256]{1,0:T(8,128)(2,1)S(1)}, bf16[512,256]{1,0:T(8,128)(2,1)S(1)}, u32[]{:S(2)}, u32[]{:S(2)}) collective-permute-start(bf16[512,256]{1,0:T(8,128)(2,1)S(1)} %get-tuple-element.87), channel_id=1, source_target_pairs={{0,1},{1,0},{2,3},{3,2},{4,5},{5,4},{6,7},{7,6},{8,9},{9,8},{10,11... | collective-permute-start | bytes 786440 | tf_op jit(solution)/shard_map/ppermute | solution.py:605
  73.0 6.1 %collective-permute-start.21 = (bf16[512,256]{1,0:T(8,128)(2,1)S(1)}, bf16[512,256]{1,0:T(8,128)(2,1)S(1)}, u32[]{:S(2)}, u32[]{:S(2)}) collective-permute-start(bf16[512,256]{1,0:T(8,128)(2,1)S(1)} %get-tuple-element.88), channel_id=1, source_target_pairs={{0,1},{1,0},{2,3},{3,2},{4,5},{5,4},{6,7},{7,6},{8,9},{9,8},{10,11... | collective-permute-start | bytes 786440 | tf_op jit(solution)/shard_map/ppermute | solution.py:605
  73.5 11.3 %collective-permute-start.22 = (bf16[512,256]{1,0:T(8,128)(2,1)S(1)}, bf16[512,256]{1,0:T(8,128)(2,1)S(1)}, u32[]{:S(2)}, u32[]{:S(2)}) collective-permute-start(bf16[512,256]{1,0:T(8,128)(2,1)S(1)} %pair_sums.3), channel_id=1, source_target_pairs={{6,4},{7,5},{0,2},{1,3},{14,12},{15,13},{8,10},{9,11},{22,20},{23,... | collective-permute-start | bytes 786440 | tf_op jit(solution)/shard_map/ppermute | solution.py:603
  77.1 7.7 %collective-permute-start.23 = (bf16[512,256]{1,0:T(8,128)(2,1)S(1)}, bf16[512,256]{1,0:T(8,128)(2,1)S(1)}, u32[]{:S(2)}, u32[]{:S(2)}) collective-permute-start(bf16[512,256]{1,0:T(8,128)(2,1)S(1)} %pair_sums.3), channel_id=1, source_target_pairs={{2,4},{3,5},{4,2},{5,3},{10,12},{11,13},{12,10},{13,11},{18,20},{1... | collective-permute-start | bytes 786440 | tf_op jit(solution)/shard_map/ppermute | solution.py:604
  77.8 5.4 %collective-permute-start.24 = (f32[136,256]{1,0:T(8,128)S(1)}, f32[136,256]{1,0:T(8,128)S(1)}, u32[]{:S(2)}, u32[]{:S(2)}) collective-permute-start(f32[136,256]{1,0:T(8,128)S(1)} %add.28), channel_id=1, source_target_pairs={{0,8},{8,0},{16,24},{24,16},{1,9},{9,1},{17,25},{25,17},{2,10},{10... | collective-permute-start | bytes 417800 | tf_op jit(solution)/shard_map/ppermute | solution.py:599
  83.3 5.1 %collective-permute-start.25 = (f32[136,256]{1,0:T(8,128)S(1)}, f32[136,256]{1,0:T(8,128)S(1)}, u32[]{:S(2)}, u32[]{:S(2)}) collective-permute-start(f32[136,256]{1,0:T(8,128)S(1)} %add.29), channel_id=1, source_target_pairs={{0,16},{8,24},{16,0},{24,8},{1,17},{9,25},{17,1},{25,9},{2,18},{10... | collective-permute-start | bytes 417800 | tf_op jit(solution)/shard_map/ppermute | solution.py:557
  84.9 14.6 %collective-permute-start.27 = (bf16[512,256]{1,0:T(8,128)(2,1)S(1)}, bf16[512,256]{1,0:T(8,128)(2,1)S(1)}, u32[]{:S(2)}, u32[]{:S(2)}) collective-permute-start(bf16[512,256]{1,0:T(8,128)(2,1)S(1)} %add_convert_fusion), channel_id=1, source_target_pairs={{0,4},{1,5},{4,0},{5,1},{2,6},{3,7},{6,2},{7,3},{8,12},{9,13},{12,... | collective-permute-start | bytes 786440 | tf_op jit(solution)/shard_map/ppermute | solution.py:614
  88.4 11.4 %collective-permute-start.26 = (bf16[512,256]{1,0:T(8,128)(2,1)S(1)}, bf16[512,256]{1,0:T(8,128)(2,1)S(1)}, u32[]{:S(2)}, u32[]{:S(2)}) collective-permute-start(bf16[512,256]{1,0:T(8,128)(2,1)S(1)} %get-tuple-element.99), channel_id=1, source_target_pairs={{0,2},{1,3},{2,0},{3,1},{4,6},{5,7},{6,4},{7,5},{8,10},{9,11},{10,... | collective-permute-start | bytes 786440 | tf_op jit(solution)/shard_map/ppermute | solution.py:616
  90.9 1.4 %collective-permute-start.28 = (f32[136,256]{1,0:T(8,128)S(1)}, f32[136,256]{1,0:T(8,128)S(1)}, u32[]{:S(2)}, u32[]{:S(2)}) collective-permute-start(f32[136,256]{1,0:T(8,128)S(1)} %add.30.mine_ref), channel_id=1, source_target_pairs={{0,1},{1,0},{2,3},{3,2},{4,5},{5,4},{6,7},{7,6},{8,9},{9,8},{10,11... | collective-permute-start | bytes 417800 | tf_op jit(solution)/shard_map/ppermute | solution.py:692
  (2 other events, 1.4 us)

commit v4 on v3

--- a/solution.py
+++ b/solution.py
@@ -42,8 +42,8 @@
     for copy in copies:
         copy.start()
     for t, copy in enumerate(copies):
-        place = ((t // per_peer) ^ pos_ref[0]) * per_peer + t % per_peer
-        rows = pl.ds(pl.multiple_of(place * TILE, TILE), TILE)
+        block = ((t // per_peer) ^ pos_ref[0]) * per_peer + t % per_peer
+        rows = pl.ds(pl.multiple_of(block * TILE, TILE), TILE)
         if not whole:
             out_ref[rows, :] = jnp.zeros((TILE, out_ref.shape[1]), out_ref.dtype)
         count = cnt_ref[t]
@@ -51,7 +51,8 @@
         for s in range(slots):
             source = src_ref[t, s]
             slot = (source // per_piece) ^ here
-            column = pl.multiple_of((slot * per_piece + source % per_piece) * TILE, TILE)
+            place = jnp.where((slot == 3) | (slot == 5), slot ^ 6, slot)
+            column = pl.multiple_of((place * per_piece + source % per_piece) * TILE, TILE)
             tile = held[t, s]
             out_ref[rows, pl.ds(column, TILE)] = jnp.where(s < count, tile, jnp.zeros_like(tile))
 
@@ -399,45 +400,51 @@
     )(dense, back)
 
 
-def backward_late_kernel(base, slots, peers, dense_ref, put_ref, first_ref, *rest):
+def backward_late_kernel(base, slots, peers, dense_ref, *rest):
+    puts, rest = rest[: len(slots)], rest[len(slots) :]
+    first_ref, rest = rest[0], rest[1:]
     backs, outs, (joined, rows) = rest[: peers - 1], rest[peers - 1 : -2], rest[-2:]
-    capacity = put_ref.shape[2]
+    capacity = puts[0].shape[2]
     block = backs[0].shape[0]
     for peer in range(1, peers):
         joined[(peer - 1) * block : peer * block, :] = backs[peer - 1][...]
-    columns = slice(base * capacity, (base + slots) * capacity)
+    columns = slice(base * capacity, (base + len(outs)) * capacity)
     rows[...] = (
         first_ref[columns, :] + back_product(dense_ref[block:, columns], joined[...])
     ).astype(BF16)
-    for slot in range(slots):
-        outs[slot][...] = jnp.dot(
-            put_ref[slot],
-            rows[slot * capacity : (slot + 1) * capacity, :],
-            preferred_element_type=F32,
-        ).astype(outs[slot].dtype)
-
-
-def backward_late(dense, put, first, backs, base):
-    slots, nodes, capacity = put.shape
+    at = 0
+    for put_ref, picked in zip(puts, slots):
+        for slot in picked:
+            outs[at][...] = jnp.dot(
+                put_ref[slot],
+                rows[at * capacity : (at + 1) * capacity, :],
+                preferred_element_type=F32,
+            ).astype(outs[at].dtype)
+            at += 1
+
+
+def backward_late(dense, puts, slots, first, backs, base):
+    _, nodes, capacity = puts[0].shape
+    count = sum(len(picked) for picked in slots)
     size = first.shape[1]
     return pl.pallas_call(
         functools.partial(backward_late_kernel, base, slots, len(backs) + 1),
         out_shape=tuple(
-            jax.ShapeDtypeStruct((nodes, size), BF16 if slot % 2 else F32)
-            for slot in range(slots)
+            jax.ShapeDtypeStruct((nodes, size), BF16 if (base + at) % 2 else F32)
+            for at in range(count)
         ),
         scratch_shapes=[
             pltpu.VMEM((len(backs) * backs[0].shape[0], size), BF16),
-            pltpu.VMEM((slots * capacity, size), BF16),
+            pltpu.VMEM((count * capacity, size), BF16),
         ],
         compiler_params=params(),
         cost_estimate=pl.CostEstimate(
-            flops=2 * slots * capacity * size * dense.shape[0],
-            bytes_accessed=2 * dense.shape[0] * slots * capacity,
+            flops=2 * count * capacity * size * dense.shape[0],
+            bytes_accessed=2 * dense.shape[0] * count * capacity,
             transcendentals=0,
         ),
         name="backward_late",
-    )(dense, put, first, *backs)
+    )(dense, *puts, first, *backs)
 
 
 def backward_blocks_kernel(peers, slots, pos_ref, put_ref, dense_ref, *rest):
@@ -572,12 +579,15 @@
     far, dense = lax.optimization_barrier((far, dense))
     ends = lax.ppermute(far, "col", LINE_OUT)
     middle = lax.ppermute(after(piece, far), "col", LINE_MIDDLE)
-    early = [[piece], [other], [near], [lax.ppermute(near, "col", CORE)], [far]]
-    early.append([lax.ppermute(far, "col", CORE)])
+    early = [[piece], [other], [near], [lax.ppermute(far, "col", CORE)], [far]]
     partial, put_early = forward_part(dense, early, 0, pos, rows, nodes, capacity)
     partial, middle, ends = lax.optimization_barrier((partial, middle, ends))
-    late = [[middle, ends], [lax.ppermute(middle, "col", CORE), lax.ppermute(ends, "col", CORE)]]
-    *blocks, put_late = forward_part(dense, late, 6, pos, rows, nodes, capacity, partial)
+    late = [
+        [lax.ppermute(near, "col", CORE)],
+        [middle, ends],
+        [lax.ppermute(middle, "col", CORE), lax.ppermute(ends, "col", CORE)],
+    ]
+    *blocks, put_late = forward_part(dense, late, 5, pos, rows, nodes, capacity, partial)
     return dense, put_early, put_late, blocks
 
 
@@ -591,13 +601,15 @@
 
 def line_reduce(dense, put_early, put_late, back, backs, pos, sums, rows, columns):
     first = backward_early(dense, back)
-    sums = exchange_add(sums, "col", columns, 2)
+    sums = sums + after(lax.ppermute(sums, "col", xor_pairs(columns, 2)), backs[2])
     sums = exchange_add(sums, "col", columns, 4)
     *backs, first, sums = lax.optimization_barrier((*backs, first, sums))
-    keep3, give3 = backward_late(dense, put_late, first, backs, 6)
+    keep3, give3 = backward_late(dense, (put_late,), ((1, 2),), first, backs, 6)
     got3 = lax.ppermute(give3, "col", CORE)
     received = lax.ppermute(sums, "row", xor_pairs(rows, 1))
-    keep0, give0, keep1, give1, keep2, give2 = backward_late(dense, put_early, first, backs, 0)
+    keep0, give0, keep1, give2, keep2, give1 = backward_late(
+        dense, (put_early, put_late), (tuple(range(5)), (0,)), first, backs, 0
+    )
     got3, give2, give1, give0, keep0 = lax.optimization_barrier((got3, give2, give1, give0, keep0))
     (last,) = pair_sums([keep3], [got3])
     passed = lax.ppermute(last, "col", LINE_IN)

time: 101 us -> 99.8 us (0.988)
  starting transfers between devices: 31.5 us -> 27.9 us
  waiting for transfers between devices: 46 us -> 48 us
    ppermute x6, waiting for transfers between devices: 12.4 us -> 17.3 us  [row_exchange(): lax.ppermute(arrays[step - 1], 'row', xor_pairs(rows, step))]
    ppermute x1, starting transfers between devices: 3.59 us -> 1.47 us  [line_reduce(): passed = lax.ppermute(last, 'col', LINE_IN)]
    ppermute x1, starting transfers between devices: 2.5 us -> 1.11 us  [line_reduce(): from_near = lax.ppermute(after(near, far), 'col', LINE_SWAP1)]
    ppermute x1, waiting for transfers between devices: 1.35 us -> 0.01 us  [per_device(): lax.ppermute(theirs, 'col', CORE if line else xor_pairs(columns, 1))]
    ppermute x1, starting transfers between devices: 3.14 us -> 1.97 us  [line_reduce(): from_far = lax.ppermute(far, 'col', LINE_SWAP2)]
    ppermute x3 -> x2, waiting for transfers between devices: 8.61 us -> 7.83 us  [exchange_add(): return value + lax.ppermute(value, axis, xor_pairs(size, step))]
    ppermute x3 -> x2, starting transfers between devices: 3.61 us -> 3.16 us  [exchange_add(): return value + lax.ppermute(value, axis, xor_pairs(size, step))]
  transfers between devices with their start and end apart: 29 -> 29, of which waited for: 16 -> 13; matrix products, arithmetic and copies ran while one was open for 0% -> 0% of each run, Pallas kernels for 13% -> 13%
where the time goes in v4:
time: 99.8 us; the launch traced here: 99.5 us
  waiting for transfers between devices  48 us (48%)
  starting transfers between devices  27.9 us (28%)
  Pallas kernels  19.3 us (19%)
  other arithmetic  1.97 us (2%)
  local copies, waits for them, and re-layouts  1.36 us (1%)
    ppermute x6, waiting for transfers between devices, row_exchange(): lax.ppermute(arrays[step - 1], 'row', xor_pairs(rows, step))  17.3 us
    ppermute x6, starting transfers between devices, row_exchange(): lax.ppermute(arrays[step - 1], 'row', xor_pairs(rows, step))  8.01 us
    ppermute x2, waiting for transfers between devices, exchange_add(): return value + lax.ppermute(value, axis, xor_pairs(size, step))  7.83 us
    ppermute x1, waiting for transfers between devices, line_reduce(): from_far = lax.ppermute(far, 'col', LINE_SWAP2)  6.54 us
    ppermute x1, waiting for transfers between devices, line_exchange(): ends = lax.ppermute(far, 'col', LINE_OUT)  6.25 us
    pallas_call x1, Pallas kernels, densify(): pl.pallas_call(functools.partial(densify_kernel, capacity // TILE, target...  6.07 us
    pallas_call x2, Pallas kernels, forward_part(): pl.pallas_call(functools.partial(forward_part_kernel, tuple((len(group) f...  4.48 us
    ppermute x1, starting transfers between devices, line_exchange(): far = lax.ppermute(piece, 'col', LINE_SWAP2)  4.1 us
  transfers between devices with their start and end apart: 29, of which 13 were waited for; matrix products, arithmetic and copies ran while one was open for 0% of the time, Pallas kernels for 13%

profile of v4, /device:TPU:0, one launch (start us, length us, event | category | flops | bytes accessed | tf_op | source)
XLA Modules:
  0.0 99.5 jit_solution(1143448059917050293)
XLA Ops:
  2.4 4.1 %collective-permute-start = (bf16[528,256]{1,0:T(8,128)(2,1)S(1)}, bf16[528,256]{1,0:T(8,128)(2,1)S(1)}, u32[]{:S(2)}, u32[]{:S(2)}) collective-permute-start(bf16[528,256]{1,0:T(8,128)(2,1)S(1)} %pad_maximum_fusion.rest_0_), channel_id=1, source_target_pairs={{0,4},{1,5},{4,0},{5,1},{2,6},{3,7},{6,2},{7,3},{8,12},{9,13},{12,... | collective-permute-start | bytes 811016 | tf_op jit(solution)/shard_map/ppermute | solution.py:575
  6.5 1.6 %collective-permute-start.1 = (bf16[528,256]{1,0:T(8,128)(2,1)S(1)}, bf16[528,256]{1,0:T(8,128)(2,1)S(1)}, u32[]{:S(2)}, u32[]{:S(2)}) collective-permute-start(bf16[528,256]{1,0:T(8,128)(2,1)S(1)} %pad_maximum_fusion.rest_0_), channel_id=1, source_target_pairs={{0,2},{1,3},{2,0},{3,1},{4,6},{5,7},{6,4},{7,5},{8,10},{9,11},{10,... | collective-permute-start | bytes 811016 | tf_op jit(solution)/shard_map/ppermute | solution.py:576
  9.5 6.1 %densify.1.dense_ref = bf16[2048,2048]{1,0:T(8,128)(2,1)S(1)} custom-call(s32[16,16]{1,0:T(8,128)S(1)} %bitcast.34, s32[16]{0:T(128)S(1)} %bitcast.36, s32[2]{0:T(128)S(1)} %pad_add_fusion.pos_ref, bf16[16,16,128,128]{3,2,1,0:T(8,128)(2,1)} %bitcast.37), custom_call_target="tpu_custom_call" | custom-call | bytes 16777216 | tf_op jit(solution)/shard_map/densify/pallas_call | solution.py:64
  15.6 3.3 %collective-permute-done.rest_4_ = bf16[528,256]{1,0:T(8,128)(2,1)S(1)} collective-permute-done((bf16[528,256]{1,0:T(8,128)(2,1)S(1)}, bf16[528,256]{1,0:T(8,128)(2,1)S(1)}, u32[]{:S(2)}, u32[]{:S(2)}) %collective-permute-start) | collective-permute-done | bytes 270368 | tf_op jit(solution)/shard_map/ppermute | solution.py:575
  19.5 1.3 %collective-permute-start.6 = (bf16[528,256]{1,0:T(8,128)(2,1)S(1)}, bf16[528,256]{1,0:T(8,128)(2,1)S(1)}, u32[]{:S(2)}, u32[]{:S(2)}) collective-permute-start(bf16[528,256]{1,0:T(8,128)(2,1)S(1)} %collective-permute-done.rest_4_), channel_id=1, source_target_pairs={{4,6},{5,7},{2,0},{3,1},{12,14},{13,15},{10,8},{11,9},{20,22},{21,... | collective-permute-start | bytes 811016 | tf_op jit(solution)/shard_map/ppermute | solution.py:580
  21.4 2.6 %forward_early.1 = (f32[2048,256]{1,0:T(8,128)S(1)}, bf16[5,512,256]{2,1,0:T(8,128)(2,1)S(1)}) custom-call(s32[2]{0:T(128)S(1)} %pad_add_fusion.pos_ref, bf16[2048,2048]{1,0:T(8,128)(2,1)S(1)} %densify.1.dense_ref, bf16[528,256]{1,0:T(8,128)(2,1)S(1)} %pad_maximum_fusion.rest_0_, bf16[528,256]{1,0:T(8,128)(2,1)S(1)} %collective-permute-done.3.rest_1_, ...), custom_call_target="tpu_custom_call" | custom-call | flops 1342177280 | bytes 5242880 | tf_op jit(solution)/shard_map/forward_early/pallas_call | solution.py:212
  24.1 6.3 %collective-permute-done.6.rest_2_ = bf16[528,256]{1,0:T(8,128)(2,1)S(1)} collective-permute-done((bf16[528,256]{1,0:T(8,128)(2,1)S(1)}, bf16[528,256]{1,0:T(8,128)(2,1)S(1)}, u32[]{:S(2)}, u32[]{:S(2)}) %collective-permute-start.6) | collective-permute-done | bytes 270368 | tf_op jit(solution)/shard_map/ppermute | solution.py:580
  30.8 1.0 %collective-permute-done.7.rest_3_ = bf16[528,256]{1,0:T(8,128)(2,1)S(1)} collective-permute-done((bf16[528,256]{1,0:T(8,128)(2,1)S(1)}, bf16[528,256]{1,0:T(8,128)(2,1)S(1)}, u32[]{:S(2)}, u32[]{:S(2)}) %collective-permute-start.7) | collective-permute-done | bytes 270368 | tf_op jit(solution)/shard_map/ppermute | solution.py:588
  32.3 1.8 %forward_late.1 = (f32[512,256]{1,0:T(8,128)S(1)}, bf16[512,256]{1,0:T(8,128)(2,1)S(1)}, bf16[512,256]{1,0:T(8,128)(2,1)S(1)}, bf16[512,256]{1,0:T(8,128)(2,1)S(1)}, bf16[3,512,256]{2,1,0:T(8,128)(2,1)S(1)}) custom-call(s32[2]{0:T(128)S(1)} %pad_add_fusion.pos_ref, bf16[2048,2048]{1,0:T(8,128)(2,1)S(1)} %densify.1.dense_ref, ...), custom_call_target="tpu_custom_call" | custom-call | flops 805306368 | bytes 3145728 | tf_op jit(solution)/shard_map/forward_late/pallas_call | solution.py:212
  34.1 1.6 %collective-permute-start.10 = (bf16[512,256]{1,0:T(8,128)(2,1)S(1)}, bf16[512,256]{1,0:T(8,128)(2,1)S(1)}, u32[]{:S(2)}, u32[]{:S(2)}) collective-permute-start(bf16[512,256]{1,0:T(8,128)(2,1)S(1)} %get-tuple-element.65), channel_id=1, source_target_pairs={{0,16},{8,24},{16,0},{24,8},{1,17},{9,25},{17,1},{25,9},{2,18},{10... | collective-permute-start | bytes 786440 | tf_op jit(solution)/shard_map/ppermute | solution.py:596
  35.8 1.4 %collective-permute-start.11 = (bf16[512,256]{1,0:T(8,128)(2,1)S(1)}, bf16[512,256]{1,0:T(8,128)(2,1)S(1)}, u32[]{:S(2)}, u32[]{:S(2)}) collective-permute-start(bf16[512,256]{1,0:T(8,128)(2,1)S(1)} %get-tuple-element.66), channel_id=1, source_target_pairs={{0,24},{8,16},{16,8},{24,0},{1,25},{9,17},{17,9},{25,1},{2,26},{10... | collective-permute-start | bytes 786440 | tf_op jit(solution)/shard_map/ppermute | solution.py:596
  37.7 10.5 %collective-permute-done.10.rest_2_ = bf16[512,256]{1,0:T(8,128)(2,1)S(1)} collective-permute-done((bf16[512,256]{1,0:T(8,128)(2,1)S(1)}, bf16[512,256]{1,0:T(8,128)(2,1)S(1)}, u32[]{:S(2)}, u32[]{:S(2)}) %collective-permute-start.10) | collective-permute-done | bytes 262176 | tf_op jit(solution)/shard_map/ppermute | solution.py:596
  48.2 1.2 %collective-permute-done.9.rest_1_ = bf16[512,256]{1,0:T(8,128)(2,1)S(1)} collective-permute-done((bf16[512,256]{1,0:T(8,128)(2,1)S(1)}, bf16[512,256]{1,0:T(8,128)(2,1)S(1)}, u32[]{:S(2)}, u32[]{:S(2)}) %collective-permute-start.9) | collective-permute-done | bytes 262176 | tf_op jit(solution)/shard_map/ppermute | solution.py:596
  49.4 1.1 %layer.1 = (bf16[512,256]{1,0:T(8,128)(2,1)}, bf16[512,256]{1,0:T(8,128)(2,1)S(1)}, bf16[512,256]{1,0:T(8,128)(2,1)S(1)}, bf16[512,256]{1,0:T(8,128)(2,1)S(1)}) custom-call(bf16[256,256]{1,0:T(8,128)(2,1)S(1)} %copy-done.1, f32[1,256]{1,0:T(1,128)S(1)} %bitcast.35, bf16[512,256]{1,0:T(8,128)(2,1)S(1)} %copy-done, f32[512,256]{1,0:T(8,128)S(1)} %get-tuple-element.63.rest_0_, ...), custom_call_target="tpu_custom_call" | custom-call | flops 134217728 | bytes 2621440 | tf_op jit(solution)/shard_map/layer/pallas_call | solution.py:304
  50.5 1.0 %weight_partials.1 = (f32[136,256]{1,0:T(8,128)S(1)}, f32[136,256]{1,0:T(8,128)S(1)}) custom-call(s32[2]{0:T(128)S(1)} %pad_add_fusion.pos_ref, bf16[512,256]{1,0:T(8,128)(2,1)S(1)} %get-tuple-element.70.agg_ref, bf16[512,256]{1,0:T(8,128)(2,1)S(1)} %get-tuple-element.71.grad_ref), custom_call_target="tpu_custom_call" | custom-call | flops 67108864 | bytes 786432 | tf_op jit(solution)/shard_map/weight_partials/pallas_call | solution.py:338
  51.6 2.5 %collective-permute-start.14 = (bf16[512,256]{1,0:T(8,128)(2,1)S(1)}, bf16[512,256]{1,0:T(8,128)(2,1)S(1)}, u32[]{:S(2)}, u32[]{:S(2)}) collective-permute-start(bf16[512,256]{1,0:T(8,128)(2,1)S(1)} %get-tuple-element.69.back_ref), channel_id=1, source_target_pairs={{0,24},{8,16},{16,8},{24,0},{1,25},{9,17},{17,9},{25,1},{2,26},{10... | collective-permute-start | bytes 786440 | tf_op jit(solution)/shard_map/ppermute | solution.py:596
  54.9 1.3 %collective-permute-start.13 = (bf16[512,256]{1,0:T(8,128)(2,1)S(1)}, bf16[512,256]{1,0:T(8,128)(2,1)S(1)}, u32[]{:S(2)}, u32[]{:S(2)}) collective-permute-start(bf16[512,256]{1,0:T(8,128)(2,1)S(1)} %get-tuple-element.69.back_ref), channel_id=1, source_target_pairs={{0,16},{8,24},{16,0},{24,8},{1,17},{9,25},{17,1},{25,9},{2,18},{10... | collective-permute-start | bytes 786440 | tf_op jit(solution)/shard_map/ppermute | solution.py:596
  56.2 5.6 %collective-permute-done.14.rest_4_.rest_5_ = bf16[512,256]{1,0:T(8,128)(2,1)S(1)} collective-permute-done((bf16[512,256]{1,0:T(8,128)(2,1)S(1)}, bf16[512,256]{1,0:T(8,128)(2,1)S(1)}, u32[]{:S(2)}, u32[]{:S(2)}) %collective-permute-start.14) | collective-permute-done | bytes 262176 | tf_op jit(solution)/shard_map/ppermute | solution.py:596
  61.8 1.5 %collective-permute-start.17 = (f32[136,256]{1,0:T(8,128)S(1)}, f32[136,256]{1,0:T(8,128)S(1)}, u32[]{:S(2)}, u32[]{:S(2)}) collective-permute-start(f32[136,256]{1,0:T(8,128)S(1)} %add.27), channel_id=1, source_target_pairs={{0,4},{1,5},{2,6},{3,7},{4,0},{5,1},{6,2},{7,3},{8,12},{9,13},{10,... | collective-permute-start | bytes 417800 | tf_op jit(solution)/shard_map/ppermute | solution.py:564
  64.1 6.4 %collective-permute-done.17 = f32[136,256]{1,0:T(8,128)S(1)} collective-permute-done((f32[136,256]{1,0:T(8,128)S(1)}, f32[136,256]{1,0:T(8,128)S(1)}, u32[]{:S(2)}, u32[]{:S(2)}) %collective-permute-start.17) | collective-permute-done | bytes 139296 | tf_op jit(solution)/shard_map/ppermute | solution.py:564
  70.5 1.0 %backward_late.2 = (f32[512,256]{1,0:T(8,128)S(1)}, bf16[512,256]{1,0:T(8,128)(2,1)S(1)}) custom-call(bf16[2048,2048]{1,0:T(8,128)(2,1)S(1)} %densify.1.dense_ref, bf16[3,512,256]{2,1,0:T(8,128)(2,1)S(1)} %get-tuple-element.68.rest_0_.rest_1_, f32[2048,256]{1,0:T(8,128)S(1)} %backward_early.1.rest_1_.rest_2_, ...), custom_call_target="tpu_custom_call" | custom-call | flops 536870912 | bytes 2097152 | tf_op jit(solution)/shard_map/backward_late/pallas_call | solution.py:430
  71.7 2.5 %backward_late.3 = (f32[512,256]{1,0:T(8,128)S(1)}, bf16[512,256]{1,0:T(8,128)(2,1)S(1)}, f32[512,256]{1,0:T(8,128)S(1)}, bf16[512,256]{1,0:T(8,128)(2,1)S(1)}, ...) custom-call(bf16[2048,2048]{1,0:T(8,128)(2,1)S(1)} %densify.1.dense_ref, ...), custom_call_target="tpu_custom_call" | custom-call | flops 1610612736 | bytes 6291456 | tf_op jit(solution)/shard_map/backward_late/pallas_call | solution.py:430
  75.3 1.5 %collective-permute-start.22 = (bf16[512,256]{1,0:T(8,128)(2,1)S(1)}, bf16[512,256]{1,0:T(8,128)(2,1)S(1)}, u32[]{:S(2)}, u32[]{:S(2)}) collective-permute-start(bf16[512,256]{1,0:T(8,128)(2,1)S(1)} %pair_sums.3), channel_id=1, source_target_pairs={{6,4},{7,5},{0,2},{1,3},{14,12},{15,13},{8,10},{9,11},{22,20},{23,... | collective-permute-start | bytes 786440 | tf_op jit(solution)/shard_map/ppermute | solution.py:615
  77.4 1.6 %collective-permute-start.24 = (f32[136,256]{1,0:T(8,128)S(1)}, f32[136,256]{1,0:T(8,128)S(1)}, u32[]{:S(2)}, u32[]{:S(2)}) collective-permute-start(f32[136,256]{1,0:T(8,128)S(1)} %add.28), channel_id=1, source_target_pairs={{0,8},{8,0},{16,24},{24,16},{1,9},{9,1},{17,25},{25,17},{2,10},{10... | collective-permute-start | bytes 417800 | tf_op jit(solution)/shard_map/ppermute | solution.py:609
  79.1 3.9 %collective-permute-done.24 = f32[136,256]{1,0:T(8,128)S(1)} collective-permute-done((f32[136,256]{1,0:T(8,128)S(1)}, f32[136,256]{1,0:T(8,128)S(1)}, u32[]{:S(2)}, u32[]{:S(2)}) %collective-permute-start.24) | collective-permute-done | bytes 139296 | tf_op jit(solution)/shard_map/ppermute | solution.py:609
  83.0 1.6 %collective-permute-start.25 = (f32[136,256]{1,0:T(8,128)S(1)}, f32[136,256]{1,0:T(8,128)S(1)}, u32[]{:S(2)}, u32[]{:S(2)}) collective-permute-start(f32[136,256]{1,0:T(8,128)S(1)} %add.29), channel_id=1, source_target_pairs={{0,16},{8,24},{16,0},{24,8},{1,17},{9,25},{17,1},{25,9},{2,18},{10... | collective-permute-start | bytes 417800 | tf_op jit(solution)/shard_map/ppermute | solution.py:564
  84.7 2.0 %collective-permute-start.27 = (bf16[512,256]{1,0:T(8,128)(2,1)S(1)}, bf16[512,256]{1,0:T(8,128)(2,1)S(1)}, u32[]{:S(2)}, u32[]{:S(2)}) collective-permute-start(bf16[512,256]{1,0:T(8,128)(2,1)S(1)} %add_convert_fusion), channel_id=1, source_target_pairs={{0,4},{1,5},{4,0},{5,1},{2,6},{3,7},{6,2},{7,3},{8,12},{9,13},{12,... | collective-permute-start | bytes 786440 | tf_op jit(solution)/shard_map/ppermute | solution.py:626
  86.7 1.4 %collective-permute-done.25 = f32[136,256]{1,0:T(8,128)S(1)} collective-permute-done((f32[136,256]{1,0:T(8,128)S(1)}, f32[136,256]{1,0:T(8,128)S(1)}, u32[]{:S(2)}, u32[]{:S(2)}) %collective-permute-start.25) | collective-permute-done | bytes 139296 | tf_op jit(solution)/shard_map/ppermute | solution.py:564
  88.2 1.1 %collective-permute-start.26 = (bf16[512,256]{1,0:T(8,128)(2,1)S(1)}, bf16[512,256]{1,0:T(8,128)(2,1)S(1)}, u32[]{:S(2)}, u32[]{:S(2)}) collective-permute-start(bf16[512,256]{1,0:T(8,128)(2,1)S(1)} %get-tuple-element.101), channel_id=1, source_target_pairs={{0,2},{1,3},{2,0},{3,1},{4,6},{5,7},{6,4},{7,5},{8,10},{9,11},{10,... | collective-permute-start | bytes 786440 | tf_op jit(solution)/shard_map/ppermute | solution.py:628
  89.3 1.4 %collective-permute-done.28.theirs_ref = f32[136,256]{1,0:T(8,128)S(1)} collective-permute-done((f32[136,256]{1,0:T(8,128)S(1)}, f32[136,256]{1,0:T(8,128)S(1)}, u32[]{:S(2)}, u32[]{:S(2)}) %collective-permute-start.28) | collective-permute-done | bytes 139296 | tf_op jit(solution)/shard_map/ppermute | solution.py:704
  90.6 1.3 %assemble.1 = (f32[256,256]{1,0:T(8,128)}, f32[1,256]{1,0:T(1,128)}) custom-call(s32[2]{0:T(128)S(1)} %pad_add_fusion.pos_ref, f32[136,256]{1,0:T(8,128)S(1)} %add.30.mine_ref, f32[136,256]{1,0:T(8,128)S(1)} %collective-permute-done.28.theirs_ref), custom_call_target="tpu_custom_call" | custom-call | bytes 1048576 | tf_op jit(solution)/shard_map/assemble/pallas_call | solution.py:363
  91.9 6.5 %collective-permute-done.27.refs_3_ = bf16[512,256]{1,0:T(8,128)(2,1)S(1)} collective-permute-done((bf16[512,256]{1,0:T(8,128)(2,1)S(1)}, bf16[512,256]{1,0:T(8,128)(2,1)S(1)}, u32[]{:S(2)}, u32[]{:S(2)}) %collective-permute-start.27) | collective-permute-done | bytes 262176 | tf_op jit(solution)/shard_map/ppermute | solution.py:626
  (57 shorter events, 10.6 us)
Async XLA Ops:
  2.4 16.5 %collective-permute-start = (bf16[528,256]{1,0:T(8,128)(2,1)S(1)}, bf16[528,256]{1,0:T(8,128)(2,1)S(1)}, u32[]{:S(2)}, u32[]{:S(2)}) collective-permute-start(bf16[528,256]{1,0:T(8,128)(2,1)S(1)} %pad_maximum_fusion.rest_0_), channel_id=1, source_target_pairs={{0,4},{1,5},{4,0},{5,1},{2,6},{3,7},{6,2},{7,3},{8,12},{9,13},{12,... | collective-permute-start | bytes 811016 | tf_op jit(solution)/shard_map/ppermute | solution.py:575
  6.5 14.4 %collective-permute-start.1 = (bf16[528,256]{1,0:T(8,128)(2,1)S(1)}, bf16[528,256]{1,0:T(8,128)(2,1)S(1)}, u32[]{:S(2)}, u32[]{:S(2)}) collective-permute-start(bf16[528,256]{1,0:T(8,128)(2,1)S(1)} %pad_maximum_fusion.rest_0_), channel_id=1, source_target_pairs={{0,2},{1,3},{2,0},{3,1},{4,6},{5,7},{6,4},{7,5},{8,10},{9,11},{10,... | collective-permute-start | bytes 811016 | tf_op jit(solution)/shard_map/ppermute | solution.py:576
  8.1 13.4 %collective-permute-start.3 = (bf16[528,256]{1,0:T(8,128)(2,1)S(1)}, bf16[528,256]{1,0:T(8,128)(2,1)S(1)}, u32[]{:S(2)}, u32[]{:S(2)}) collective-permute-start(bf16[528,256]{1,0:T(8,128)(2,1)S(1)} %pad_maximum_fusion.rest_0_), channel_id=1, source_target_pairs={{0,1},{1,0},{2,3},{3,2},{4,5},{5,4},{6,7},{7,6},{8,9},{9,8},{10,11... | collective-permute-start | bytes 811016 | tf_op jit(solution)/shard_map/ppermute | solution.py:577
  18.9 2.6 %collective-permute-start.4 = (bf16[528,256]{1,0:T(8,128)(2,1)S(1)}, bf16[528,256]{1,0:T(8,128)(2,1)S(1)}, u32[]{:S(2)}, u32[]{:S(2)}) collective-permute-start(bf16[528,256]{1,0:T(8,128)(2,1)S(1)} %collective-permute-done.rest_4_), channel_id=1, source_target_pairs={{0,1},{1,0},{2,3},{3,2},{4,5},{5,4},{6,7},{7,6},{8,9},{9,8},{10,11... | collective-permute-start | bytes 811016 | tf_op jit(solution)/shard_map/ppermute | solution.py:582
  18.9 5.2 %collective-permute-start.5 = (bf16[528,256]{1,0:T(8,128)(2,1)S(1)}, bf16[528,256]{1,0:T(8,128)(2,1)S(1)}, u32[]{:S(2)}, u32[]{:S(2)}) collective-permute-start(bf16[528,256]{1,0:T(8,128)(2,1)S(1)} %pad_maximum_fusion.rest_0_), channel_id=1, source_target_pairs={{2,4},{3,5},{4,2},{5,3},{10,12},{11,13},{12,10},{13,11},{18,20},{1... | collective-permute-start | bytes 811016 | tf_op jit(solution)/shard_map/ppermute | solution.py:581
  19.5 10.8 %collective-permute-start.6 = (bf16[528,256]{1,0:T(8,128)(2,1)S(1)}, bf16[528,256]{1,0:T(8,128)(2,1)S(1)}, u32[]{:S(2)}, u32[]{:S(2)}) collective-permute-start(bf16[528,256]{1,0:T(8,128)(2,1)S(1)} %collective-permute-done.rest_4_), channel_id=1, source_target_pairs={{4,6},{5,7},{2,0},{3,1},{12,14},{13,15},{10,8},{11,9},{20,22},{21,... | collective-permute-start | bytes 811016 | tf_op jit(solution)/shard_map/ppermute | solution.py:580
  20.8 10.0 %collective-permute-start.2 = (bf16[528,256]{1,0:T(8,128)(2,1)S(1)}, bf16[528,256]{1,0:T(8,128)(2,1)S(1)}, u32[]{:S(2)}, u32[]{:S(2)}) collective-permute-start(bf16[528,256]{1,0:T(8,128)(2,1)S(1)} %collective-permute-done.1.rest_2_), channel_id=1, source_target_pairs={{0,1},{1,0},{2,3},{3,2},{4,5},{5,4},{6,7},{7,6},{8,9},{9,8},{10,11... | collective-permute-start | bytes 811016 | tf_op jit(solution)/shard_map/ppermute | solution.py:586
  30.3 19.1 %copy-start = (bf16[512,256]{1,0:T(8,128)(2,1)S(1)}, bf16[512,256]{1,0:T(8,128)(2,1)}, u32[]{:S(2)}) copy-start(bf16[512,256]{1,0:T(8,128)(2,1)} %cot_ref.1) | copy-start | bytes 786436
  30.3 19.1 %copy-start.1 = (bf16[256,256]{1,0:T(8,128)(2,1)S(1)}, bf16[256,256]{1,0:T(8,128)(2,1)}, u32[]{:S(2)}) copy-start(bf16[256,256]{1,0:T(8,128)(2,1)} %weight_ref.1) | copy-start | bytes 393220
  30.3 19.1 %copy-start.3 = (f32[256]{0:T(256)S(1)}, f32[256]{0:T(256)}, u32[]{:S(2)}) copy-start(f32[256]{0:T(256)} %param.11) | copy-start | bytes 3076
  30.3 1.5 %collective-permute-start.7 = (bf16[528,256]{1,0:T(8,128)(2,1)S(1)}, bf16[528,256]{1,0:T(8,128)(2,1)S(1)}, u32[]{:S(2)}, u32[]{:S(2)}) collective-permute-start(bf16[528,256]{1,0:T(8,128)(2,1)S(1)} %collective-permute-done.5.rest_1_), channel_id=1, source_target_pairs={{0,1},{1,0},{2,3},{3,2},{4,5},{5,4},{6,7},{7,6},{8,9},{9,8},{10,11... | collective-permute-start | bytes 811016 | tf_op jit(solution)/shard_map/ppermute | solution.py:588
  30.3 1.9 %collective-permute-start.8 = (bf16[528,256]{1,0:T(8,128)(2,1)S(1)}, bf16[528,256]{1,0:T(8,128)(2,1)S(1)}, u32[]{:S(2)}, u32[]{:S(2)}) collective-permute-start(bf16[528,256]{1,0:T(8,128)(2,1)S(1)} %collective-permute-done.6.rest_2_), channel_id=1, source_target_pairs={{0,1},{1,0},{2,3},{3,2},{4,5},{5,4},{6,7},{7,6},{8,9},{9,8},{10,11... | collective-permute-start | bytes 811016 | tf_op jit(solution)/shard_map/ppermute | solution.py:588
  34.1 14.0 %collective-permute-start.10 = (bf16[512,256]{1,0:T(8,128)(2,1)S(1)}, bf16[512,256]{1,0:T(8,128)(2,1)S(1)}, u32[]{:S(2)}, u32[]{:S(2)}) collective-permute-start(bf16[512,256]{1,0:T(8,128)(2,1)S(1)} %get-tuple-element.65), channel_id=1, source_target_pairs={{0,16},{8,24},{16,0},{24,8},{1,17},{9,25},{17,1},{25,9},{2,18},{10... | collective-permute-start | bytes 786440 | tf_op jit(solution)/shard_map/ppermute | solution.py:596
  35.8 12.4 %collective-permute-start.11 = (bf16[512,256]{1,0:T(8,128)(2,1)S(1)}, bf16[512,256]{1,0:T(8,128)(2,1)S(1)}, u32[]{:S(2)}, u32[]{:S(2)}) collective-permute-start(bf16[512,256]{1,0:T(8,128)(2,1)S(1)} %get-tuple-element.66), channel_id=1, source_target_pairs={{0,24},{8,16},{16,8},{24,0},{1,25},{9,17},{17,9},{25,1},{2,26},{10... | collective-permute-start | bytes 786440 | tf_op jit(solution)/shard_map/ppermute | solution.py:596
  37.2 12.2 %collective-permute-start.9 = (bf16[512,256]{1,0:T(8,128)(2,1)S(1)}, bf16[512,256]{1,0:T(8,128)(2,1)S(1)}, u32[]{:S(2)}, u32[]{:S(2)}) collective-permute-start(bf16[512,256]{1,0:T(8,128)(2,1)S(1)} %get-tuple-element.64), channel_id=1, source_target_pairs={{0,8},{8,0},{16,24},{24,16},{1,9},{9,1},{17,25},{25,17},{2,10},{10... | collective-permute-start | bytes 786440 | tf_op jit(solution)/shard_map/ppermute | solution.py:596
  51.5 2.6 %collective-permute-start.15 = (f32[136,256]{1,0:T(8,128)S(1)}, f32[136,256]{1,0:T(8,128)S(1)}, u32[]{:S(2)}, u32[]{:S(2)}) collective-permute-start(f32[136,256]{1,0:T(8,128)S(1)} %get-tuple-element.73), channel_id=1, source_target_pairs={{0,1},{1,0},{2,3},{3,2},{4,5},{5,4},{6,7},{7,6},{8,9},{9,8},{10,11... | collective-permute-start | bytes 417800 | tf_op jit(solution)/shard_map/ppermute | solution.py:683
  51.6 10.1 %collective-permute-start.14 = (bf16[512,256]{1,0:T(8,128)(2,1)S(1)}, bf16[512,256]{1,0:T(8,128)(2,1)S(1)}, u32[]{:S(2)}, u32[]{:S(2)}) collective-permute-start(bf16[512,256]{1,0:T(8,128)(2,1)S(1)} %get-tuple-element.69.back_ref), channel_id=1, source_target_pairs={{0,24},{8,16},{16,8},{24,0},{1,25},{9,17},{17,9},{25,1},{2,26},{10... | collective-permute-start | bytes 786440 | tf_op jit(solution)/shard_map/ppermute | solution.py:596
  54.2 7.5 %collective-permute-start.16 = (f32[136,256]{1,0:T(8,128)S(1)}, f32[136,256]{1,0:T(8,128)S(1)}, u32[]{:S(2)}, u32[]{:S(2)}) collective-permute-start(f32[136,256]{1,0:T(8,128)S(1)} %add.26), channel_id=1, source_target_pairs={{0,2},{1,3},{2,0},{3,1},{4,6},{5,7},{6,4},{7,5},{8,10},{9,11},{10,... | collective-permute-start | bytes 417800 | tf_op jit(solution)/shard_map/ppermute | solution.py:604
  54.3 16.2 %collective-permute-start.12 = (bf16[512,256]{1,0:T(8,128)(2,1)S(1)}, bf16[512,256]{1,0:T(8,128)(2,1)S(1)}, u32[]{:S(2)}, u32[]{:S(2)}) collective-permute-start(bf16[512,256]{1,0:T(8,128)(2,1)S(1)} %get-tuple-element.69.back_ref), channel_id=1, source_target_pairs={{0,8},{8,0},{16,24},{24,16},{1,9},{9,1},{17,25},{25,17},{2,10},{10... | collective-permute-start | bytes 786440 | tf_op jit(solution)/shard_map/ppermute | solution.py:596
  54.9 15.6 %collective-permute-start.13 = (bf16[512,256]{1,0:T(8,128)(2,1)S(1)}, bf16[512,256]{1,0:T(8,128)(2,1)S(1)}, u32[]{:S(2)}, u32[]{:S(2)}) collective-permute-start(bf16[512,256]{1,0:T(8,128)(2,1)S(1)} %get-tuple-element.69.back_ref), channel_id=1, source_target_pairs={{0,16},{8,24},{16,0},{24,8},{1,17},{9,25},{17,1},{25,9},{2,18},{10... | collective-permute-start | bytes 786440 | tf_op jit(solution)/shard_map/ppermute | solution.py:596
  61.8 8.7 %collective-permute-start.17 = (f32[136,256]{1,0:T(8,128)S(1)}, f32[136,256]{1,0:T(8,128)S(1)}, u32[]{:S(2)}, u32[]{:S(2)}) collective-permute-start(f32[136,256]{1,0:T(8,128)S(1)} %add.27), channel_id=1, source_target_pairs={{0,4},{1,5},{2,6},{3,7},{4,0},{5,1},{6,2},{7,3},{8,12},{9,13},{10,... | collective-permute-start | bytes 417800 | tf_op jit(solution)/shard_map/ppermute | solution.py:564
  71.6 2.5 %collective-permute-start.18 = (bf16[512,256]{1,0:T(8,128)(2,1)S(1)}, bf16[512,256]{1,0:T(8,128)(2,1)S(1)}, u32[]{:S(2)}, u32[]{:S(2)}) collective-permute-start(bf16[512,256]{1,0:T(8,128)(2,1)S(1)} %get-tuple-element.79), channel_id=1, source_target_pairs={{0,1},{1,0},{2,3},{3,2},{4,5},{5,4},{6,7},{7,6},{8,9},{9,8},{10,11... | collective-permute-start | bytes 786440 | tf_op jit(solution)/shard_map/ppermute | solution.py:608
  74.2 3.3 %collective-permute-start.19 = (bf16[512,256]{1,0:T(8,128)(2,1)S(1)}, bf16[512,256]{1,0:T(8,128)(2,1)S(1)}, u32[]{:S(2)}, u32[]{:S(2)}) collective-permute-start(bf16[512,256]{1,0:T(8,128)(2,1)S(1)} %get-tuple-element.88), channel_id=1, source_target_pairs={{0,1},{1,0},{2,3},{3,2},{4,5},{5,4},{6,7},{7,6},{8,9},{9,8},{10,11... | collective-permute-start | bytes 786440 | tf_op jit(solution)/shard_map/ppermute | solution.py:617
  74.7 4.3 %collective-permute-start.20 = (bf16[512,256]{1,0:T(8,128)(2,1)S(1)}, bf16[512,256]{1,0:T(8,128)(2,1)S(1)}, u32[]{:S(2)}, u32[]{:S(2)}) collective-permute-start(bf16[512,256]{1,0:T(8,128)(2,1)S(1)} %get-tuple-element.89), channel_id=1, source_target_pairs={{0,1},{1,0},{2,3},{3,2},{4,5},{5,4},{6,7},{7,6},{8,9},{9,8},{10,11... | collective-permute-start | bytes 786440 | tf_op jit(solution)/shard_map/ppermute | solution.py:617
  74.8 4.2 %collective-permute-start.21 = (bf16[512,256]{1,0:T(8,128)(2,1)S(1)}, bf16[512,256]{1,0:T(8,128)(2,1)S(1)}, u32[]{:S(2)}, u32[]{:S(2)}) collective-permute-start(bf16[512,256]{1,0:T(8,128)(2,1)S(1)} %get-tuple-element.90), channel_id=1, source_target_pairs={{0,1},{1,0},{2,3},{3,2},{4,5},{5,4},{6,7},{7,6},{8,9},{9,8},{10,11... | collective-permute-start | bytes 786440 | tf_op jit(solution)/shard_map/ppermute | solution.py:617
  75.3 9.4 %collective-permute-start.22 = (bf16[512,256]{1,0:T(8,128)(2,1)S(1)}, bf16[512,256]{1,0:T(8,128)(2,1)S(1)}, u32[]{:S(2)}, u32[]{:S(2)}) collective-permute-start(bf16[512,256]{1,0:T(8,128)(2,1)S(1)} %pair_sums.3), channel_id=1, source_target_pairs={{6,4},{7,5},{0,2},{1,3},{14,12},{15,13},{8,10},{9,11},{22,20},{23,... | collective-permute-start | bytes 786440 | tf_op jit(solution)/shard_map/ppermute | solution.py:615
  76.7 7.9 %collective-permute-start.23 = (bf16[512,256]{1,0:T(8,128)(2,1)S(1)}, bf16[512,256]{1,0:T(8,128)(2,1)S(1)}, u32[]{:S(2)}, u32[]{:S(2)}) collective-permute-start(bf16[512,256]{1,0:T(8,128)(2,1)S(1)} %pair_sums.3), channel_id=1, source_target_pairs={{2,4},{3,5},{4,2},{5,3},{10,12},{11,13},{12,10},{13,11},{18,20},{1... | collective-permute-start | bytes 786440 | tf_op jit(solution)/shard_map/ppermute | solution.py:616
  77.4 5.6 %collective-permute-start.24 = (f32[136,256]{1,0:T(8,128)S(1)}, f32[136,256]{1,0:T(8,128)S(1)}, u32[]{:S(2)}, u32[]{:S(2)}) collective-permute-start(f32[136,256]{1,0:T(8,128)S(1)} %add.28), channel_id=1, source_target_pairs={{0,8},{8,0},{16,24},{24,16},{1,9},{9,1},{17,25},{25,17},{2,10},{10... | collective-permute-start | bytes 417800 | tf_op jit(solution)/shard_map/ppermute | solution.py:609
  83.0 5.1 %collective-permute-start.25 = (f32[136,256]{1,0:T(8,128)S(1)}, f32[136,256]{1,0:T(8,128)S(1)}, u32[]{:S(2)}, u32[]{:S(2)}) collective-permute-start(f32[136,256]{1,0:T(8,128)S(1)} %add.29), channel_id=1, source_target_pairs={{0,16},{8,24},{16,0},{24,8},{1,17},{9,25},{17,1},{25,9},{2,18},{10... | collective-permute-start | bytes 417800 | tf_op jit(solution)/shard_map/ppermute | solution.py:564
  84.7 13.7 %collective-permute-start.27 = (bf16[512,256]{1,0:T(8,128)(2,1)S(1)}, bf16[512,256]{1,0:T(8,128)(2,1)S(1)}, u32[]{:S(2)}, u32[]{:S(2)}) collective-permute-start(bf16[512,256]{1,0:T(8,128)(2,1)S(1)} %add_convert_fusion), channel_id=1, source_target_pairs={{0,4},{1,5},{4,0},{5,1},{2,6},{3,7},{6,2},{7,3},{8,12},{9,13},{12,... | collective-permute-start | bytes 786440 | tf_op jit(solution)/shard_map/ppermute | solution.py:626
  88.2 10.5 %collective-permute-start.26 = (bf16[512,256]{1,0:T(8,128)(2,1)S(1)}, bf16[512,256]{1,0:T(8,128)(2,1)S(1)}, u32[]{:S(2)}, u32[]{:S(2)}) collective-permute-start(bf16[512,256]{1,0:T(8,128)(2,1)S(1)} %get-tuple-element.101), channel_id=1, source_target_pairs={{0,2},{1,3},{2,0},{3,1},{4,6},{5,7},{6,4},{7,5},{8,10},{9,11},{10,... | collective-permute-start | bytes 786440 | tf_op jit(solution)/shard_map/ppermute | solution.py:628
  89.3 1.4 %collective-permute-start.28 = (f32[136,256]{1,0:T(8,128)S(1)}, f32[136,256]{1,0:T(8,128)S(1)}, u32[]{:S(2)}, u32[]{:S(2)}) collective-permute-start(f32[136,256]{1,0:T(8,128)S(1)} %add.30.mine_ref), channel_id=1, source_target_pairs={{0,1},{1,0},{2,3},{3,2},{4,5},{5,4},{6,7},{7,6},{8,9},{9,8},{10,11... | collective-permute-start | bytes 417800 | tf_op jit(solution)/shard_map/ppermute | solution.py:704
  (2 other events, 1.4 us)

commit v5 on v4

--- a/solution.py
+++ b/solution.py
@@ -165,13 +165,11 @@
     return rows.astype(BF16)
 
 
-def forward_part_kernel(groups, base, peers, last, pos_ref, dense_ref, *rest):
+def forward_part_kernel(groups, base, peers, added, last, pos_ref, dense_ref, *rest):
     total = sum(groups)
-    sources, rest = rest[:total], rest[total:]
-    if last:
-        partial_ref, outs, put_ref, gathered = rest[0], rest[1 : 1 + peers], rest[1 + peers], rest[-1]
-    else:
-        partial_ref, put_ref, gathered = rest
+    sources, rest = rest[:total], list(rest[total:])
+    before_ref = rest.pop(0) if added else None
+    *outs, put_ref, gathered = rest
     here = pos_ref[1]
     capacity = put_ref.shape[2]
     at = 0
@@ -180,40 +178,40 @@
         gathered[slot * capacity : (slot + 1) * capacity, :] = rows
         at += count
     columns = slice(base * capacity, (base + len(groups)) * capacity)
-    if not last:
-        partial_ref[...] = jnp.dot(
-            dense_ref[:, columns], gathered[...], preferred_element_type=F32
-        )
-        return
-    block = outs[0].shape[0]
+    block = dense_ref.shape[0] // peers
     for peer in range(peers):
         here_rows = slice(peer * block, (peer + 1) * block)
-        result = partial_ref[here_rows, :] + jnp.dot(
+        result = jnp.dot(
             dense_ref[here_rows, columns], gathered[...], preferred_element_type=F32
         )
-        outs[peer][...] = result.astype(outs[peer].dtype)
-
-
-def forward_part(dense, groups, base, pos, peers, nodes, capacity, before=None):
+        if added:
+            result = before_ref[here_rows, :] + result
+        if last:
+            outs[peer][...] = result.astype(outs[peer].dtype)
+        else:
+            outs[0][here_rows, :] = result
+
+
+def forward_part(dense, groups, base, pos, peers, nodes, capacity, before=None, last=False):
     rows = dense.shape[0]
     flat = [array for group in groups for array in group]
     width = flat[0].shape[1]
-    last = before is not None
-    put = jax.ShapeDtypeStruct((len(groups), nodes, capacity), BF16)
+    added = before is not None
     if last:
         outs = tuple(
             jax.ShapeDtypeStruct((rows // peers, width), F32 if peer == 0 else BF16)
             for peer in range(peers)
-        ) + (put,)
+        )
+    else:
+        outs = (jax.ShapeDtypeStruct((rows, width), F32),)
+    depth = len(groups) * capacity
+    if added:
         flat = flat + [before]
-    else:
-        outs = (jax.ShapeDtypeStruct((rows, width), F32), put)
-    depth = len(groups) * capacity
     return pl.pallas_call(
         functools.partial(
-            forward_part_kernel, tuple(len(group) for group in groups), base, peers, last
-        ),
-        out_shape=outs,
+            forward_part_kernel, tuple(len(group) for group in groups), base, peers, added, last
+        ),
+        out_shape=outs + (jax.ShapeDtypeStruct((len(groups), nodes, capacity), BF16),),
         in_specs=[pl.BlockSpec(memory_space=pltpu.SMEM)]
         + [pl.BlockSpec(memory_space=pltpu.VMEM)] * (1 + len(flat)),
         scratch_shapes=[pltpu.VMEM((depth, width), BF16)],
@@ -221,7 +219,7 @@
         cost_estimate=pl.CostEstimate(
             flops=2 * rows * depth * width, bytes_accessed=2 * rows * depth, transcendentals=0
         ),
-        name="forward_late" if last else "forward_early",
+        name="forward_last" if last else "forward_part",
     )(pos, dense, *flat)
 
 
@@ -280,9 +278,8 @@
     )(pos, pick, dense, *flat)
 
 
-def layer_kernel(peers, weight_ref, bias_ref, cot_ref, *rest):
-    parts, outs = rest[:peers], rest[peers:]
-    out_ref, agg_ref, grad_ref = outs[:3]
+def layer_kernel(peers, scale, pos_ref, weight_ref, bias_ref, cot_ref, *rest):
+    parts, (out_ref, back_ref, mine_ref, theirs_ref) = rest[:peers], rest[peers:]
     total = parts[0][...].astype(F32)
     for peer in range(1, peers):
         total = total + parts[peer][...].astype(F32)
@@ -292,32 +289,11 @@
     sigma = 1.0 / (1.0 + jnp.exp(-preact))
     out_ref[...] = (preact * sigma).astype(BF16)
     grad = (cot_ref[...].astype(F32) * sigma * (1.0 + preact * (1.0 - sigma))).astype(BF16)
-    agg_ref[...] = agg
-    grad_ref[...] = grad
-    outs[3][...] = lax.dot_general(
+    back_ref[...] = lax.dot_general(
         grad, weight, (((1,), (1,)), ((), ())), preferred_element_type=F32
     ).astype(BF16)
-
-
-def layer(weight, bias_vector, cotangent, parts):
-    nodes, width = cotangent.shape
-    return pl.pallas_call(
-        functools.partial(layer_kernel, len(parts)),
-        out_shape=(jax.ShapeDtypeStruct((nodes, width), BF16),) * 4,
-        compiler_params=params(),
-        cost_estimate=pl.CostEstimate(
-            flops=4 * nodes * width * width,
-            bytes_accessed=2 * nodes * width * 10,
-            transcendentals=nodes * width,
-        ),
-        name="layer",
-    )(weight, bias_vector.reshape(1, -1), cotangent, *parts)
-
-
-def weights_kernel(scale, pos_ref, agg_ref, grad_ref, mine_ref, theirs_ref):
-    grad = grad_ref[...]
     product = scale * lax.dot_general(
-        agg_ref[...], grad, (((0,), (0,)), ((), ())), preferred_element_type=F32
+        agg, grad, (((0,), (0,)), ((), ())), preferred_element_type=F32
     )
     bias = scale * jnp.sum(grad.astype(F32).reshape(-1, 8, grad.shape[1]), axis=0)
     half = product.shape[0] // 2
@@ -333,19 +309,22 @@
     theirs_ref[half:] = bias
 
 
-def weight_partials(agg, grad, pos, scale):
-    nodes, width = agg.shape
-    return pl.pallas_call(
-        functools.partial(weights_kernel, scale),
-        out_shape=(jax.ShapeDtypeStruct((width // 2 + 8, width), F32),) * 2,
+def layer(weight, bias_vector, cotangent, parts, pos, scale):
+    nodes, width = cotangent.shape
+    return pl.pallas_call(
+        functools.partial(layer_kernel, len(parts), scale),
+        out_shape=(jax.ShapeDtypeStruct((nodes, width), BF16),) * 2
+        + (jax.ShapeDtypeStruct((width // 2 + 8, width), F32),) * 2,
         in_specs=[pl.BlockSpec(memory_space=pltpu.SMEM)]
-        + [pl.BlockSpec(memory_space=pltpu.VMEM)] * 2,
+        + [pl.BlockSpec(memory_space=pltpu.VMEM)] * (3 + len(parts)),
         compiler_params=params(),
         cost_estimate=pl.CostEstimate(
-            flops=2 * nodes * width * width, bytes_accessed=6 * nodes * width, transcendentals=0
-        ),
-        name="weight_partials",
-    )(pos, agg, grad)
+            flops=6 * nodes * width * width,
+            bytes_accessed=2 * nodes * width * 10,
+            transcendentals=nodes * width,
+        ),
+        name="layer",
+    )(pos, weight, bias_vector.reshape(1, -1), cotangent, *parts)
 
 
 def assemble_kernel(pos_ref, mine_ref, theirs_ref, weight_ref, bias_ref):
@@ -582,13 +561,13 @@
     early = [[piece], [other], [near], [lax.ppermute(far, "col", CORE)], [far]]
     partial, put_early = forward_part(dense, early, 0, pos, rows, nodes, capacity)
     partial, middle, ends = lax.optimization_barrier((partial, middle, ends))
-    late = [
-        [lax.ppermute(near, "col", CORE)],
-        [middle, ends],
-        [lax.ppermute(middle, "col", CORE), lax.ppermute(ends, "col", CORE)],
-    ]
-    *blocks, put_late = forward_part(dense, late, 5, pos, rows, nodes, capacity, partial)
-    return dense, put_early, put_late, blocks
+    other = [lax.ppermute(middle, "col", CORE), lax.ppermute(ends, "col", CORE)]
+    late = [[lax.ppermute(near, "col", CORE)], [middle, ends]]
+    partial, put_late = forward_part(dense, late, 5, pos, rows, nodes, capacity, partial)
+    *blocks, put_last = forward_part(
+        dense, [other], 7, pos, rows, nodes, capacity, partial, True
+    )
+    return dense, (put_early, put_late, put_last), blocks
 
 
 def row_exchange(own, arrays, rows):
@@ -599,12 +578,15 @@
     return [own] + received[::-1]
 
 
-def line_reduce(dense, put_early, put_late, back, backs, pos, sums, rows, columns):
+def line_reduce(dense, puts, back, backs, sums, rows, columns):
+    put_early, put_late, put_last = puts
     first = backward_early(dense, back)
-    sums = sums + after(lax.ppermute(sums, "col", xor_pairs(columns, 2)), backs[2])
-    sums = exchange_add(sums, "col", columns, 4)
+    sums = sums + after(lax.ppermute(sums, "col", xor_pairs(columns, 4)), backs[2])
+    sums = exchange_add(sums, "col", columns, 2)
     *backs, first, sums = lax.optimization_barrier((*backs, first, sums))
-    keep3, give3 = backward_late(dense, (put_late,), ((1, 2),), first, backs, 6)
+    keep3, give3 = backward_late(
+        dense, (put_late, put_last), ((1,), (0,)), first, backs, 6
+    )
     got3 = lax.ppermute(give3, "col", CORE)
     received = lax.ppermute(sums, "row", xor_pairs(rows, 1))
     keep0, give0, keep1, give2, keep2, give1 = backward_late(
@@ -649,7 +631,7 @@
     line = columns == 8 and 2 * tiles.shape[0] * TILE * columns * capacity <= RESIDENT
 
     if line:
-        dense, put_early, put_late, blocks = line_exchange(
+        dense, puts, blocks = line_exchange(
             piece,
             lambda: densify(tiles, source, count, pos, rows, columns, capacity),
             pos,
@@ -676,15 +658,14 @@
         blocks = forward_blocks(dense, pick, [[a[:nodes]] for a in pieces], pos, rows)
 
     parts = row_exchange(blocks[0], blocks[1:], rows)
-    output, agg, grad_pre, back = layer(weight, bias_vector, cotangent, parts)
+    scale = 1.0 / math.sqrt(nodes * rows * columns)
+    output, back, mine, theirs = layer(weight, bias_vector, cotangent, parts, pos, scale)
     backs = row_exchange(back, [back] * (rows - 1), rows)
-    scale = 1.0 / math.sqrt(nodes * rows * columns)
-    mine, theirs = weight_partials(agg, grad_pre, pos, scale)
     sums = mine + lax.ppermute(theirs, "col", CORE if line else xor_pairs(columns, 1))
 
     if line:
         terms, sums = line_reduce(
-            dense, put_early, put_late, back, backs[1:], pos, sums, rows, columns
+            dense, puts, back, backs[1:], sums, rows, columns
         )
     else:
         scattered = backward_blocks(dense, put, backs, pos, (0,))

time: 99.8 us -> 99.2 us (level)
  waiting for transfers between devices: 48 us -> 43.9 us
  starting transfers between devices: 27.9 us -> 30.6 us
    ppermute x2, waiting for transfers between devices: 7.83 us -> 4.28 us  [exchange_add(): return value + lax.ppermute(value, axis, xor_pairs(size, step))]
    ppermute x2, starting transfers between devices: 3.16 us -> 0.65 us  [exchange_add(): return value + lax.ppermute(value, axis, xor_pairs(size, step))]
    ppermute x1, starting transfers between devices: 1.97 us -> 4.42 us  [line_reduce(): from_far = lax.ppermute(far, 'col', LINE_SWAP2)]
    ppermute x1, starting transfers between devices: 1.11 us -> 2.77 us  [line_reduce(): from_near = lax.ppermute(after(near, far), 'col', LINE_SWAP1)]
    ppermute x6, waiting for transfers between devices: 17.3 us -> 15.7 us  [row_exchange(): lax.ppermute(arrays[step - 1], 'row', xor_pairs(rows, step))]
    ppermute x4, starting transfers between devices: 1.15 us -> 2.61 us  [the longest x1 1.53 us: line_reduce(): lax.ppermute(sums, 'col', xor_pairs(columns, 4))]
    pallas_call x2 -> x3, Pallas kernels: 4.48 us -> 5.43 us  [forward_part(): pl.pallas_call(functools.partial(forward_part_kernel, tuple((len(group) f...]
    pallas_call x2 -> x1, Pallas kernels: 2.14 us -> 2.07 us  [layer(): pl.pallas_call(functools.partial(layer_kernel, len(parts), scale), out_sh...]
  transfers between devices with their start and end apart: 29 -> 29, of which waited for: 13 -> 12; matrix products, arithmetic and copies ran while one was open for 0% -> 0% of each run, Pallas kernels for 13% -> 15%
where the time goes in v5:
time: 99.2 us; the launch traced here: 98.9 us
  waiting for transfers between devices  43.9 us (44%)
  starting transfers between devices  30.6 us (31%)
  Pallas kernels  20.2 us (20%)
  other arithmetic  1.98 us (2%)
  local copies, waits for them, and re-layouts  1.37 us (1%)
    ppermute x6, waiting for transfers between devices, row_exchange(): lax.ppermute(arrays[step - 1], 'row', xor_pairs(rows, step))  15.7 us
    ppermute x6, starting transfers between devices, row_exchange(): lax.ppermute(arrays[step - 1], 'row', xor_pairs(rows, step))  7.96 us
    ppermute x1, waiting for transfers between devices, line_exchange(): ends = lax.ppermute(far, 'col', LINE_OUT)  6.3 us
    pallas_call x1, Pallas kernels, densify(): pl.pallas_call(functools.partial(densify_kernel, capacity // TILE, target...  6.07 us
    ppermute x1, waiting for transfers between devices, line_reduce(): from_far = lax.ppermute(far, 'col', LINE_SWAP2)  5.96 us
    pallas_call x3, Pallas kernels, forward_part(): pl.pallas_call(functools.partial(forward_part_kernel, tuple((len(group) f...  5.43 us
    ppermute x1, waiting for transfers between devices, line_reduce(): received = lax.ppermute(sums, 'row', xor_pairs(rows, 1))  4.7 us
    ppermute x1, starting transfers between devices, line_reduce(): from_far = lax.ppermute(far, 'col', LINE_SWAP2)  4.42 us
  transfers between devices with their start and end apart: 29, of which 12 were waited for; matrix products, arithmetic and copies ran while one was open for 0% of the time, Pallas kernels for 15%

profile of v5, /device:TPU:0, one launch (start us, length us, event | category | flops | bytes accessed | tf_op | source)
XLA Modules:
  0.0 98.9 jit_solution(11415149106373745704)
XLA Ops:
  1.4 1.0 pad_maximum_fusion.rest_0_
  2.4 4.1 %collective-permute-start = (bf16[528,256]{1,0:T(8,128)(2,1)S(1)}, bf16[528,256]{1,0:T(8,128)(2,1)S(1)}, u32[]{:S(2)}, u32[]{:S(2)}) collective-permute-start(bf16[528,256]{1,0:T(8,128)(2,1)S(1)} %pad_maximum_fusion.rest_0_), channel_id=1, source_target_pairs={{0,4},{1,5},{4,0},{5,1},{2,6},{3,7},{6,2},{7,3},{8,12},{9,13},{12,... | collective-permute-start | bytes 811016 | tf_op jit(solution)/shard_map/ppermute | solution.py:554
  6.5 1.6 %collective-permute-start.2 = (bf16[528,256]{1,0:T(8,128)(2,1)S(1)}, bf16[528,256]{1,0:T(8,128)(2,1)S(1)}, u32[]{:S(2)}, u32[]{:S(2)}) collective-permute-start(bf16[528,256]{1,0:T(8,128)(2,1)S(1)} %pad_maximum_fusion.rest_0_), channel_id=1, source_target_pairs={{0,2},{1,3},{2,0},{3,1},{4,6},{5,7},{6,4},{7,5},{8,10},{9,11},{10,... | collective-permute-start | bytes 811016 | tf_op jit(solution)/shard_map/ppermute | solution.py:555
  9.5 6.1 %densify.1.dense_ref = bf16[2048,2048]{1,0:T(8,128)(2,1)S(1)} custom-call(s32[16,16]{1,0:T(8,128)S(1)} %bitcast.34, s32[16]{0:T(128)S(1)} %bitcast.36, s32[2]{0:T(128)S(1)} %pad_add_fusion.pos_ref, bf16[16,16,128,128]{3,2,1,0:T(8,128)(2,1)} %bitcast.37), custom_call_target="tpu_custom_call" | custom-call | bytes 16777216 | tf_op jit(solution)/shard_map/densify/pallas_call | solution.py:64
  15.6 3.3 %collective-permute-done.rest_4_ = bf16[528,256]{1,0:T(8,128)(2,1)S(1)} collective-permute-done((bf16[528,256]{1,0:T(8,128)(2,1)S(1)}, bf16[528,256]{1,0:T(8,128)(2,1)S(1)}, u32[]{:S(2)}, u32[]{:S(2)}) %collective-permute-start) | collective-permute-done | bytes 270368 | tf_op jit(solution)/shard_map/ppermute | solution.py:554
  19.5 1.3 %collective-permute-start.5 = (bf16[528,256]{1,0:T(8,128)(2,1)S(1)}, bf16[528,256]{1,0:T(8,128)(2,1)S(1)}, u32[]{:S(2)}, u32[]{:S(2)}) collective-permute-start(bf16[528,256]{1,0:T(8,128)(2,1)S(1)} %collective-permute-done.rest_4_), channel_id=1, source_target_pairs={{4,6},{5,7},{2,0},{3,1},{12,14},{13,15},{10,8},{11,9},{20,22},{21,... | collective-permute-start | bytes 811016 | tf_op jit(solution)/shard_map/ppermute | solution.py:559
  21.4 2.6 %forward_part.2 = (f32[2048,256]{1,0:T(8,128)S(1)}, bf16[5,512,256]{2,1,0:T(8,128)(2,1)S(1)}) custom-call(s32[2]{0:T(128)S(1)} %pad_add_fusion.pos_ref, bf16[2048,2048]{1,0:T(8,128)(2,1)S(1)} %densify.1.dense_ref, bf16[528,256]{1,0:T(8,128)(2,1)S(1)} %pad_maximum_fusion.rest_0_, bf16[528,256]{1,0:T(8,128)(2,1)S(1)} %collective-permute-done.1.rest_1_, ...), custom_call_target="tpu_custom_call" | custom-call | flops 1342177280 | bytes 5242880 | tf_op jit(solution)/shard_map/forward_part/pallas_call | solution.py:210
  24.0 6.3 %collective-permute-done.5.rest_2_ = bf16[528,256]{1,0:T(8,128)(2,1)S(1)} collective-permute-done((bf16[528,256]{1,0:T(8,128)(2,1)S(1)}, bf16[528,256]{1,0:T(8,128)(2,1)S(1)}, u32[]{:S(2)}, u32[]{:S(2)}) %collective-permute-start.5) | collective-permute-done | bytes 270368 | tf_op jit(solution)/shard_map/ppermute | solution.py:559
  30.8 1.6 %forward_part.3 = (f32[2048,256]{1,0:T(8,128)S(1)}, bf16[2,512,256]{2,1,0:T(8,128)(2,1)S(1)}) custom-call(s32[2]{0:T(128)S(1)} %pad_add_fusion.pos_ref, bf16[2048,2048]{1,0:T(8,128)(2,1)S(1)} %densify.1.dense_ref, bf16[528,256]{1,0:T(8,128)(2,1)S(1)} %collective-permute-done.8.rest_0_, bf16[528,256]{1,0:T(8,128)(2,1)S(1)} %collective-permute-done.4.rest_1_, ...), custom_call_target="tpu_custom_call" | custom-call | flops 536870912 | bytes 2097152 | tf_op jit(solution)/shard_map/forward_part/pallas_call | solution.py:210
  32.5 1.3 %forward_last.1 = (f32[512,256]{1,0:T(8,128)S(1)}, bf16[512,256]{1,0:T(8,128)(2,1)S(1)}, bf16[512,256]{1,0:T(8,128)(2,1)S(1)}, bf16[512,256]{1,0:T(8,128)(2,1)S(1)}, bf16[1,512,256]{2,1,0:T(8,128)(2,1)S(1)}) custom-call(s32[2]{0:T(128)S(1)} %pad_add_fusion.pos_ref, bf16[2048,2048]{1,0:T(8,128)(2,1)S(1)} %densify.1.dense_ref, ...), custom_call_target="tpu_custom_call" | custom-call | flops 268435456 | bytes 1048576 | tf_op jit(solution)/shard_map/forward_last/pallas_call | solution.py:210
  33.7 1.6 %collective-permute-start.10 = (bf16[512,256]{1,0:T(8,128)(2,1)S(1)}, bf16[512,256]{1,0:T(8,128)(2,1)S(1)}, u32[]{:S(2)}, u32[]{:S(2)}) collective-permute-start(bf16[512,256]{1,0:T(8,128)(2,1)S(1)} %get-tuple-element.66), channel_id=1, source_target_pairs={{0,16},{8,24},{16,0},{24,8},{1,17},{9,25},{17,1},{25,9},{2,18},{10... | collective-permute-start | bytes 786440 | tf_op jit(solution)/shard_map/ppermute | solution.py:575
  35.4 1.4 %collective-permute-start.11 = (bf16[512,256]{1,0:T(8,128)(2,1)S(1)}, bf16[512,256]{1,0:T(8,128)(2,1)S(1)}, u32[]{:S(2)}, u32[]{:S(2)}) collective-permute-start(bf16[512,256]{1,0:T(8,128)(2,1)S(1)} %get-tuple-element.67), channel_id=1, source_target_pairs={{0,24},{8,16},{16,8},{24,0},{1,25},{9,17},{17,9},{25,1},{2,26},{10... | collective-permute-start | bytes 786440 | tf_op jit(solution)/shard_map/ppermute | solution.py:575
  37.3 10.3 %collective-permute-done.10.rest_2_ = bf16[512,256]{1,0:T(8,128)(2,1)S(1)} collective-permute-done((bf16[512,256]{1,0:T(8,128)(2,1)S(1)}, bf16[512,256]{1,0:T(8,128)(2,1)S(1)}, u32[]{:S(2)}, u32[]{:S(2)}) %collective-permute-start.10) | collective-permute-done | bytes 262176 | tf_op jit(solution)/shard_map/ppermute | solution.py:575
  47.6 1.2 %collective-permute-done.9.rest_1_ = bf16[512,256]{1,0:T(8,128)(2,1)S(1)} collective-permute-done((bf16[512,256]{1,0:T(8,128)(2,1)S(1)}, bf16[512,256]{1,0:T(8,128)(2,1)S(1)}, u32[]{:S(2)}, u32[]{:S(2)}) %collective-permute-start.9) | collective-permute-done | bytes 262176 | tf_op jit(solution)/shard_map/ppermute | solution.py:575
  48.9 2.1 %layer.1 = (bf16[512,256]{1,0:T(8,128)(2,1)}, bf16[512,256]{1,0:T(8,128)(2,1)S(1)}, f32[136,256]{1,0:T(8,128)S(1)}, f32[136,256]{1,0:T(8,128)S(1)}) custom-call(s32[2]{0:T(128)S(1)} %pad_add_fusion.pos_ref, bf16[256,256]{1,0:T(8,128)(2,1)S(1)} %copy-done.1, f32[1,256]{1,0:T(1,128)S(1)} %bitcast.35, bf16[512,256]{1,0:T(8,128)(2,1)S(1)} %copy-done, ...), custom_call_target="tpu_custom_call" | custom-call | flops 201326592 | bytes 2621440 | tf_op jit(solution)/shard_map/layer/pallas_call | solution.py:314
  51.0 2.5 %collective-permute-start.14 = (bf16[512,256]{1,0:T(8,128)(2,1)S(1)}, bf16[512,256]{1,0:T(8,128)(2,1)S(1)}, u32[]{:S(2)}, u32[]{:S(2)}) collective-permute-start(bf16[512,256]{1,0:T(8,128)(2,1)S(1)} %get-tuple-element.71.back_ref), channel_id=1, source_target_pairs={{0,24},{8,16},{16,8},{24,0},{1,25},{9,17},{17,9},{25,1},{2,26},{10... | collective-permute-start | bytes 786440 | tf_op jit(solution)/shard_map/ppermute | solution.py:575
  53.5 1.5 %collective-permute-start.16 = (f32[136,256]{1,0:T(8,128)S(1)}, f32[136,256]{1,0:T(8,128)S(1)}, u32[]{:S(2)}, u32[]{:S(2)}) collective-permute-start(f32[136,256]{1,0:T(8,128)S(1)} %add.26), channel_id=1, source_target_pairs={{0,4},{1,5},{2,6},{3,7},{4,0},{5,1},{6,2},{7,3},{8,12},{9,13},{10,... | collective-permute-start | bytes 417800 | tf_op jit(solution)/shard_map/ppermute | solution.py:584
  55.5 1.4 %collective-permute-start.13 = (bf16[512,256]{1,0:T(8,128)(2,1)S(1)}, bf16[512,256]{1,0:T(8,128)(2,1)S(1)}, u32[]{:S(2)}, u32[]{:S(2)}) collective-permute-start(bf16[512,256]{1,0:T(8,128)(2,1)S(1)} %get-tuple-element.71.back_ref), channel_id=1, source_target_pairs={{0,16},{8,24},{16,0},{24,8},{1,17},{9,25},{17,1},{25,9},{2,18},{10... | collective-permute-start | bytes 786440 | tf_op jit(solution)/shard_map/ppermute | solution.py:575
  56.9 4.1 %collective-permute-done.14.rest_5_ = bf16[512,256]{1,0:T(8,128)(2,1)S(1)} collective-permute-done((bf16[512,256]{1,0:T(8,128)(2,1)S(1)}, bf16[512,256]{1,0:T(8,128)(2,1)S(1)}, u32[]{:S(2)}, u32[]{:S(2)}) %collective-permute-start.14) | collective-permute-done | bytes 262176 | tf_op jit(solution)/shard_map/ppermute | solution.py:575
  61.0 2.2 %collective-permute-done.16 = f32[136,256]{1,0:T(8,128)S(1)} collective-permute-done((f32[136,256]{1,0:T(8,128)S(1)}, f32[136,256]{1,0:T(8,128)S(1)}, u32[]{:S(2)}, u32[]{:S(2)}) %collective-permute-start.16) | collective-permute-done | bytes 139296 | tf_op jit(solution)/shard_map/ppermute | solution.py:584
  63.3 0.8 backward_early.1.rest_2_
  64.1 4.2 %collective-permute-done.17 = f32[136,256]{1,0:T(8,128)S(1)} collective-permute-done((f32[136,256]{1,0:T(8,128)S(1)}, f32[136,256]{1,0:T(8,128)S(1)}, u32[]{:S(2)}, u32[]{:S(2)}) %collective-permute-start.17) | collective-permute-done | bytes 139296 | tf_op jit(solution)/shard_map/ppermute | solution.py:543
  68.4 1.0 %backward_late.2 = (f32[512,256]{1,0:T(8,128)S(1)}, bf16[512,256]{1,0:T(8,128)(2,1)S(1)}) custom-call(bf16[2048,2048]{1,0:T(8,128)(2,1)S(1)} %densify.1.dense_ref, bf16[2,512,256]{2,1,0:T(8,128)(2,1)S(1)} %get-tuple-element.69.rest_0_.rest_1_, bf16[1,512,256]{2,1,0:T(8,128)(2,1)S(1)} %get-tuple-element.70.rest_1_, f32[2048,256]{1,0:T(8,128)S(1)} %backward_early.1.rest_2_, ...), custom_call_target="tpu_custom_call" | custom-call | flops 536870912 | bytes 2097152 | tf_op jit(solution)/shard_map/backward_late/pallas_call | solution.py:409
  69.5 2.5 %backward_late.3 = (f32[512,256]{1,0:T(8,128)S(1)}, bf16[512,256]{1,0:T(8,128)(2,1)S(1)}, f32[512,256]{1,0:T(8,128)S(1)}, bf16[512,256]{1,0:T(8,128)(2,1)S(1)}, ...) custom-call(bf16[2048,2048]{1,0:T(8,128)(2,1)S(1)} %densify.1.dense_ref, ...), custom_call_target="tpu_custom_call" | custom-call | flops 1610612736 | bytes 6291456 | tf_op jit(solution)/shard_map/backward_late/pallas_call | solution.py:409
  73.2 2.1 %collective-permute-start.22 = (bf16[512,256]{1,0:T(8,128)(2,1)S(1)}, bf16[512,256]{1,0:T(8,128)(2,1)S(1)}, u32[]{:S(2)}, u32[]{:S(2)}) collective-permute-start(bf16[512,256]{1,0:T(8,128)(2,1)S(1)} %pair_sums.3), channel_id=1, source_target_pairs={{6,4},{7,5},{0,2},{1,3},{14,12},{15,13},{8,10},{9,11},{22,20},{23,... | collective-permute-start | bytes 786440 | tf_op jit(solution)/shard_map/ppermute | solution.py:597
  76.7 4.7 %collective-permute-done.24 = f32[136,256]{1,0:T(8,128)S(1)} collective-permute-done((f32[136,256]{1,0:T(8,128)S(1)}, f32[136,256]{1,0:T(8,128)S(1)}, u32[]{:S(2)}, u32[]{:S(2)}) %collective-permute-start.24) | collective-permute-done | bytes 139296 | tf_op jit(solution)/shard_map/ppermute | solution.py:591
  82.1 4.4 %collective-permute-start.27 = (bf16[512,256]{1,0:T(8,128)(2,1)S(1)}, bf16[512,256]{1,0:T(8,128)(2,1)S(1)}, u32[]{:S(2)}, u32[]{:S(2)}) collective-permute-start(bf16[512,256]{1,0:T(8,128)(2,1)S(1)} %add_convert_fusion), channel_id=1, source_target_pairs={{0,4},{1,5},{4,0},{5,1},{2,6},{3,7},{6,2},{7,3},{8,12},{9,13},{12,... | collective-permute-start | bytes 786440 | tf_op jit(solution)/shard_map/ppermute | solution.py:608
  86.6 2.8 %collective-permute-start.26 = (bf16[512,256]{1,0:T(8,128)(2,1)S(1)}, bf16[512,256]{1,0:T(8,128)(2,1)S(1)}, u32[]{:S(2)}, u32[]{:S(2)}) collective-permute-start(bf16[512,256]{1,0:T(8,128)(2,1)S(1)} %get-tuple-element.101), channel_id=1, source_target_pairs={{0,2},{1,3},{2,0},{3,1},{4,6},{5,7},{6,4},{7,5},{8,10},{9,11},{10,... | collective-permute-start | bytes 786440 | tf_op jit(solution)/shard_map/ppermute | solution.py:610
  89.4 1.4 %collective-permute-done.28.theirs_ref = f32[136,256]{1,0:T(8,128)S(1)} collective-permute-done((f32[136,256]{1,0:T(8,128)S(1)}, f32[136,256]{1,0:T(8,128)S(1)}, u32[]{:S(2)}, u32[]{:S(2)}) %collective-permute-start.28) | collective-permute-done | bytes 139296 | tf_op jit(solution)/shard_map/ppermute | solution.py:685
  90.7 1.3 %assemble.1 = (f32[256,256]{1,0:T(8,128)}, f32[1,256]{1,0:T(1,128)}) custom-call(s32[2]{0:T(128)S(1)} %pad_add_fusion.pos_ref, f32[136,256]{1,0:T(8,128)S(1)} %add.30.mine_ref, f32[136,256]{1,0:T(8,128)S(1)} %collective-permute-done.28.theirs_ref), custom_call_target="tpu_custom_call" | custom-call | bytes 1048576 | tf_op jit(solution)/shard_map/assemble/pallas_call | solution.py:342
  92.0 6.0 %collective-permute-done.27.refs_3_ = bf16[512,256]{1,0:T(8,128)(2,1)S(1)} collective-permute-done((bf16[512,256]{1,0:T(8,128)(2,1)S(1)}, bf16[512,256]{1,0:T(8,128)(2,1)S(1)}, u32[]{:S(2)}, u32[]{:S(2)}) %collective-permute-start.27) | collective-permute-done | bytes 262176 | tf_op jit(solution)/shard_map/ppermute | solution.py:608
  98.1 0.8 finish.1
  (57 shorter events, 8.6 us)
Async XLA Ops:
  2.4 16.5 %collective-permute-start = (bf16[528,256]{1,0:T(8,128)(2,1)S(1)}, bf16[528,256]{1,0:T(8,128)(2,1)S(1)}, u32[]{:S(2)}, u32[]{:S(2)}) collective-permute-start(bf16[528,256]{1,0:T(8,128)(2,1)S(1)} %pad_maximum_fusion.rest_0_), channel_id=1, source_target_pairs={{0,4},{1,5},{4,0},{5,1},{2,6},{3,7},{6,2},{7,3},{8,12},{9,13},{12,... | collective-permute-start | bytes 811016 | tf_op jit(solution)/shard_map/ppermute | solution.py:554
  6.5 14.4 %collective-permute-start.2 = (bf16[528,256]{1,0:T(8,128)(2,1)S(1)}, bf16[528,256]{1,0:T(8,128)(2,1)S(1)}, u32[]{:S(2)}, u32[]{:S(2)}) collective-permute-start(bf16[528,256]{1,0:T(8,128)(2,1)S(1)} %pad_maximum_fusion.rest_0_), channel_id=1, source_target_pairs={{0,2},{1,3},{2,0},{3,1},{4,6},{5,7},{6,4},{7,5},{8,10},{9,11},{10,... | collective-permute-start | bytes 811016 | tf_op jit(solution)/shard_map/ppermute | solution.py:555
  8.1 13.4 %collective-permute-start.1 = (bf16[528,256]{1,0:T(8,128)(2,1)S(1)}, bf16[528,256]{1,0:T(8,128)(2,1)S(1)}, u32[]{:S(2)}, u32[]{:S(2)}) collective-permute-start(bf16[528,256]{1,0:T(8,128)(2,1)S(1)} %pad_maximum_fusion.rest_0_), channel_id=1, source_target_pairs={{0,1},{1,0},{2,3},{3,2},{4,5},{5,4},{6,7},{7,6},{8,9},{9,8},{10,11... | collective-permute-start | bytes 811016 | tf_op jit(solution)/shard_map/ppermute | solution.py:556
  18.9 2.6 %collective-permute-start.3 = (bf16[528,256]{1,0:T(8,128)(2,1)S(1)}, bf16[528,256]{1,0:T(8,128)(2,1)S(1)}, u32[]{:S(2)}, u32[]{:S(2)}) collective-permute-start(bf16[528,256]{1,0:T(8,128)(2,1)S(1)} %collective-permute-done.rest_4_), channel_id=1, source_target_pairs={{0,1},{1,0},{2,3},{3,2},{4,5},{5,4},{6,7},{7,6},{8,9},{9,8},{10,11... | collective-permute-start | bytes 811016 | tf_op jit(solution)/shard_map/ppermute | solution.py:561
  18.9 5.2 %collective-permute-start.4 = (bf16[528,256]{1,0:T(8,128)(2,1)S(1)}, bf16[528,256]{1,0:T(8,128)(2,1)S(1)}, u32[]{:S(2)}, u32[]{:S(2)}) collective-permute-start(bf16[528,256]{1,0:T(8,128)(2,1)S(1)} %pad_maximum_fusion.rest_0_), channel_id=1, source_target_pairs={{2,4},{3,5},{4,2},{5,3},{10,12},{11,13},{12,10},{13,11},{18,20},{1... | collective-permute-start | bytes 811016 | tf_op jit(solution)/shard_map/ppermute | solution.py:560
  19.5 10.8 %collective-permute-start.5 = (bf16[528,256]{1,0:T(8,128)(2,1)S(1)}, bf16[528,256]{1,0:T(8,128)(2,1)S(1)}, u32[]{:S(2)}, u32[]{:S(2)}) collective-permute-start(bf16[528,256]{1,0:T(8,128)(2,1)S(1)} %collective-permute-done.rest_4_), channel_id=1, source_target_pairs={{4,6},{5,7},{2,0},{3,1},{12,14},{13,15},{10,8},{11,9},{20,22},{21,... | collective-permute-start | bytes 811016 | tf_op jit(solution)/shard_map/ppermute | solution.py:559
  20.8 10.0 %collective-permute-start.8 = (bf16[528,256]{1,0:T(8,128)(2,1)S(1)}, bf16[528,256]{1,0:T(8,128)(2,1)S(1)}, u32[]{:S(2)}, u32[]{:S(2)}) collective-permute-start(bf16[528,256]{1,0:T(8,128)(2,1)S(1)} %collective-permute-done.2.rest_2_), channel_id=1, source_target_pairs={{0,1},{1,0},{2,3},{3,2},{4,5},{5,4},{6,7},{7,6},{8,9},{9,8},{10,11... | collective-permute-start | bytes 811016 | tf_op jit(solution)/shard_map/ppermute | solution.py:565
  30.3 2.1 %collective-permute-start.6 = (bf16[528,256]{1,0:T(8,128)(2,1)S(1)}, bf16[528,256]{1,0:T(8,128)(2,1)S(1)}, u32[]{:S(2)}, u32[]{:S(2)}) collective-permute-start(bf16[528,256]{1,0:T(8,128)(2,1)S(1)} %collective-permute-done.4.rest_1_), channel_id=1, source_target_pairs={{0,1},{1,0},{2,3},{3,2},{4,5},{5,4},{6,7},{7,6},{8,9},{9,8},{10,11... | collective-permute-start | bytes 811016 | tf_op jit(solution)/shard_map/ppermute | solution.py:564
  30.3 2.1 %collective-permute-start.7 = (bf16[528,256]{1,0:T(8,128)(2,1)S(1)}, bf16[528,256]{1,0:T(8,128)(2,1)S(1)}, u32[]{:S(2)}, u32[]{:S(2)}) collective-permute-start(bf16[528,256]{1,0:T(8,128)(2,1)S(1)} %collective-permute-done.5.rest_2_), channel_id=1, source_target_pairs={{0,1},{1,0},{2,3},{3,2},{4,5},{5,4},{6,7},{7,6},{8,9},{9,8},{10,11... | collective-permute-start | bytes 811016 | tf_op jit(solution)/shard_map/ppermute | solution.py:564
  32.4 16.4 %copy-start = (bf16[512,256]{1,0:T(8,128)(2,1)S(1)}, bf16[512,256]{1,0:T(8,128)(2,1)}, u32[]{:S(2)}) copy-start(bf16[512,256]{1,0:T(8,128)(2,1)} %cot_ref.1) | copy-start | bytes 786436
  32.4 16.4 %copy-start.1 = (bf16[256,256]{1,0:T(8,128)(2,1)S(1)}, bf16[256,256]{1,0:T(8,128)(2,1)}, u32[]{:S(2)}) copy-start(bf16[256,256]{1,0:T(8,128)(2,1)} %weight_ref.1) | copy-start | bytes 393220
  32.5 16.4 %copy-start.3 = (f32[256]{0:T(256)S(1)}, f32[256]{0:T(256)}, u32[]{:S(2)}) copy-start(f32[256]{0:T(256)} %param.11) | copy-start | bytes 3076
  33.7 13.9 %collective-permute-start.10 = (bf16[512,256]{1,0:T(8,128)(2,1)S(1)}, bf16[512,256]{1,0:T(8,128)(2,1)S(1)}, u32[]{:S(2)}, u32[]{:S(2)}) collective-permute-start(bf16[512,256]{1,0:T(8,128)(2,1)S(1)} %get-tuple-element.66), channel_id=1, source_target_pairs={{0,16},{8,24},{16,0},{24,8},{1,17},{9,25},{17,1},{25,9},{2,18},{10... | collective-permute-start | bytes 786440 | tf_op jit(solution)/shard_map/ppermute | solution.py:575
  35.4 12.3 %collective-permute-start.11 = (bf16[512,256]{1,0:T(8,128)(2,1)S(1)}, bf16[512,256]{1,0:T(8,128)(2,1)S(1)}, u32[]{:S(2)}, u32[]{:S(2)}) collective-permute-start(bf16[512,256]{1,0:T(8,128)(2,1)S(1)} %get-tuple-element.67), channel_id=1, source_target_pairs={{0,24},{8,16},{16,8},{24,0},{1,25},{9,17},{17,9},{25,1},{2,26},{10... | collective-permute-start | bytes 786440 | tf_op jit(solution)/shard_map/ppermute | solution.py:575
  36.8 12.1 %collective-permute-start.9 = (bf16[512,256]{1,0:T(8,128)(2,1)S(1)}, bf16[512,256]{1,0:T(8,128)(2,1)S(1)}, u32[]{:S(2)}, u32[]{:S(2)}) collective-permute-start(bf16[512,256]{1,0:T(8,128)(2,1)S(1)} %get-tuple-element.65), channel_id=1, source_target_pairs={{0,8},{8,0},{16,24},{24,16},{1,9},{9,1},{17,25},{25,17},{2,10},{10... | collective-permute-start | bytes 786440 | tf_op jit(solution)/shard_map/ppermute | solution.py:575
  51.0 2.5 %collective-permute-start.15 = (f32[136,256]{1,0:T(8,128)S(1)}, f32[136,256]{1,0:T(8,128)S(1)}, u32[]{:S(2)}, u32[]{:S(2)}) collective-permute-start(f32[136,256]{1,0:T(8,128)S(1)} %get-tuple-element.73), channel_id=1, source_target_pairs={{0,1},{1,0},{2,3},{3,2},{4,5},{5,4},{6,7},{7,6},{8,9},{9,8},{10,11... | collective-permute-start | bytes 417800 | tf_op jit(solution)/shard_map/ppermute | solution.py:664
  51.0 10.0 %collective-permute-start.14 = (bf16[512,256]{1,0:T(8,128)(2,1)S(1)}, bf16[512,256]{1,0:T(8,128)(2,1)S(1)}, u32[]{:S(2)}, u32[]{:S(2)}) collective-permute-start(bf16[512,256]{1,0:T(8,128)(2,1)S(1)} %get-tuple-element.71.back_ref), channel_id=1, source_target_pairs={{0,24},{8,16},{16,8},{24,0},{1,25},{9,17},{17,9},{25,1},{2,26},{10... | collective-permute-start | bytes 786440 | tf_op jit(solution)/shard_map/ppermute | solution.py:575
  53.5 9.8 %collective-permute-start.16 = (f32[136,256]{1,0:T(8,128)S(1)}, f32[136,256]{1,0:T(8,128)S(1)}, u32[]{:S(2)}, u32[]{:S(2)}) collective-permute-start(f32[136,256]{1,0:T(8,128)S(1)} %add.26), channel_id=1, source_target_pairs={{0,4},{1,5},{2,6},{3,7},{4,0},{5,1},{6,2},{7,3},{8,12},{9,13},{10,... | collective-permute-start | bytes 417800 | tf_op jit(solution)/shard_map/ppermute | solution.py:584
  55.0 13.4 %collective-permute-start.12 = (bf16[512,256]{1,0:T(8,128)(2,1)S(1)}, bf16[512,256]{1,0:T(8,128)(2,1)S(1)}, u32[]{:S(2)}, u32[]{:S(2)}) collective-permute-start(bf16[512,256]{1,0:T(8,128)(2,1)S(1)} %get-tuple-element.71.back_ref), channel_id=1, source_target_pairs={{0,8},{8,0},{16,24},{24,16},{1,9},{9,1},{17,25},{25,17},{2,10},{10... | collective-permute-start | bytes 786440 | tf_op jit(solution)/shard_map/ppermute | solution.py:575
  55.5 12.9 %collective-permute-start.13 = (bf16[512,256]{1,0:T(8,128)(2,1)S(1)}, bf16[512,256]{1,0:T(8,128)(2,1)S(1)}, u32[]{:S(2)}, u32[]{:S(2)}) collective-permute-start(bf16[512,256]{1,0:T(8,128)(2,1)S(1)} %get-tuple-element.71.back_ref), channel_id=1, source_target_pairs={{0,16},{8,24},{16,0},{24,8},{1,17},{9,25},{17,1},{25,9},{2,18},{10... | collective-permute-start | bytes 786440 | tf_op jit(solution)/shard_map/ppermute | solution.py:575
  63.3 5.1 %collective-permute-start.17 = (f32[136,256]{1,0:T(8,128)S(1)}, f32[136,256]{1,0:T(8,128)S(1)}, u32[]{:S(2)}, u32[]{:S(2)}) collective-permute-start(f32[136,256]{1,0:T(8,128)S(1)} %add.27), channel_id=1, source_target_pairs={{0,2},{1,3},{2,0},{3,1},{4,6},{5,7},{6,4},{7,5},{8,10},{9,11},{10,... | collective-permute-start | bytes 417800 | tf_op jit(solution)/shard_map/ppermute | solution.py:543
  69.5 2.6 %collective-permute-start.18 = (bf16[512,256]{1,0:T(8,128)(2,1)S(1)}, bf16[512,256]{1,0:T(8,128)(2,1)S(1)}, u32[]{:S(2)}, u32[]{:S(2)}) collective-permute-start(bf16[512,256]{1,0:T(8,128)(2,1)S(1)} %get-tuple-element.79), channel_id=1, source_target_pairs={{0,1},{1,0},{2,3},{3,2},{4,5},{5,4},{6,7},{7,6},{8,9},{9,8},{10,11... | collective-permute-start | bytes 786440 | tf_op jit(solution)/shard_map/ppermute | solution.py:590
  72.0 3.9 %collective-permute-start.19 = (bf16[512,256]{1,0:T(8,128)(2,1)S(1)}, bf16[512,256]{1,0:T(8,128)(2,1)S(1)}, u32[]{:S(2)}, u32[]{:S(2)}) collective-permute-start(bf16[512,256]{1,0:T(8,128)(2,1)S(1)} %get-tuple-element.88), channel_id=1, source_target_pairs={{0,1},{1,0},{2,3},{3,2},{4,5},{5,4},{6,7},{7,6},{8,9},{9,8},{10,11... | collective-permute-start | bytes 786440 | tf_op jit(solution)/shard_map/ppermute | solution.py:599
  72.6 4.0 %collective-permute-start.20 = (bf16[512,256]{1,0:T(8,128)(2,1)S(1)}, bf16[512,256]{1,0:T(8,128)(2,1)S(1)}, u32[]{:S(2)}, u32[]{:S(2)}) collective-permute-start(bf16[512,256]{1,0:T(8,128)(2,1)S(1)} %get-tuple-element.89), channel_id=1, source_target_pairs={{0,1},{1,0},{2,3},{3,2},{4,5},{5,4},{6,7},{7,6},{8,9},{9,8},{10,11... | collective-permute-start | bytes 786440 | tf_op jit(solution)/shard_map/ppermute | solution.py:599
  72.7 3.9 %collective-permute-start.21 = (bf16[512,256]{1,0:T(8,128)(2,1)S(1)}, bf16[512,256]{1,0:T(8,128)(2,1)S(1)}, u32[]{:S(2)}, u32[]{:S(2)}) collective-permute-start(bf16[512,256]{1,0:T(8,128)(2,1)S(1)} %get-tuple-element.90), channel_id=1, source_target_pairs={{0,1},{1,0},{2,3},{3,2},{4,5},{5,4},{6,7},{7,6},{8,9},{9,8},{10,11... | collective-permute-start | bytes 786440 | tf_op jit(solution)/shard_map/ppermute | solution.py:599
  73.2 8.9 %collective-permute-start.22 = (bf16[512,256]{1,0:T(8,128)(2,1)S(1)}, bf16[512,256]{1,0:T(8,128)(2,1)S(1)}, u32[]{:S(2)}, u32[]{:S(2)}) collective-permute-start(bf16[512,256]{1,0:T(8,128)(2,1)S(1)} %pair_sums.3), channel_id=1, source_target_pairs={{6,4},{7,5},{0,2},{1,3},{14,12},{15,13},{8,10},{9,11},{22,20},{23,... | collective-permute-start | bytes 786440 | tf_op jit(solution)/shard_map/ppermute | solution.py:597
  75.3 6.7 %collective-permute-start.23 = (bf16[512,256]{1,0:T(8,128)(2,1)S(1)}, bf16[512,256]{1,0:T(8,128)(2,1)S(1)}, u32[]{:S(2)}, u32[]{:S(2)}) collective-permute-start(bf16[512,256]{1,0:T(8,128)(2,1)S(1)} %pair_sums.3), channel_id=1, source_target_pairs={{2,4},{3,5},{4,2},{5,3},{10,12},{11,13},{12,10},{13,11},{18,20},{1... | collective-permute-start | bytes 786440 | tf_op jit(solution)/shard_map/ppermute | solution.py:598
  76.0 5.4 %collective-permute-start.24 = (f32[136,256]{1,0:T(8,128)S(1)}, f32[136,256]{1,0:T(8,128)S(1)}, u32[]{:S(2)}, u32[]{:S(2)}) collective-permute-start(f32[136,256]{1,0:T(8,128)S(1)} %add.28), channel_id=1, source_target_pairs={{0,8},{8,0},{16,24},{24,16},{1,9},{9,1},{17,25},{25,17},{2,10},{10... | collective-permute-start | bytes 417800 | tf_op jit(solution)/shard_map/ppermute | solution.py:591
  81.5 5.1 %collective-permute-start.25 = (f32[136,256]{1,0:T(8,128)S(1)}, f32[136,256]{1,0:T(8,128)S(1)}, u32[]{:S(2)}, u32[]{:S(2)}) collective-permute-start(f32[136,256]{1,0:T(8,128)S(1)} %add.29), channel_id=1, source_target_pairs={{0,16},{8,24},{16,0},{24,8},{1,17},{9,25},{17,1},{25,9},{2,18},{10... | collective-permute-start | bytes 417800 | tf_op jit(solution)/shard_map/ppermute | solution.py:543
  82.1 15.8 %collective-permute-start.27 = (bf16[512,256]{1,0:T(8,128)(2,1)S(1)}, bf16[512,256]{1,0:T(8,128)(2,1)S(1)}, u32[]{:S(2)}, u32[]{:S(2)}) collective-permute-start(bf16[512,256]{1,0:T(8,128)(2,1)S(1)} %add_convert_fusion), channel_id=1, source_target_pairs={{0,4},{1,5},{4,0},{5,1},{2,6},{3,7},{6,2},{7,3},{8,12},{9,13},{12,... | collective-permute-start | bytes 786440 | tf_op jit(solution)/shard_map/ppermute | solution.py:608
  86.6 11.5 %collective-permute-start.26 = (bf16[512,256]{1,0:T(8,128)(2,1)S(1)}, bf16[512,256]{1,0:T(8,128)(2,1)S(1)}, u32[]{:S(2)}, u32[]{:S(2)}) collective-permute-start(bf16[512,256]{1,0:T(8,128)(2,1)S(1)} %get-tuple-element.101), channel_id=1, source_target_pairs={{0,2},{1,3},{2,0},{3,1},{4,6},{5,7},{6,4},{7,5},{8,10},{9,11},{10,... | collective-permute-start | bytes 786440 | tf_op jit(solution)/shard_map/ppermute | solution.py:610
  89.4 1.4 %collective-permute-start.28 = (f32[136,256]{1,0:T(8,128)S(1)}, f32[136,256]{1,0:T(8,128)S(1)}, u32[]{:S(2)}, u32[]{:S(2)}) collective-permute-start(f32[136,256]{1,0:T(8,128)S(1)} %add.30.mine_ref), channel_id=1, source_target_pairs={{0,1},{1,0},{2,3},{3,2},{4,5},{5,4},{6,7},{7,6},{8,9},{9,8},{10,11... | collective-permute-start | bytes 417800 | tf_op jit(solution)/shard_map/ppermute | solution.py:685
  (2 other events, 1.4 us)

commit v6 on v5

--- a/solution.py
+++ b/solution.py
@@ -598,16 +598,16 @@
     middle = lax.ppermute(last, "col", LINE_MIDDLE)
     got = [lax.ppermute(give, "col", CORE) for give in (give0, give1, give2)]
     own, near, far = pair_sums([keep0, keep1, keep2], got, 0)
+    from_near = lax.ppermute(near, "col", LINE_SWAP1)
     sums = sums + after(received, own)
     step = 2
     while step < rows:
         sums = exchange_add(sums, "row", rows, step)
         step *= 2
-    passed, middle = lax.optimization_barrier((passed, middle))
     far = (far.astype(F32) + passed.astype(F32)).astype(BF16)
     from_far = lax.ppermute(far, "col", LINE_SWAP2)
-    near, sums = lax.optimization_barrier((near, sums))
-    from_near = lax.ppermute(after(near, far), "col", LINE_SWAP1)
+    middle, sums = lax.optimization_barrier((middle, sums))
+    sums = after(sums, from_near)
     return [own, middle, from_near, from_far], sums
 
 

time: 99.2 us -> 97.8 us (0.986)
  starting transfers between devices: 30.6 us -> 27.5 us
  waiting for transfers between devices: 43.9 us -> 45.5 us
    ppermute x1, waiting for transfers between devices: 0.11 us -> 7.16 us  [line_reduce(): from_near = lax.ppermute(near, 'col', LINE_SWAP1)]
    ppermute x1, waiting for transfers between devices: 5.96 us -> 0.89 us  [line_reduce(): from_far = lax.ppermute(far, 'col', LINE_SWAP2)]
    ppermute x1, starting transfers between devices: 2.77 us -> 0.01 us  [line_reduce(): from_near = lax.ppermute(near, 'col', LINE_SWAP1)]
where the time goes in v6:
time: 97.8 us; the launch traced here: 97.4 us
  waiting for transfers between devices  45.5 us (47%)
  starting transfers between devices  27.5 us (28%)
  Pallas kernels  20.2 us (21%)
  other arithmetic  1.98 us (2%)
  local copies, waits for them, and re-layouts  1.37 us (1%)
    ppermute x6, waiting for transfers between devices, row_exchange(): lax.ppermute(arrays[step - 1], 'row', xor_pairs(rows, step))  15.7 us
    ppermute x6, starting transfers between devices, row_exchange(): lax.ppermute(arrays[step - 1], 'row', xor_pairs(rows, step))  7.96 us
    ppermute x1, waiting for transfers between devices, line_reduce(): from_near = lax.ppermute(near, 'col', LINE_SWAP1)  7.16 us
    ppermute x1, waiting for transfers between devices, line_exchange(): ends = lax.ppermute(far, 'col', LINE_OUT)  6.3 us
    pallas_call x1, Pallas kernels, densify(): pl.pallas_call(functools.partial(densify_kernel, capacity // TILE, target...  6.07 us
    pallas_call x3, Pallas kernels, forward_part(): pl.pallas_call(functools.partial(forward_part_kernel, tuple((len(group) f...  5.43 us
    ppermute x2, waiting for transfers between devices, exchange_add(): return value + lax.ppermute(value, axis, xor_pairs(size, step))  4.25 us
    ppermute x1, starting transfers between devices, line_exchange(): far = lax.ppermute(piece, 'col', LINE_SWAP2)  4.1 us
  transfers between devices with their start and end apart: 29, of which 12 were waited for; matrix products, arithmetic and copies ran while one was open for 0% of the time, Pallas kernels for 15%

profile of v6, /device:TPU:0, one launch (start us, length us, event | category | flops | bytes accessed | tf_op | source)
XLA Modules:
  0.0 97.4 jit_solution(11817217684891362603)
XLA Ops:
  1.4 1.0 pad_maximum_fusion.rest_0_
  2.4 4.1 %collective-permute-start = (bf16[528,256]{1,0:T(8,128)(2,1)S(1)}, bf16[528,256]{1,0:T(8,128)(2,1)S(1)}, u32[]{:S(2)}, u32[]{:S(2)}) collective-permute-start(bf16[528,256]{1,0:T(8,128)(2,1)S(1)} %pad_maximum_fusion.rest_0_), channel_id=1, source_target_pairs={{0,4},{1,5},{4,0},{5,1},{2,6},{3,7},{6,2},{7,3},{8,12},{9,13},{12,... | collective-permute-start | bytes 811016 | tf_op jit(solution)/shard_map/ppermute | solution.py:554
  6.5 1.6 %collective-permute-start.2 = (bf16[528,256]{1,0:T(8,128)(2,1)S(1)}, bf16[528,256]{1,0:T(8,128)(2,1)S(1)}, u32[]{:S(2)}, u32[]{:S(2)}) collective-permute-start(bf16[528,256]{1,0:T(8,128)(2,1)S(1)} %pad_maximum_fusion.rest_0_), channel_id=1, source_target_pairs={{0,2},{1,3},{2,0},{3,1},{4,6},{5,7},{6,4},{7,5},{8,10},{9,11},{10,... | collective-permute-start | bytes 811016 | tf_op jit(solution)/shard_map/ppermute | solution.py:555
  9.5 6.1 %densify.1.dense_ref = bf16[2048,2048]{1,0:T(8,128)(2,1)S(1)} custom-call(s32[16,16]{1,0:T(8,128)S(1)} %bitcast.34, s32[16]{0:T(128)S(1)} %bitcast.36, s32[2]{0:T(128)S(1)} %pad_add_fusion.pos_ref, bf16[16,16,128,128]{3,2,1,0:T(8,128)(2,1)} %bitcast.37), custom_call_target="tpu_custom_call" | custom-call | bytes 16777216 | tf_op jit(solution)/shard_map/densify/pallas_call | solution.py:64
  15.6 3.3 %collective-permute-done.rest_4_ = bf16[528,256]{1,0:T(8,128)(2,1)S(1)} collective-permute-done((bf16[528,256]{1,0:T(8,128)(2,1)S(1)}, bf16[528,256]{1,0:T(8,128)(2,1)S(1)}, u32[]{:S(2)}, u32[]{:S(2)}) %collective-permute-start) | collective-permute-done | bytes 270368 | tf_op jit(solution)/shard_map/ppermute | solution.py:554
  19.5 1.3 %collective-permute-start.5 = (bf16[528,256]{1,0:T(8,128)(2,1)S(1)}, bf16[528,256]{1,0:T(8,128)(2,1)S(1)}, u32[]{:S(2)}, u32[]{:S(2)}) collective-permute-start(bf16[528,256]{1,0:T(8,128)(2,1)S(1)} %collective-permute-done.rest_4_), channel_id=1, source_target_pairs={{4,6},{5,7},{2,0},{3,1},{12,14},{13,15},{10,8},{11,9},{20,22},{21,... | collective-permute-start | bytes 811016 | tf_op jit(solution)/shard_map/ppermute | solution.py:559
  21.4 2.6 %forward_part.2 = (f32[2048,256]{1,0:T(8,128)S(1)}, bf16[5,512,256]{2,1,0:T(8,128)(2,1)S(1)}) custom-call(s32[2]{0:T(128)S(1)} %pad_add_fusion.pos_ref, bf16[2048,2048]{1,0:T(8,128)(2,1)S(1)} %densify.1.dense_ref, bf16[528,256]{1,0:T(8,128)(2,1)S(1)} %pad_maximum_fusion.rest_0_, bf16[528,256]{1,0:T(8,128)(2,1)S(1)} %collective-permute-done.1.rest_1_, ...), custom_call_target="tpu_custom_call" | custom-call | flops 1342177280 | bytes 5242880 | tf_op jit(solution)/shard_map/forward_part/pallas_call | solution.py:210
  24.0 6.3 %collective-permute-done.5.rest_2_ = bf16[528,256]{1,0:T(8,128)(2,1)S(1)} collective-permute-done((bf16[528,256]{1,0:T(8,128)(2,1)S(1)}, bf16[528,256]{1,0:T(8,128)(2,1)S(1)}, u32[]{:S(2)}, u32[]{:S(2)}) %collective-permute-start.5) | collective-permute-done | bytes 270368 | tf_op jit(solution)/shard_map/ppermute | solution.py:559
  30.8 1.6 %forward_part.3 = (f32[2048,256]{1,0:T(8,128)S(1)}, bf16[2,512,256]{2,1,0:T(8,128)(2,1)S(1)}) custom-call(s32[2]{0:T(128)S(1)} %pad_add_fusion.pos_ref, bf16[2048,2048]{1,0:T(8,128)(2,1)S(1)} %densify.1.dense_ref, bf16[528,256]{1,0:T(8,128)(2,1)S(1)} %collective-permute-done.8.rest_0_, bf16[528,256]{1,0:T(8,128)(2,1)S(1)} %collective-permute-done.4.rest_1_, ...), custom_call_target="tpu_custom_call" | custom-call | flops 536870912 | bytes 2097152 | tf_op jit(solution)/shard_map/forward_part/pallas_call | solution.py:210
  32.5 1.3 %forward_last.1 = (f32[512,256]{1,0:T(8,128)S(1)}, bf16[512,256]{1,0:T(8,128)(2,1)S(1)}, bf16[512,256]{1,0:T(8,128)(2,1)S(1)}, bf16[512,256]{1,0:T(8,128)(2,1)S(1)}, bf16[1,512,256]{2,1,0:T(8,128)(2,1)S(1)}) custom-call(s32[2]{0:T(128)S(1)} %pad_add_fusion.pos_ref, bf16[2048,2048]{1,0:T(8,128)(2,1)S(1)} %densify.1.dense_ref, ...), custom_call_target="tpu_custom_call" | custom-call | flops 268435456 | bytes 1048576 | tf_op jit(solution)/shard_map/forward_last/pallas_call | solution.py:210
  33.7 1.6 %collective-permute-start.10 = (bf16[512,256]{1,0:T(8,128)(2,1)S(1)}, bf16[512,256]{1,0:T(8,128)(2,1)S(1)}, u32[]{:S(2)}, u32[]{:S(2)}) collective-permute-start(bf16[512,256]{1,0:T(8,128)(2,1)S(1)} %get-tuple-element.64), channel_id=1, source_target_pairs={{0,16},{8,24},{16,0},{24,8},{1,17},{9,25},{17,1},{25,9},{2,18},{10... | collective-permute-start | bytes 786440 | tf_op jit(solution)/shard_map/ppermute | solution.py:575
  35.4 1.4 %collective-permute-start.11 = (bf16[512,256]{1,0:T(8,128)(2,1)S(1)}, bf16[512,256]{1,0:T(8,128)(2,1)S(1)}, u32[]{:S(2)}, u32[]{:S(2)}) collective-permute-start(bf16[512,256]{1,0:T(8,128)(2,1)S(1)} %get-tuple-element.65), channel_id=1, source_target_pairs={{0,24},{8,16},{16,8},{24,0},{1,25},{9,17},{17,9},{25,1},{2,26},{10... | collective-permute-start | bytes 786440 | tf_op jit(solution)/shard_map/ppermute | solution.py:575
  37.3 10.3 %collective-permute-done.10.rest_2_ = bf16[512,256]{1,0:T(8,128)(2,1)S(1)} collective-permute-done((bf16[512,256]{1,0:T(8,128)(2,1)S(1)}, bf16[512,256]{1,0:T(8,128)(2,1)S(1)}, u32[]{:S(2)}, u32[]{:S(2)}) %collective-permute-start.10) | collective-permute-done | bytes 262176 | tf_op jit(solution)/shard_map/ppermute | solution.py:575
  47.6 1.2 %collective-permute-done.9.rest_1_ = bf16[512,256]{1,0:T(8,128)(2,1)S(1)} collective-permute-done((bf16[512,256]{1,0:T(8,128)(2,1)S(1)}, bf16[512,256]{1,0:T(8,128)(2,1)S(1)}, u32[]{:S(2)}, u32[]{:S(2)}) %collective-permute-start.9) | collective-permute-done | bytes 262176 | tf_op jit(solution)/shard_map/ppermute | solution.py:575
  48.9 2.1 %layer.1 = (bf16[512,256]{1,0:T(8,128)(2,1)}, bf16[512,256]{1,0:T(8,128)(2,1)S(1)}, f32[136,256]{1,0:T(8,128)S(1)}, f32[136,256]{1,0:T(8,128)S(1)}) custom-call(s32[2]{0:T(128)S(1)} %pad_add_fusion.pos_ref, bf16[256,256]{1,0:T(8,128)(2,1)S(1)} %copy-done.1, f32[1,256]{1,0:T(1,128)S(1)} %bitcast.35, bf16[512,256]{1,0:T(8,128)(2,1)S(1)} %copy-done, ...), custom_call_target="tpu_custom_call" | custom-call | flops 201326592 | bytes 2621440 | tf_op jit(solution)/shard_map/layer/pallas_call | solution.py:314
  51.0 2.5 %collective-permute-start.14 = (bf16[512,256]{1,0:T(8,128)(2,1)S(1)}, bf16[512,256]{1,0:T(8,128)(2,1)S(1)}, u32[]{:S(2)}, u32[]{:S(2)}) collective-permute-start(bf16[512,256]{1,0:T(8,128)(2,1)S(1)} %get-tuple-element.69.back_ref), channel_id=1, source_target_pairs={{0,24},{8,16},{16,8},{24,0},{1,25},{9,17},{17,9},{25,1},{2,26},{10... | collective-permute-start | bytes 786440 | tf_op jit(solution)/shard_map/ppermute | solution.py:575
  53.5 1.5 %collective-permute-start.16 = (f32[136,256]{1,0:T(8,128)S(1)}, f32[136,256]{1,0:T(8,128)S(1)}, u32[]{:S(2)}, u32[]{:S(2)}) collective-permute-start(f32[136,256]{1,0:T(8,128)S(1)} %add.26), channel_id=1, source_target_pairs={{0,4},{1,5},{2,6},{3,7},{4,0},{5,1},{6,2},{7,3},{8,12},{9,13},{10,... | collective-permute-start | bytes 417800 | tf_op jit(solution)/shard_map/ppermute | solution.py:584
  55.5 1.4 %collective-permute-start.13 = (bf16[512,256]{1,0:T(8,128)(2,1)S(1)}, bf16[512,256]{1,0:T(8,128)(2,1)S(1)}, u32[]{:S(2)}, u32[]{:S(2)}) collective-permute-start(bf16[512,256]{1,0:T(8,128)(2,1)S(1)} %get-tuple-element.69.back_ref), channel_id=1, source_target_pairs={{0,16},{8,24},{16,0},{24,8},{1,17},{9,25},{17,1},{25,9},{2,18},{10... | collective-permute-start | bytes 786440 | tf_op jit(solution)/shard_map/ppermute | solution.py:575
  56.9 4.1 %collective-permute-done.14.rest_5_ = bf16[512,256]{1,0:T(8,128)(2,1)S(1)} collective-permute-done((bf16[512,256]{1,0:T(8,128)(2,1)S(1)}, bf16[512,256]{1,0:T(8,128)(2,1)S(1)}, u32[]{:S(2)}, u32[]{:S(2)}) %collective-permute-start.14) | collective-permute-done | bytes 262176 | tf_op jit(solution)/shard_map/ppermute | solution.py:575
  61.0 2.2 %collective-permute-done.16 = f32[136,256]{1,0:T(8,128)S(1)} collective-permute-done((f32[136,256]{1,0:T(8,128)S(1)}, f32[136,256]{1,0:T(8,128)S(1)}, u32[]{:S(2)}, u32[]{:S(2)}) %collective-permute-start.16) | collective-permute-done | bytes 139296 | tf_op jit(solution)/shard_map/ppermute | solution.py:584
  63.3 0.8 backward_early.1.rest_2_
  64.1 4.2 %collective-permute-done.17 = f32[136,256]{1,0:T(8,128)S(1)} collective-permute-done((f32[136,256]{1,0:T(8,128)S(1)}, f32[136,256]{1,0:T(8,128)S(1)}, u32[]{:S(2)}, u32[]{:S(2)}) %collective-permute-start.17) | collective-permute-done | bytes 139296 | tf_op jit(solution)/shard_map/ppermute | solution.py:543
  68.4 1.0 %backward_late.2 = (f32[512,256]{1,0:T(8,128)S(1)}, bf16[512,256]{1,0:T(8,128)(2,1)S(1)}) custom-call(bf16[2048,2048]{1,0:T(8,128)(2,1)S(1)} %densify.1.dense_ref, bf16[2,512,256]{2,1,0:T(8,128)(2,1)S(1)} %get-tuple-element.67.rest_0_.rest_1_, bf16[1,512,256]{2,1,0:T(8,128)(2,1)S(1)} %get-tuple-element.68.rest_1_, f32[2048,256]{1,0:T(8,128)S(1)} %backward_early.1.rest_2_, ...), custom_call_target="tpu_custom_call" | custom-call | flops 536870912 | bytes 2097152 | tf_op jit(solution)/shard_map/backward_late/pallas_call | solution.py:409
  69.5 2.5 %backward_late.3 = (f32[512,256]{1,0:T(8,128)S(1)}, bf16[512,256]{1,0:T(8,128)(2,1)S(1)}, f32[512,256]{1,0:T(8,128)S(1)}, bf16[512,256]{1,0:T(8,128)(2,1)S(1)}, ...) custom-call(bf16[2048,2048]{1,0:T(8,128)(2,1)S(1)} %densify.1.dense_ref, ...), custom_call_target="tpu_custom_call" | custom-call | flops 1610612736 | bytes 6291456 | tf_op jit(solution)/shard_map/backward_late/pallas_call | solution.py:409
  73.2 2.1 %collective-permute-start.26 = (bf16[512,256]{1,0:T(8,128)(2,1)S(1)}, bf16[512,256]{1,0:T(8,128)(2,1)S(1)}, u32[]{:S(2)}, u32[]{:S(2)}) collective-permute-start(bf16[512,256]{1,0:T(8,128)(2,1)S(1)} %pair_sums.3), channel_id=1, source_target_pairs={{6,4},{7,5},{0,2},{1,3},{14,12},{15,13},{8,10},{9,11},{22,20},{23,... | collective-permute-start | bytes 786440 | tf_op jit(solution)/shard_map/ppermute | solution.py:597
  76.7 4.0 %collective-permute-done.23 = f32[136,256]{1,0:T(8,128)S(1)} collective-permute-done((f32[136,256]{1,0:T(8,128)S(1)}, f32[136,256]{1,0:T(8,128)S(1)}, u32[]{:S(2)}, u32[]{:S(2)}) %collective-permute-start.23) | collective-permute-done | bytes 139296 | tf_op jit(solution)/shard_map/ppermute | solution.py:591
  81.8 4.1 %collective-permute-start.27 = (bf16[512,256]{1,0:T(8,128)(2,1)S(1)}, bf16[512,256]{1,0:T(8,128)(2,1)S(1)}, u32[]{:S(2)}, u32[]{:S(2)}) collective-permute-start(bf16[512,256]{1,0:T(8,128)(2,1)S(1)} %add_convert_fusion), channel_id=1, source_target_pairs={{0,4},{1,5},{4,0},{5,1},{2,6},{3,7},{6,2},{7,3},{8,12},{9,13},{12,... | collective-permute-start | bytes 786440 | tf_op jit(solution)/shard_map/ppermute | solution.py:608
  85.9 7.2 %collective-permute-done.25.refs_2_ = bf16[512,256]{1,0:T(8,128)(2,1)S(1)} collective-permute-done((bf16[512,256]{1,0:T(8,128)(2,1)S(1)}, bf16[512,256]{1,0:T(8,128)(2,1)S(1)}, u32[]{:S(2)}, u32[]{:S(2)}) %collective-permute-start.25) | collective-permute-done | bytes 262176 | tf_op jit(solution)/shard_map/ppermute | solution.py:601
  93.1 1.4 %collective-permute-done.28.theirs_ref = f32[136,256]{1,0:T(8,128)S(1)} collective-permute-done((f32[136,256]{1,0:T(8,128)S(1)}, f32[136,256]{1,0:T(8,128)S(1)}, u32[]{:S(2)}, u32[]{:S(2)}) %collective-permute-start.28) | collective-permute-done | bytes 139296 | tf_op jit(solution)/shard_map/ppermute | solution.py:685
  94.4 1.3 %assemble.1 = (f32[256,256]{1,0:T(8,128)}, f32[1,256]{1,0:T(1,128)}) custom-call(s32[2]{0:T(128)S(1)} %pad_add_fusion.pos_ref, f32[136,256]{1,0:T(8,128)S(1)} %add.30.mine_ref, f32[136,256]{1,0:T(8,128)S(1)} %collective-permute-done.28.theirs_ref), custom_call_target="tpu_custom_call" | custom-call | bytes 1048576 | tf_op jit(solution)/shard_map/assemble/pallas_call | solution.py:342
  95.7 0.9 collective-permute-done.27.refs_3_
  96.6 0.8 finish.1
  (57 shorter events, 8.8 us)
Async XLA Ops:
  2.4 16.5 %collective-permute-start = (bf16[528,256]{1,0:T(8,128)(2,1)S(1)}, bf16[528,256]{1,0:T(8,128)(2,1)S(1)}, u32[]{:S(2)}, u32[]{:S(2)}) collective-permute-start(bf16[528,256]{1,0:T(8,128)(2,1)S(1)} %pad_maximum_fusion.rest_0_), channel_id=1, source_target_pairs={{0,4},{1,5},{4,0},{5,1},{2,6},{3,7},{6,2},{7,3},{8,12},{9,13},{12,... | collective-permute-start | bytes 811016 | tf_op jit(solution)/shard_map/ppermute | solution.py:554
  6.5 14.4 %collective-permute-start.2 = (bf16[528,256]{1,0:T(8,128)(2,1)S(1)}, bf16[528,256]{1,0:T(8,128)(2,1)S(1)}, u32[]{:S(2)}, u32[]{:S(2)}) collective-permute-start(bf16[528,256]{1,0:T(8,128)(2,1)S(1)} %pad_maximum_fusion.rest_0_), channel_id=1, source_target_pairs={{0,2},{1,3},{2,0},{3,1},{4,6},{5,7},{6,4},{7,5},{8,10},{9,11},{10,... | collective-permute-start | bytes 811016 | tf_op jit(solution)/shard_map/ppermute | solution.py:555
  8.1 13.4 %collective-permute-start.1 = (bf16[528,256]{1,0:T(8,128)(2,1)S(1)}, bf16[528,256]{1,0:T(8,128)(2,1)S(1)}, u32[]{:S(2)}, u32[]{:S(2)}) collective-permute-start(bf16[528,256]{1,0:T(8,128)(2,1)S(1)} %pad_maximum_fusion.rest_0_), channel_id=1, source_target_pairs={{0,1},{1,0},{2,3},{3,2},{4,5},{5,4},{6,7},{7,6},{8,9},{9,8},{10,11... | collective-permute-start | bytes 811016 | tf_op jit(solution)/shard_map/ppermute | solution.py:556
  18.9 2.6 %collective-permute-start.3 = (bf16[528,256]{1,0:T(8,128)(2,1)S(1)}, bf16[528,256]{1,0:T(8,128)(2,1)S(1)}, u32[]{:S(2)}, u32[]{:S(2)}) collective-permute-start(bf16[528,256]{1,0:T(8,128)(2,1)S(1)} %collective-permute-done.rest_4_), channel_id=1, source_target_pairs={{0,1},{1,0},{2,3},{3,2},{4,5},{5,4},{6,7},{7,6},{8,9},{9,8},{10,11... | collective-permute-start | bytes 811016 | tf_op jit(solution)/shard_map/ppermute | solution.py:561
  18.9 5.2 %collective-permute-start.4 = (bf16[528,256]{1,0:T(8,128)(2,1)S(1)}, bf16[528,256]{1,0:T(8,128)(2,1)S(1)}, u32[]{:S(2)}, u32[]{:S(2)}) collective-permute-start(bf16[528,256]{1,0:T(8,128)(2,1)S(1)} %pad_maximum_fusion.rest_0_), channel_id=1, source_target_pairs={{2,4},{3,5},{4,2},{5,3},{10,12},{11,13},{12,10},{13,11},{18,20},{1... | collective-permute-start | bytes 811016 | tf_op jit(solution)/shard_map/ppermute | solution.py:560
  19.5 10.8 %collective-permute-start.5 = (bf16[528,256]{1,0:T(8,128)(2,1)S(1)}, bf16[528,256]{1,0:T(8,128)(2,1)S(1)}, u32[]{:S(2)}, u32[]{:S(2)}) collective-permute-start(bf16[528,256]{1,0:T(8,128)(2,1)S(1)} %collective-permute-done.rest_4_), channel_id=1, source_target_pairs={{4,6},{5,7},{2,0},{3,1},{12,14},{13,15},{10,8},{11,9},{20,22},{21,... | collective-permute-start | bytes 811016 | tf_op jit(solution)/shard_map/ppermute | solution.py:559
  20.8 10.0 %collective-permute-start.8 = (bf16[528,256]{1,0:T(8,128)(2,1)S(1)}, bf16[528,256]{1,0:T(8,128)(2,1)S(1)}, u32[]{:S(2)}, u32[]{:S(2)}) collective-permute-start(bf16[528,256]{1,0:T(8,128)(2,1)S(1)} %collective-permute-done.2.rest_2_), channel_id=1, source_target_pairs={{0,1},{1,0},{2,3},{3,2},{4,5},{5,4},{6,7},{7,6},{8,9},{9,8},{10,11... | collective-permute-start | bytes 811016 | tf_op jit(solution)/shard_map/ppermute | solution.py:565
  30.3 2.1 %collective-permute-start.6 = (bf16[528,256]{1,0:T(8,128)(2,1)S(1)}, bf16[528,256]{1,0:T(8,128)(2,1)S(1)}, u32[]{:S(2)}, u32[]{:S(2)}) collective-permute-start(bf16[528,256]{1,0:T(8,128)(2,1)S(1)} %collective-permute-done.4.rest_1_), channel_id=1, source_target_pairs={{0,1},{1,0},{2,3},{3,2},{4,5},{5,4},{6,7},{7,6},{8,9},{9,8},{10,11... | collective-permute-start | bytes 811016 | tf_op jit(solution)/shard_map/ppermute | solution.py:564
  30.3 2.1 %collective-permute-start.7 = (bf16[528,256]{1,0:T(8,128)(2,1)S(1)}, bf16[528,256]{1,0:T(8,128)(2,1)S(1)}, u32[]{:S(2)}, u32[]{:S(2)}) collective-permute-start(bf16[528,256]{1,0:T(8,128)(2,1)S(1)} %collective-permute-done.5.rest_2_), channel_id=1, source_target_pairs={{0,1},{1,0},{2,3},{3,2},{4,5},{5,4},{6,7},{7,6},{8,9},{9,8},{10,11... | collective-permute-start | bytes 811016 | tf_op jit(solution)/shard_map/ppermute | solution.py:564
  32.4 16.4 %copy-start = (bf16[512,256]{1,0:T(8,128)(2,1)S(1)}, bf16[512,256]{1,0:T(8,128)(2,1)}, u32[]{:S(2)}) copy-start(bf16[512,256]{1,0:T(8,128)(2,1)} %cot_ref.1) | copy-start | bytes 786436
  32.4 16.4 %copy-start.1 = (bf16[256,256]{1,0:T(8,128)(2,1)S(1)}, bf16[256,256]{1,0:T(8,128)(2,1)}, u32[]{:S(2)}) copy-start(bf16[256,256]{1,0:T(8,128)(2,1)} %weight_ref.1) | copy-start | bytes 393220
  32.5 16.4 %copy-start.3 = (f32[256]{0:T(256)S(1)}, f32[256]{0:T(256)}, u32[]{:S(2)}) copy-start(f32[256]{0:T(256)} %param.11) | copy-start | bytes 3076
  33.7 13.9 %collective-permute-start.10 = (bf16[512,256]{1,0:T(8,128)(2,1)S(1)}, bf16[512,256]{1,0:T(8,128)(2,1)S(1)}, u32[]{:S(2)}, u32[]{:S(2)}) collective-permute-start(bf16[512,256]{1,0:T(8,128)(2,1)S(1)} %get-tuple-element.64), channel_id=1, source_target_pairs={{0,16},{8,24},{16,0},{24,8},{1,17},{9,25},{17,1},{25,9},{2,18},{10... | collective-permute-start | bytes 786440 | tf_op jit(solution)/shard_map/ppermute | solution.py:575
  35.4 12.3 %collective-permute-start.11 = (bf16[512,256]{1,0:T(8,128)(2,1)S(1)}, bf16[512,256]{1,0:T(8,128)(2,1)S(1)}, u32[]{:S(2)}, u32[]{:S(2)}) collective-permute-start(bf16[512,256]{1,0:T(8,128)(2,1)S(1)} %get-tuple-element.65), channel_id=1, source_target_pairs={{0,24},{8,16},{16,8},{24,0},{1,25},{9,17},{17,9},{25,1},{2,26},{10... | collective-permute-start | bytes 786440 | tf_op jit(solution)/shard_map/ppermute | solution.py:575
  36.8 12.1 %collective-permute-start.9 = (bf16[512,256]{1,0:T(8,128)(2,1)S(1)}, bf16[512,256]{1,0:T(8,128)(2,1)S(1)}, u32[]{:S(2)}, u32[]{:S(2)}) collective-permute-start(bf16[512,256]{1,0:T(8,128)(2,1)S(1)} %get-tuple-element.63), channel_id=1, source_target_pairs={{0,8},{8,0},{16,24},{24,16},{1,9},{9,1},{17,25},{25,17},{2,10},{10... | collective-permute-start | bytes 786440 | tf_op jit(solution)/shard_map/ppermute | solution.py:575
  51.0 2.5 %collective-permute-start.15 = (f32[136,256]{1,0:T(8,128)S(1)}, f32[136,256]{1,0:T(8,128)S(1)}, u32[]{:S(2)}, u32[]{:S(2)}) collective-permute-start(f32[136,256]{1,0:T(8,128)S(1)} %get-tuple-element.71), channel_id=1, source_target_pairs={{0,1},{1,0},{2,3},{3,2},{4,5},{5,4},{6,7},{7,6},{8,9},{9,8},{10,11... | collective-permute-start | bytes 417800 | tf_op jit(solution)/shard_map/ppermute | solution.py:664
  51.0 10.0 %collective-permute-start.14 = (bf16[512,256]{1,0:T(8,128)(2,1)S(1)}, bf16[512,256]{1,0:T(8,128)(2,1)S(1)}, u32[]{:S(2)}, u32[]{:S(2)}) collective-permute-start(bf16[512,256]{1,0:T(8,128)(2,1)S(1)} %get-tuple-element.69.back_ref), channel_id=1, source_target_pairs={{0,24},{8,16},{16,8},{24,0},{1,25},{9,17},{17,9},{25,1},{2,26},{10... | collective-permute-start | bytes 786440 | tf_op jit(solution)/shard_map/ppermute | solution.py:575
  53.5 9.8 %collective-permute-start.16 = (f32[136,256]{1,0:T(8,128)S(1)}, f32[136,256]{1,0:T(8,128)S(1)}, u32[]{:S(2)}, u32[]{:S(2)}) collective-permute-start(f32[136,256]{1,0:T(8,128)S(1)} %add.26), channel_id=1, source_target_pairs={{0,4},{1,5},{2,6},{3,7},{4,0},{5,1},{6,2},{7,3},{8,12},{9,13},{10,... | collective-permute-start | bytes 417800 | tf_op jit(solution)/shard_map/ppermute | solution.py:584
  55.0 13.4 %collective-permute-start.12 = (bf16[512,256]{1,0:T(8,128)(2,1)S(1)}, bf16[512,256]{1,0:T(8,128)(2,1)S(1)}, u32[]{:S(2)}, u32[]{:S(2)}) collective-permute-start(bf16[512,256]{1,0:T(8,128)(2,1)S(1)} %get-tuple-element.69.back_ref), channel_id=1, source_target_pairs={{0,8},{8,0},{16,24},{24,16},{1,9},{9,1},{17,25},{25,17},{2,10},{10... | collective-permute-start | bytes 786440 | tf_op jit(solution)/shard_map/ppermute | solution.py:575
  55.5 12.9 %collective-permute-start.13 = (bf16[512,256]{1,0:T(8,128)(2,1)S(1)}, bf16[512,256]{1,0:T(8,128)(2,1)S(1)}, u32[]{:S(2)}, u32[]{:S(2)}) collective-permute-start(bf16[512,256]{1,0:T(8,128)(2,1)S(1)} %get-tuple-element.69.back_ref), channel_id=1, source_target_pairs={{0,16},{8,24},{16,0},{24,8},{1,17},{9,25},{17,1},{25,9},{2,18},{10... | collective-permute-start | bytes 786440 | tf_op jit(solution)/shard_map/ppermute | solution.py:575
  63.3 5.1 %collective-permute-start.17 = (f32[136,256]{1,0:T(8,128)S(1)}, f32[136,256]{1,0:T(8,128)S(1)}, u32[]{:S(2)}, u32[]{:S(2)}) collective-permute-start(f32[136,256]{1,0:T(8,128)S(1)} %add.27), channel_id=1, source_target_pairs={{0,2},{1,3},{2,0},{3,1},{4,6},{5,7},{6,4},{7,5},{8,10},{9,11},{10,... | collective-permute-start | bytes 417800 | tf_op jit(solution)/shard_map/ppermute | solution.py:543
  69.5 2.6 %collective-permute-start.18 = (bf16[512,256]{1,0:T(8,128)(2,1)S(1)}, bf16[512,256]{1,0:T(8,128)(2,1)S(1)}, u32[]{:S(2)}, u32[]{:S(2)}) collective-permute-start(bf16[512,256]{1,0:T(8,128)(2,1)S(1)} %get-tuple-element.77), channel_id=1, source_target_pairs={{0,1},{1,0},{2,3},{3,2},{4,5},{5,4},{6,7},{7,6},{8,9},{9,8},{10,11... | collective-permute-start | bytes 786440 | tf_op jit(solution)/shard_map/ppermute | solution.py:590
  72.0 3.9 %collective-permute-start.19 = (bf16[512,256]{1,0:T(8,128)(2,1)S(1)}, bf16[512,256]{1,0:T(8,128)(2,1)S(1)}, u32[]{:S(2)}, u32[]{:S(2)}) collective-permute-start(bf16[512,256]{1,0:T(8,128)(2,1)S(1)} %get-tuple-element.86), channel_id=1, source_target_pairs={{0,1},{1,0},{2,3},{3,2},{4,5},{5,4},{6,7},{7,6},{8,9},{9,8},{10,11... | collective-permute-start | bytes 786440 | tf_op jit(solution)/shard_map/ppermute | solution.py:599
  72.6 4.0 %collective-permute-start.20 = (bf16[512,256]{1,0:T(8,128)(2,1)S(1)}, bf16[512,256]{1,0:T(8,128)(2,1)S(1)}, u32[]{:S(2)}, u32[]{:S(2)}) collective-permute-start(bf16[512,256]{1,0:T(8,128)(2,1)S(1)} %get-tuple-element.87), channel_id=1, source_target_pairs={{0,1},{1,0},{2,3},{3,2},{4,5},{5,4},{6,7},{7,6},{8,9},{9,8},{10,11... | collective-permute-start | bytes 786440 | tf_op jit(solution)/shard_map/ppermute | solution.py:599
  72.7 3.9 %collective-permute-start.21 = (bf16[512,256]{1,0:T(8,128)(2,1)S(1)}, bf16[512,256]{1,0:T(8,128)(2,1)S(1)}, u32[]{:S(2)}, u32[]{:S(2)}) collective-permute-start(bf16[512,256]{1,0:T(8,128)(2,1)S(1)} %get-tuple-element.88), channel_id=1, source_target_pairs={{0,1},{1,0},{2,3},{3,2},{4,5},{5,4},{6,7},{7,6},{8,9},{9,8},{10,11... | collective-permute-start | bytes 786440 | tf_op jit(solution)/shard_map/ppermute | solution.py:599
  73.2 8.5 %collective-permute-start.26 = (bf16[512,256]{1,0:T(8,128)(2,1)S(1)}, bf16[512,256]{1,0:T(8,128)(2,1)S(1)}, u32[]{:S(2)}, u32[]{:S(2)}) collective-permute-start(bf16[512,256]{1,0:T(8,128)(2,1)S(1)} %pair_sums.3), channel_id=1, source_target_pairs={{6,4},{7,5},{0,2},{1,3},{14,12},{15,13},{8,10},{9,11},{22,20},{23,... | collective-permute-start | bytes 786440 | tf_op jit(solution)/shard_map/ppermute | solution.py:597
  75.3 5.4 %collective-permute-start.23 = (f32[136,256]{1,0:T(8,128)S(1)}, f32[136,256]{1,0:T(8,128)S(1)}, u32[]{:S(2)}, u32[]{:S(2)}) collective-permute-start(f32[136,256]{1,0:T(8,128)S(1)} %add.28), channel_id=1, source_target_pairs={{0,8},{8,0},{16,24},{24,16},{1,9},{9,1},{17,25},{25,17},{2,10},{10... | collective-permute-start | bytes 417800 | tf_op jit(solution)/shard_map/ppermute | solution.py:591
  75.9 10.0 %collective-permute-start.22 = (bf16[512,256]{1,0:T(8,128)(2,1)S(1)}, bf16[512,256]{1,0:T(8,128)(2,1)S(1)}, u32[]{:S(2)}, u32[]{:S(2)}) collective-permute-start(bf16[512,256]{1,0:T(8,128)(2,1)S(1)} %pair_sums.3), channel_id=1, source_target_pairs={{2,4},{3,5},{4,2},{5,3},{10,12},{11,13},{12,10},{13,11},{18,20},{1... | collective-permute-start | bytes 786440 | tf_op jit(solution)/shard_map/ppermute | solution.py:598
  80.8 5.1 %collective-permute-start.24 = (f32[136,256]{1,0:T(8,128)S(1)}, f32[136,256]{1,0:T(8,128)S(1)}, u32[]{:S(2)}, u32[]{:S(2)}) collective-permute-start(f32[136,256]{1,0:T(8,128)S(1)} %add.29), channel_id=1, source_target_pairs={{0,16},{8,24},{16,0},{24,8},{1,17},{9,25},{17,1},{25,9},{2,18},{10... | collective-permute-start | bytes 417800 | tf_op jit(solution)/shard_map/ppermute | solution.py:543
  81.3 11.7 %collective-permute-start.25 = (bf16[512,256]{1,0:T(8,128)(2,1)S(1)}, bf16[512,256]{1,0:T(8,128)(2,1)S(1)}, u32[]{:S(2)}, u32[]{:S(2)}) collective-permute-start(bf16[512,256]{1,0:T(8,128)(2,1)S(1)} %get-tuple-element.95), channel_id=1, source_target_pairs={{0,2},{1,3},{2,0},{3,1},{4,6},{5,7},{6,4},{7,5},{8,10},{9,11},{10,... | collective-permute-start | bytes 786440 | tf_op jit(solution)/shard_map/ppermute | solution.py:601
  81.8 14.8 %collective-permute-start.27 = (bf16[512,256]{1,0:T(8,128)(2,1)S(1)}, bf16[512,256]{1,0:T(8,128)(2,1)S(1)}, u32[]{:S(2)}, u32[]{:S(2)}) collective-permute-start(bf16[512,256]{1,0:T(8,128)(2,1)S(1)} %add_convert_fusion), channel_id=1, source_target_pairs={{0,4},{1,5},{4,0},{5,1},{2,6},{3,7},{6,2},{7,3},{8,12},{9,13},{12,... | collective-permute-start | bytes 786440 | tf_op jit(solution)/shard_map/ppermute | solution.py:608
  93.1 1.4 %collective-permute-start.28 = (f32[136,256]{1,0:T(8,128)S(1)}, f32[136,256]{1,0:T(8,128)S(1)}, u32[]{:S(2)}, u32[]{:S(2)}) collective-permute-start(f32[136,256]{1,0:T(8,128)S(1)} %add.30.mine_ref), channel_id=1, source_target_pairs={{0,1},{1,0},{2,3},{3,2},{4,5},{5,4},{6,7},{7,6},{8,9},{9,8},{10,11... | collective-permute-start | bytes 417800 | tf_op jit(solution)/shard_map/ppermute | solution.py:685
  (2 other events, 1.4 us)

commit v7 on v6

--- a/solution.py
+++ b/solution.py
@@ -503,6 +503,23 @@
     )(*kept, *received)
 
 
+def triple_sum_kernel(first_ref, second_ref, third_ref, out_ref):
+    total = first_ref[...] + second_ref[...].astype(F32) + third_ref[...].astype(F32)
+    out_ref[...] = total.astype(BF16)
+
+
+def triple_sum(first, second, third):
+    return pl.pallas_call(
+        triple_sum_kernel,
+        out_shape=jax.ShapeDtypeStruct(first.shape, BF16),
+        compiler_params=params(),
+        cost_estimate=pl.CostEstimate(
+            flops=0, bytes_accessed=10 * first.size, transcendentals=0
+        ),
+        name="triple_sum",
+    )(first, second, third)
+
+
 def finish_kernel(chunks, each, *refs):
     out_ref = refs[-1]
     size = out_ref.shape[1] // chunks
@@ -597,14 +614,14 @@
     passed = lax.ppermute(last, "col", LINE_IN)
     middle = lax.ppermute(last, "col", LINE_MIDDLE)
     got = [lax.ppermute(give, "col", CORE) for give in (give0, give1, give2)]
-    own, near, far = pair_sums([keep0, keep1, keep2], got, 0)
+    own, near = pair_sums([keep0, keep1], got[:2], 0)
     from_near = lax.ppermute(near, "col", LINE_SWAP1)
     sums = sums + after(received, own)
     step = 2
     while step < rows:
         sums = exchange_add(sums, "row", rows, step)
         step *= 2
-    far = (far.astype(F32) + passed.astype(F32)).astype(BF16)
+    far = triple_sum(keep2, got[2], passed)
     from_far = lax.ppermute(far, "col", LINE_SWAP2)
     middle, sums = lax.optimization_barrier((middle, sums))
     sums = after(sums, from_near)

time: 97.8 us -> 98.1 us (level)
  starting transfers between devices: 27.5 us -> 30.1 us
  waiting for transfers between devices: 45.5 us -> 43.3 us
    ppermute x1, waiting for transfers between devices: 7.16 us -> 0.82 us  [line_reduce(): from_near = lax.ppermute(near, 'col', LINE_SWAP1)]
    ppermute x1, waiting for transfers between devices: 0.89 us -> 7.22 us  [line_reduce(): from_far = lax.ppermute(far, 'col', LINE_SWAP2)]
    ppermute x1, starting transfers between devices: 0.01 us -> 3.04 us  [line_reduce(): from_near = lax.ppermute(near, 'col', LINE_SWAP1)]
    ppermute x1, waiting for transfers between devices: 4 us -> 1.56 us  [line_reduce(): received = lax.ppermute(sums, 'row', xor_pairs(rows, 1))]
where the time goes in v7:
time: 98.1 us; the launch traced here: 97.8 us
  waiting for transfers between devices  43.3 us (44%)
  starting transfers between devices  30.1 us (31%)
  Pallas kernels  20.2 us (21%)
  other arithmetic  1.91 us (2%)
  local copies, waits for them, and re-layouts  1.37 us (1%)
    ppermute x6, waiting for transfers between devices, row_exchange(): lax.ppermute(arrays[step - 1], 'row', xor_pairs(rows, step))  15.7 us
    ppermute x6, starting transfers between devices, row_exchange(): lax.ppermute(arrays[step - 1], 'row', xor_pairs(rows, step))  7.96 us
    ppermute x1, waiting for transfers between devices, line_reduce(): from_far = lax.ppermute(far, 'col', LINE_SWAP2)  7.22 us
    ppermute x1, waiting for transfers between devices, line_exchange(): ends = lax.ppermute(far, 'col', LINE_OUT)  6.3 us
    pallas_call x1, Pallas kernels, densify(): pl.pallas_call(functools.partial(densify_kernel, capacity // TILE, target...  6.08 us
    pallas_call x3, Pallas kernels, forward_part(): pl.pallas_call(functools.partial(forward_part_kernel, tuple((len(group) f...  5.43 us
    ppermute x2, waiting for transfers between devices, exchange_add(): return value + lax.ppermute(value, axis, xor_pairs(size, step))  4.82 us
    ppermute x1, starting transfers between devices, line_exchange(): far = lax.ppermute(piece, 'col', LINE_SWAP2)  4.1 us
  transfers between devices with their start and end apart: 29, of which 12 were waited for; matrix products, arithmetic and copies ran while one was open for 0% of the time, Pallas kernels for 15%

profile of v7, /device:TPU:0, one launch (start us, length us, event | category | flops | bytes accessed | tf_op | source)
XLA Modules:
  0.0 97.8 jit_solution(3887486382475599341)
XLA Ops:
  1.4 1.0 pad_maximum_fusion.rest_0_
  2.4 4.1 %collective-permute-start = (bf16[528,256]{1,0:T(8,128)(2,1)S(1)}, bf16[528,256]{1,0:T(8,128)(2,1)S(1)}, u32[]{:S(2)}, u32[]{:S(2)}) collective-permute-start(bf16[528,256]{1,0:T(8,128)(2,1)S(1)} %pad_maximum_fusion.rest_0_), channel_id=1, source_target_pairs={{0,4},{1,5},{4,0},{5,1},{2,6},{3,7},{6,2},{7,3},{8,12},{9,13},{12,... | collective-permute-start | bytes 811016 | tf_op jit(solution)/shard_map/ppermute | solution.py:571
  6.5 1.6 %collective-permute-start.2 = (bf16[528,256]{1,0:T(8,128)(2,1)S(1)}, bf16[528,256]{1,0:T(8,128)(2,1)S(1)}, u32[]{:S(2)}, u32[]{:S(2)}) collective-permute-start(bf16[528,256]{1,0:T(8,128)(2,1)S(1)} %pad_maximum_fusion.rest_0_), channel_id=1, source_target_pairs={{0,2},{1,3},{2,0},{3,1},{4,6},{5,7},{6,4},{7,5},{8,10},{9,11},{10,... | collective-permute-start | bytes 811016 | tf_op jit(solution)/shard_map/ppermute | solution.py:572
  9.5 6.1 %densify.1.dense_ref = bf16[2048,2048]{1,0:T(8,128)(2,1)S(1)} custom-call(s32[16,16]{1,0:T(8,128)S(1)} %bitcast.34, s32[16]{0:T(128)S(1)} %bitcast.36, s32[2]{0:T(128)S(1)} %pad_add_fusion.pos_ref, bf16[16,16,128,128]{3,2,1,0:T(8,128)(2,1)} %bitcast.37), custom_call_target="tpu_custom_call" | custom-call | bytes 16777216 | tf_op jit(solution)/shard_map/densify/pallas_call | solution.py:64
  15.6 3.3 %collective-permute-done.rest_4_ = bf16[528,256]{1,0:T(8,128)(2,1)S(1)} collective-permute-done((bf16[528,256]{1,0:T(8,128)(2,1)S(1)}, bf16[528,256]{1,0:T(8,128)(2,1)S(1)}, u32[]{:S(2)}, u32[]{:S(2)}) %collective-permute-start) | collective-permute-done | bytes 270368 | tf_op jit(solution)/shard_map/ppermute | solution.py:571
  19.5 1.3 %collective-permute-start.5 = (bf16[528,256]{1,0:T(8,128)(2,1)S(1)}, bf16[528,256]{1,0:T(8,128)(2,1)S(1)}, u32[]{:S(2)}, u32[]{:S(2)}) collective-permute-start(bf16[528,256]{1,0:T(8,128)(2,1)S(1)} %collective-permute-done.rest_4_), channel_id=1, source_target_pairs={{4,6},{5,7},{2,0},{3,1},{12,14},{13,15},{10,8},{11,9},{20,22},{21,... | collective-permute-start | bytes 811016 | tf_op jit(solution)/shard_map/ppermute | solution.py:576
  21.4 2.6 %forward_part.2 = (f32[2048,256]{1,0:T(8,128)S(1)}, bf16[5,512,256]{2,1,0:T(8,128)(2,1)S(1)}) custom-call(s32[2]{0:T(128)S(1)} %pad_add_fusion.pos_ref, bf16[2048,2048]{1,0:T(8,128)(2,1)S(1)} %densify.1.dense_ref, bf16[528,256]{1,0:T(8,128)(2,1)S(1)} %pad_maximum_fusion.rest_0_, bf16[528,256]{1,0:T(8,128)(2,1)S(1)} %collective-permute-done.1.rest_1_, ...), custom_call_target="tpu_custom_call" | custom-call | flops 1342177280 | bytes 5242880 | tf_op jit(solution)/shard_map/forward_part/pallas_call | solution.py:210
  24.0 6.3 %collective-permute-done.5.rest_2_ = bf16[528,256]{1,0:T(8,128)(2,1)S(1)} collective-permute-done((bf16[528,256]{1,0:T(8,128)(2,1)S(1)}, bf16[528,256]{1,0:T(8,128)(2,1)S(1)}, u32[]{:S(2)}, u32[]{:S(2)}) %collective-permute-start.5) | collective-permute-done | bytes 270368 | tf_op jit(solution)/shard_map/ppermute | solution.py:576
  30.8 1.6 %forward_part.3 = (f32[2048,256]{1,0:T(8,128)S(1)}, bf16[2,512,256]{2,1,0:T(8,128)(2,1)S(1)}) custom-call(s32[2]{0:T(128)S(1)} %pad_add_fusion.pos_ref, bf16[2048,2048]{1,0:T(8,128)(2,1)S(1)} %densify.1.dense_ref, bf16[528,256]{1,0:T(8,128)(2,1)S(1)} %collective-permute-done.8.rest_0_, bf16[528,256]{1,0:T(8,128)(2,1)S(1)} %collective-permute-done.4.rest_1_, ...), custom_call_target="tpu_custom_call" | custom-call | flops 536870912 | bytes 2097152 | tf_op jit(solution)/shard_map/forward_part/pallas_call | solution.py:210
  32.5 1.3 %forward_last.1 = (f32[512,256]{1,0:T(8,128)S(1)}, bf16[512,256]{1,0:T(8,128)(2,1)S(1)}, bf16[512,256]{1,0:T(8,128)(2,1)S(1)}, bf16[512,256]{1,0:T(8,128)(2,1)S(1)}, bf16[1,512,256]{2,1,0:T(8,128)(2,1)S(1)}) custom-call(s32[2]{0:T(128)S(1)} %pad_add_fusion.pos_ref, bf16[2048,2048]{1,0:T(8,128)(2,1)S(1)} %densify.1.dense_ref, ...), custom_call_target="tpu_custom_call" | custom-call | flops 268435456 | bytes 1048576 | tf_op jit(solution)/shard_map/forward_last/pallas_call | solution.py:210
  33.7 1.6 %collective-permute-start.10 = (bf16[512,256]{1,0:T(8,128)(2,1)S(1)}, bf16[512,256]{1,0:T(8,128)(2,1)S(1)}, u32[]{:S(2)}, u32[]{:S(2)}) collective-permute-start(bf16[512,256]{1,0:T(8,128)(2,1)S(1)} %get-tuple-element.63), channel_id=1, source_target_pairs={{0,16},{8,24},{16,0},{24,8},{1,17},{9,25},{17,1},{25,9},{2,18},{10... | collective-permute-start | bytes 786440 | tf_op jit(solution)/shard_map/ppermute | solution.py:592
  35.4 1.4 %collective-permute-start.11 = (bf16[512,256]{1,0:T(8,128)(2,1)S(1)}, bf16[512,256]{1,0:T(8,128)(2,1)S(1)}, u32[]{:S(2)}, u32[]{:S(2)}) collective-permute-start(bf16[512,256]{1,0:T(8,128)(2,1)S(1)} %get-tuple-element.64), channel_id=1, source_target_pairs={{0,24},{8,16},{16,8},{24,0},{1,25},{9,17},{17,9},{25,1},{2,26},{10... | collective-permute-start | bytes 786440 | tf_op jit(solution)/shard_map/ppermute | solution.py:592
  37.3 10.3 %collective-permute-done.10.rest_2_ = bf16[512,256]{1,0:T(8,128)(2,1)S(1)} collective-permute-done((bf16[512,256]{1,0:T(8,128)(2,1)S(1)}, bf16[512,256]{1,0:T(8,128)(2,1)S(1)}, u32[]{:S(2)}, u32[]{:S(2)}) %collective-permute-start.10) | collective-permute-done | bytes 262176 | tf_op jit(solution)/shard_map/ppermute | solution.py:592
  47.6 1.2 %collective-permute-done.9.rest_1_ = bf16[512,256]{1,0:T(8,128)(2,1)S(1)} collective-permute-done((bf16[512,256]{1,0:T(8,128)(2,1)S(1)}, bf16[512,256]{1,0:T(8,128)(2,1)S(1)}, u32[]{:S(2)}, u32[]{:S(2)}) %collective-permute-start.9) | collective-permute-done | bytes 262176 | tf_op jit(solution)/shard_map/ppermute | solution.py:592
  48.9 2.1 %layer.1 = (bf16[512,256]{1,0:T(8,128)(2,1)}, bf16[512,256]{1,0:T(8,128)(2,1)S(1)}, f32[136,256]{1,0:T(8,128)S(1)}, f32[136,256]{1,0:T(8,128)S(1)}) custom-call(s32[2]{0:T(128)S(1)} %pad_add_fusion.pos_ref, bf16[256,256]{1,0:T(8,128)(2,1)S(1)} %copy-done.1, f32[1,256]{1,0:T(1,128)S(1)} %bitcast.35, bf16[512,256]{1,0:T(8,128)(2,1)S(1)} %copy-done, ...), custom_call_target="tpu_custom_call" | custom-call | flops 201326592 | bytes 2621440 | tf_op jit(solution)/shard_map/layer/pallas_call | solution.py:314
  51.0 2.5 %collective-permute-start.14 = (bf16[512,256]{1,0:T(8,128)(2,1)S(1)}, bf16[512,256]{1,0:T(8,128)(2,1)S(1)}, u32[]{:S(2)}, u32[]{:S(2)}) collective-permute-start(bf16[512,256]{1,0:T(8,128)(2,1)S(1)} %get-tuple-element.68.back_ref), channel_id=1, source_target_pairs={{0,24},{8,16},{16,8},{24,0},{1,25},{9,17},{17,9},{25,1},{2,26},{10... | collective-permute-start | bytes 786440 | tf_op jit(solution)/shard_map/ppermute | solution.py:592
  53.5 1.5 %collective-permute-start.16 = (f32[136,256]{1,0:T(8,128)S(1)}, f32[136,256]{1,0:T(8,128)S(1)}, u32[]{:S(2)}, u32[]{:S(2)}) collective-permute-start(f32[136,256]{1,0:T(8,128)S(1)} %add.23), channel_id=1, source_target_pairs={{0,4},{1,5},{2,6},{3,7},{4,0},{5,1},{6,2},{7,3},{8,12},{9,13},{10,... | collective-permute-start | bytes 417800 | tf_op jit(solution)/shard_map/ppermute | solution.py:601
  55.5 1.4 %collective-permute-start.13 = (bf16[512,256]{1,0:T(8,128)(2,1)S(1)}, bf16[512,256]{1,0:T(8,128)(2,1)S(1)}, u32[]{:S(2)}, u32[]{:S(2)}) collective-permute-start(bf16[512,256]{1,0:T(8,128)(2,1)S(1)} %get-tuple-element.68.back_ref), channel_id=1, source_target_pairs={{0,16},{8,24},{16,0},{24,8},{1,17},{9,25},{17,1},{25,9},{2,18},{10... | collective-permute-start | bytes 786440 | tf_op jit(solution)/shard_map/ppermute | solution.py:592
  56.9 4.1 %collective-permute-done.14.rest_5_ = bf16[512,256]{1,0:T(8,128)(2,1)S(1)} collective-permute-done((bf16[512,256]{1,0:T(8,128)(2,1)S(1)}, bf16[512,256]{1,0:T(8,128)(2,1)S(1)}, u32[]{:S(2)}, u32[]{:S(2)}) %collective-permute-start.14) | collective-permute-done | bytes 262176 | tf_op jit(solution)/shard_map/ppermute | solution.py:592
  61.0 2.2 %collective-permute-done.16 = f32[136,256]{1,0:T(8,128)S(1)} collective-permute-done((f32[136,256]{1,0:T(8,128)S(1)}, f32[136,256]{1,0:T(8,128)S(1)}, u32[]{:S(2)}, u32[]{:S(2)}) %collective-permute-start.16) | collective-permute-done | bytes 139296 | tf_op jit(solution)/shard_map/ppermute | solution.py:601
  64.1 4.2 %collective-permute-done.17 = f32[136,256]{1,0:T(8,128)S(1)} collective-permute-done((f32[136,256]{1,0:T(8,128)S(1)}, f32[136,256]{1,0:T(8,128)S(1)}, u32[]{:S(2)}, u32[]{:S(2)}) %collective-permute-start.17) | collective-permute-done | bytes 139296 | tf_op jit(solution)/shard_map/ppermute | solution.py:560
  68.4 1.0 %backward_late.2 = (f32[512,256]{1,0:T(8,128)S(1)}, bf16[512,256]{1,0:T(8,128)(2,1)S(1)}) custom-call(bf16[2048,2048]{1,0:T(8,128)(2,1)S(1)} %densify.1.dense_ref, bf16[2,512,256]{2,1,0:T(8,128)(2,1)S(1)} %get-tuple-element.66.rest_0_.rest_1_, bf16[1,512,256]{2,1,0:T(8,128)(2,1)S(1)} %get-tuple-element.67.rest_1_, f32[2048,256]{1,0:T(8,128)S(1)} %backward_early.1.rest_2_, ...), custom_call_target="tpu_custom_call" | custom-call | flops 536870912 | bytes 2097152 | tf_op jit(solution)/shard_map/backward_late/pallas_call | solution.py:409
  69.5 2.5 %backward_late.3 = (f32[512,256]{1,0:T(8,128)S(1)}, bf16[512,256]{1,0:T(8,128)(2,1)S(1)}, f32[512,256]{1,0:T(8,128)S(1)}, bf16[512,256]{1,0:T(8,128)(2,1)S(1)}, ...) custom-call(bf16[2048,2048]{1,0:T(8,128)(2,1)S(1)} %densify.1.dense_ref, ...), custom_call_target="tpu_custom_call" | custom-call | flops 1610612736 | bytes 6291456 | tf_op jit(solution)/shard_map/backward_late/pallas_call | solution.py:409
  72.7 2.1 %collective-permute-start.26 = (bf16[512,256]{1,0:T(8,128)(2,1)S(1)}, bf16[512,256]{1,0:T(8,128)(2,1)S(1)}, u32[]{:S(2)}, u32[]{:S(2)}) collective-permute-start(bf16[512,256]{1,0:T(8,128)(2,1)S(1)} %pair_sums.3), channel_id=1, source_target_pairs={{6,4},{7,5},{0,2},{1,3},{14,12},{15,13},{8,10},{9,11},{22,20},{23,... | collective-permute-start | bytes 786440 | tf_op jit(solution)/shard_map/ppermute | solution.py:614
  76.4 3.0 %collective-permute-start.24 = (bf16[512,256]{1,0:T(8,128)(2,1)S(1)}, bf16[512,256]{1,0:T(8,128)(2,1)S(1)}, u32[]{:S(2)}, u32[]{:S(2)}) collective-permute-start(bf16[512,256]{1,0:T(8,128)(2,1)S(1)} %get-tuple-element.92), channel_id=1, source_target_pairs={{0,2},{1,3},{2,0},{3,1},{4,6},{5,7},{6,4},{7,5},{8,10},{9,11},{10,... | collective-permute-start | bytes 786440 | tf_op jit(solution)/shard_map/ppermute | solution.py:618
  79.5 1.6 %collective-permute-done.22 = f32[136,256]{1,0:T(8,128)S(1)} collective-permute-done((f32[136,256]{1,0:T(8,128)S(1)}, f32[136,256]{1,0:T(8,128)S(1)}, u32[]{:S(2)}, u32[]{:S(2)}) %collective-permute-start.22) | collective-permute-done | bytes 139296 | tf_op jit(solution)/shard_map/ppermute | solution.py:608
  81.7 3.9 %collective-permute-start.27 = (bf16[512,256]{1,0:T(8,128)(2,1)S(1)}, bf16[512,256]{1,0:T(8,128)(2,1)S(1)}, u32[]{:S(2)}, u32[]{:S(2)}) collective-permute-start(bf16[512,256]{1,0:T(8,128)(2,1)S(1)} %triple_sum.1), channel_id=1, source_target_pairs={{0,4},{1,5},{4,0},{5,1},{2,6},{3,7},{6,2},{7,3},{8,12},{9,13},{12,... | collective-permute-start | bytes 786440 | tf_op jit(solution)/shard_map/ppermute | solution.py:625
  86.3 0.8 collective-permute-done.24.refs_2_
  87.1 1.4 %collective-permute-done.28.theirs_ref = f32[136,256]{1,0:T(8,128)S(1)} collective-permute-done((f32[136,256]{1,0:T(8,128)S(1)}, f32[136,256]{1,0:T(8,128)S(1)}, u32[]{:S(2)}, u32[]{:S(2)}) %collective-permute-start.28) | collective-permute-done | bytes 139296 | tf_op jit(solution)/shard_map/ppermute | solution.py:702
  88.4 1.3 %assemble.1 = (f32[256,256]{1,0:T(8,128)}, f32[1,256]{1,0:T(1,128)}) custom-call(s32[2]{0:T(128)S(1)} %pad_add_fusion.pos_ref, f32[136,256]{1,0:T(8,128)S(1)} %add.27.mine_ref, f32[136,256]{1,0:T(8,128)S(1)} %collective-permute-done.28.theirs_ref), custom_call_target="tpu_custom_call" | custom-call | bytes 1048576 | tf_op jit(solution)/shard_map/assemble/pallas_call | solution.py:342
  89.7 7.2 %collective-permute-done.27.refs_3_ = bf16[512,256]{1,0:T(8,128)(2,1)S(1)} collective-permute-done((bf16[512,256]{1,0:T(8,128)(2,1)S(1)}, bf16[512,256]{1,0:T(8,128)(2,1)S(1)}, u32[]{:S(2)}, u32[]{:S(2)}) %collective-permute-start.27) | collective-permute-done | bytes 262176 | tf_op jit(solution)/shard_map/ppermute | solution.py:625
  96.9 0.8 finish.1
  (57 shorter events, 9.5 us)
Async XLA Ops:
  2.4 16.5 %collective-permute-start = (bf16[528,256]{1,0:T(8,128)(2,1)S(1)}, bf16[528,256]{1,0:T(8,128)(2,1)S(1)}, u32[]{:S(2)}, u32[]{:S(2)}) collective-permute-start(bf16[528,256]{1,0:T(8,128)(2,1)S(1)} %pad_maximum_fusion.rest_0_), channel_id=1, source_target_pairs={{0,4},{1,5},{4,0},{5,1},{2,6},{3,7},{6,2},{7,3},{8,12},{9,13},{12,... | collective-permute-start | bytes 811016 | tf_op jit(solution)/shard_map/ppermute | solution.py:571
  6.5 14.4 %collective-permute-start.2 = (bf16[528,256]{1,0:T(8,128)(2,1)S(1)}, bf16[528,256]{1,0:T(8,128)(2,1)S(1)}, u32[]{:S(2)}, u32[]{:S(2)}) collective-permute-start(bf16[528,256]{1,0:T(8,128)(2,1)S(1)} %pad_maximum_fusion.rest_0_), channel_id=1, source_target_pairs={{0,2},{1,3},{2,0},{3,1},{4,6},{5,7},{6,4},{7,5},{8,10},{9,11},{10,... | collective-permute-start | bytes 811016 | tf_op jit(solution)/shard_map/ppermute | solution.py:572
  8.1 13.4 %collective-permute-start.1 = (bf16[528,256]{1,0:T(8,128)(2,1)S(1)}, bf16[528,256]{1,0:T(8,128)(2,1)S(1)}, u32[]{:S(2)}, u32[]{:S(2)}) collective-permute-start(bf16[528,256]{1,0:T(8,128)(2,1)S(1)} %pad_maximum_fusion.rest_0_), channel_id=1, source_target_pairs={{0,1},{1,0},{2,3},{3,2},{4,5},{5,4},{6,7},{7,6},{8,9},{9,8},{10,11... | collective-permute-start | bytes 811016 | tf_op jit(solution)/shard_map/ppermute | solution.py:573
  18.9 2.6 %collective-permute-start.3 = (bf16[528,256]{1,0:T(8,128)(2,1)S(1)}, bf16[528,256]{1,0:T(8,128)(2,1)S(1)}, u32[]{:S(2)}, u32[]{:S(2)}) collective-permute-start(bf16[528,256]{1,0:T(8,128)(2,1)S(1)} %collective-permute-done.rest_4_), channel_id=1, source_target_pairs={{0,1},{1,0},{2,3},{3,2},{4,5},{5,4},{6,7},{7,6},{8,9},{9,8},{10,11... | collective-permute-start | bytes 811016 | tf_op jit(solution)/shard_map/ppermute | solution.py:578
  18.9 5.2 %collective-permute-start.4 = (bf16[528,256]{1,0:T(8,128)(2,1)S(1)}, bf16[528,256]{1,0:T(8,128)(2,1)S(1)}, u32[]{:S(2)}, u32[]{:S(2)}) collective-permute-start(bf16[528,256]{1,0:T(8,128)(2,1)S(1)} %pad_maximum_fusion.rest_0_), channel_id=1, source_target_pairs={{2,4},{3,5},{4,2},{5,3},{10,12},{11,13},{12,10},{13,11},{18,20},{1... | collective-permute-start | bytes 811016 | tf_op jit(solution)/shard_map/ppermute | solution.py:577
  19.5 10.8 %collective-permute-start.5 = (bf16[528,256]{1,0:T(8,128)(2,1)S(1)}, bf16[528,256]{1,0:T(8,128)(2,1)S(1)}, u32[]{:S(2)}, u32[]{:S(2)}) collective-permute-start(bf16[528,256]{1,0:T(8,128)(2,1)S(1)} %collective-permute-done.rest_4_), channel_id=1, source_target_pairs={{4,6},{5,7},{2,0},{3,1},{12,14},{13,15},{10,8},{11,9},{20,22},{21,... | collective-permute-start | bytes 811016 | tf_op jit(solution)/shard_map/ppermute | solution.py:576
  20.8 10.0 %collective-permute-start.8 = (bf16[528,256]{1,0:T(8,128)(2,1)S(1)}, bf16[528,256]{1,0:T(8,128)(2,1)S(1)}, u32[]{:S(2)}, u32[]{:S(2)}) collective-permute-start(bf16[528,256]{1,0:T(8,128)(2,1)S(1)} %collective-permute-done.2.rest_2_), channel_id=1, source_target_pairs={{0,1},{1,0},{2,3},{3,2},{4,5},{5,4},{6,7},{7,6},{8,9},{9,8},{10,11... | collective-permute-start | bytes 811016 | tf_op jit(solution)/shard_map/ppermute | solution.py:582
  30.3 2.1 %collective-permute-start.6 = (bf16[528,256]{1,0:T(8,128)(2,1)S(1)}, bf16[528,256]{1,0:T(8,128)(2,1)S(1)}, u32[]{:S(2)}, u32[]{:S(2)}) collective-permute-start(bf16[528,256]{1,0:T(8,128)(2,1)S(1)} %collective-permute-done.4.rest_1_), channel_id=1, source_target_pairs={{0,1},{1,0},{2,3},{3,2},{4,5},{5,4},{6,7},{7,6},{8,9},{9,8},{10,11... | collective-permute-start | bytes 811016 | tf_op jit(solution)/shard_map/ppermute | solution.py:581
  30.3 2.1 %collective-permute-start.7 = (bf16[528,256]{1,0:T(8,128)(2,1)S(1)}, bf16[528,256]{1,0:T(8,128)(2,1)S(1)}, u32[]{:S(2)}, u32[]{:S(2)}) collective-permute-start(bf16[528,256]{1,0:T(8,128)(2,1)S(1)} %collective-permute-done.5.rest_2_), channel_id=1, source_target_pairs={{0,1},{1,0},{2,3},{3,2},{4,5},{5,4},{6,7},{7,6},{8,9},{9,8},{10,11... | collective-permute-start | bytes 811016 | tf_op jit(solution)/shard_map/ppermute | solution.py:581
  32.4 16.4 %copy-start = (bf16[512,256]{1,0:T(8,128)(2,1)S(1)}, bf16[512,256]{1,0:T(8,128)(2,1)}, u32[]{:S(2)}) copy-start(bf16[512,256]{1,0:T(8,128)(2,1)} %cot_ref.1) | copy-start | bytes 786436
  32.4 16.4 %copy-start.1 = (bf16[256,256]{1,0:T(8,128)(2,1)S(1)}, bf16[256,256]{1,0:T(8,128)(2,1)}, u32[]{:S(2)}) copy-start(bf16[256,256]{1,0:T(8,128)(2,1)} %weight_ref.1) | copy-start | bytes 393220
  32.5 16.4 %copy-start.3 = (f32[256]{0:T(256)S(1)}, f32[256]{0:T(256)}, u32[]{:S(2)}) copy-start(f32[256]{0:T(256)} %param.11) | copy-start | bytes 3076
  33.7 13.9 %collective-permute-start.10 = (bf16[512,256]{1,0:T(8,128)(2,1)S(1)}, bf16[512,256]{1,0:T(8,128)(2,1)S(1)}, u32[]{:S(2)}, u32[]{:S(2)}) collective-permute-start(bf16[512,256]{1,0:T(8,128)(2,1)S(1)} %get-tuple-element.63), channel_id=1, source_target_pairs={{0,16},{8,24},{16,0},{24,8},{1,17},{9,25},{17,1},{25,9},{2,18},{10... | collective-permute-start | bytes 786440 | tf_op jit(solution)/shard_map/ppermute | solution.py:592
  35.4 12.3 %collective-permute-start.11 = (bf16[512,256]{1,0:T(8,128)(2,1)S(1)}, bf16[512,256]{1,0:T(8,128)(2,1)S(1)}, u32[]{:S(2)}, u32[]{:S(2)}) collective-permute-start(bf16[512,256]{1,0:T(8,128)(2,1)S(1)} %get-tuple-element.64), channel_id=1, source_target_pairs={{0,24},{8,16},{16,8},{24,0},{1,25},{9,17},{17,9},{25,1},{2,26},{10... | collective-permute-start | bytes 786440 | tf_op jit(solution)/shard_map/ppermute | solution.py:592
  36.8 12.1 %collective-permute-start.9 = (bf16[512,256]{1,0:T(8,128)(2,1)S(1)}, bf16[512,256]{1,0:T(8,128)(2,1)S(1)}, u32[]{:S(2)}, u32[]{:S(2)}) collective-permute-start(bf16[512,256]{1,0:T(8,128)(2,1)S(1)} %get-tuple-element.62), channel_id=1, source_target_pairs={{0,8},{8,0},{16,24},{24,16},{1,9},{9,1},{17,25},{25,17},{2,10},{10... | collective-permute-start | bytes 786440 | tf_op jit(solution)/shard_map/ppermute | solution.py:592
  51.0 2.5 %collective-permute-start.15 = (f32[136,256]{1,0:T(8,128)S(1)}, f32[136,256]{1,0:T(8,128)S(1)}, u32[]{:S(2)}, u32[]{:S(2)}) collective-permute-start(f32[136,256]{1,0:T(8,128)S(1)} %get-tuple-element.70), channel_id=1, source_target_pairs={{0,1},{1,0},{2,3},{3,2},{4,5},{5,4},{6,7},{7,6},{8,9},{9,8},{10,11... | collective-permute-start | bytes 417800 | tf_op jit(solution)/shard_map/ppermute | solution.py:681
  51.0 10.0 %collective-permute-start.14 = (bf16[512,256]{1,0:T(8,128)(2,1)S(1)}, bf16[512,256]{1,0:T(8,128)(2,1)S(1)}, u32[]{:S(2)}, u32[]{:S(2)}) collective-permute-start(bf16[512,256]{1,0:T(8,128)(2,1)S(1)} %get-tuple-element.68.back_ref), channel_id=1, source_target_pairs={{0,24},{8,16},{16,8},{24,0},{1,25},{9,17},{17,9},{25,1},{2,26},{10... | collective-permute-start | bytes 786440 | tf_op jit(solution)/shard_map/ppermute | solution.py:592
  53.5 9.8 %collective-permute-start.16 = (f32[136,256]{1,0:T(8,128)S(1)}, f32[136,256]{1,0:T(8,128)S(1)}, u32[]{:S(2)}, u32[]{:S(2)}) collective-permute-start(f32[136,256]{1,0:T(8,128)S(1)} %add.23), channel_id=1, source_target_pairs={{0,4},{1,5},{2,6},{3,7},{4,0},{5,1},{6,2},{7,3},{8,12},{9,13},{10,... | collective-permute-start | bytes 417800 | tf_op jit(solution)/shard_map/ppermute | solution.py:601
  55.0 13.4 %collective-permute-start.12 = (bf16[512,256]{1,0:T(8,128)(2,1)S(1)}, bf16[512,256]{1,0:T(8,128)(2,1)S(1)}, u32[]{:S(2)}, u32[]{:S(2)}) collective-permute-start(bf16[512,256]{1,0:T(8,128)(2,1)S(1)} %get-tuple-element.68.back_ref), channel_id=1, source_target_pairs={{0,8},{8,0},{16,24},{24,16},{1,9},{9,1},{17,25},{25,17},{2,10},{10... | collective-permute-start | bytes 786440 | tf_op jit(solution)/shard_map/ppermute | solution.py:592
  55.5 12.9 %collective-permute-start.13 = (bf16[512,256]{1,0:T(8,128)(2,1)S(1)}, bf16[512,256]{1,0:T(8,128)(2,1)S(1)}, u32[]{:S(2)}, u32[]{:S(2)}) collective-permute-start(bf16[512,256]{1,0:T(8,128)(2,1)S(1)} %get-tuple-element.68.back_ref), channel_id=1, source_target_pairs={{0,16},{8,24},{16,0},{24,8},{1,17},{9,25},{17,1},{25,9},{2,18},{10... | collective-permute-start | bytes 786440 | tf_op jit(solution)/shard_map/ppermute | solution.py:592
  63.3 5.1 %collective-permute-start.17 = (f32[136,256]{1,0:T(8,128)S(1)}, f32[136,256]{1,0:T(8,128)S(1)}, u32[]{:S(2)}, u32[]{:S(2)}) collective-permute-start(f32[136,256]{1,0:T(8,128)S(1)} %add.24), channel_id=1, source_target_pairs={{0,2},{1,3},{2,0},{3,1},{4,6},{5,7},{6,4},{7,5},{8,10},{9,11},{10,... | collective-permute-start | bytes 417800 | tf_op jit(solution)/shard_map/ppermute | solution.py:560
  69.5 2.6 %collective-permute-start.18 = (bf16[512,256]{1,0:T(8,128)(2,1)S(1)}, bf16[512,256]{1,0:T(8,128)(2,1)S(1)}, u32[]{:S(2)}, u32[]{:S(2)}) collective-permute-start(bf16[512,256]{1,0:T(8,128)(2,1)S(1)} %get-tuple-element.76), channel_id=1, source_target_pairs={{0,1},{1,0},{2,3},{3,2},{4,5},{5,4},{6,7},{7,6},{8,9},{9,8},{10,11... | collective-permute-start | bytes 786440 | tf_op jit(solution)/shard_map/ppermute | solution.py:607
  72.0 3.6 %collective-permute-start.19 = (bf16[512,256]{1,0:T(8,128)(2,1)S(1)}, bf16[512,256]{1,0:T(8,128)(2,1)S(1)}, u32[]{:S(2)}, u32[]{:S(2)}) collective-permute-start(bf16[512,256]{1,0:T(8,128)(2,1)S(1)} %get-tuple-element.84), channel_id=1, source_target_pairs={{0,1},{1,0},{2,3},{3,2},{4,5},{5,4},{6,7},{7,6},{8,9},{9,8},{10,11... | collective-permute-start | bytes 786440 | tf_op jit(solution)/shard_map/ppermute | solution.py:616
  72.6 3.7 %collective-permute-start.20 = (bf16[512,256]{1,0:T(8,128)(2,1)S(1)}, bf16[512,256]{1,0:T(8,128)(2,1)S(1)}, u32[]{:S(2)}, u32[]{:S(2)}) collective-permute-start(bf16[512,256]{1,0:T(8,128)(2,1)S(1)} %get-tuple-element.85), channel_id=1, source_target_pairs={{0,1},{1,0},{2,3},{3,2},{4,5},{5,4},{6,7},{7,6},{8,9},{9,8},{10,11... | collective-permute-start | bytes 786440 | tf_op jit(solution)/shard_map/ppermute | solution.py:616
  72.7 8.9 %collective-permute-start.26 = (bf16[512,256]{1,0:T(8,128)(2,1)S(1)}, bf16[512,256]{1,0:T(8,128)(2,1)S(1)}, u32[]{:S(2)}, u32[]{:S(2)}) collective-permute-start(bf16[512,256]{1,0:T(8,128)(2,1)S(1)} %pair_sums.3), channel_id=1, source_target_pairs={{6,4},{7,5},{0,2},{1,3},{14,12},{15,13},{8,10},{9,11},{22,20},{23,... | collective-permute-start | bytes 786440 | tf_op jit(solution)/shard_map/ppermute | solution.py:614
  74.9 6.8 %collective-permute-start.25 = (bf16[512,256]{1,0:T(8,128)(2,1)S(1)}, bf16[512,256]{1,0:T(8,128)(2,1)S(1)}, u32[]{:S(2)}, u32[]{:S(2)}) collective-permute-start(bf16[512,256]{1,0:T(8,128)(2,1)S(1)} %get-tuple-element.94), channel_id=1, source_target_pairs={{0,1},{1,0},{2,3},{3,2},{4,5},{5,4},{6,7},{7,6},{8,9},{9,8},{10,11... | collective-permute-start | bytes 786440 | tf_op jit(solution)/shard_map/ppermute | solution.py:616
  75.1 5.9 %collective-permute-start.22 = (f32[136,256]{1,0:T(8,128)S(1)}, f32[136,256]{1,0:T(8,128)S(1)}, u32[]{:S(2)}, u32[]{:S(2)}) collective-permute-start(f32[136,256]{1,0:T(8,128)S(1)} %add.25), channel_id=1, source_target_pairs={{0,8},{8,0},{16,24},{24,16},{1,9},{9,1},{17,25},{25,17},{2,10},{10... | collective-permute-start | bytes 417800 | tf_op jit(solution)/shard_map/ppermute | solution.py:608
  75.6 10.6 %collective-permute-start.21 = (bf16[512,256]{1,0:T(8,128)(2,1)S(1)}, bf16[512,256]{1,0:T(8,128)(2,1)S(1)}, u32[]{:S(2)}, u32[]{:S(2)}) collective-permute-start(bf16[512,256]{1,0:T(8,128)(2,1)S(1)} %pair_sums.3), channel_id=1, source_target_pairs={{2,4},{3,5},{4,2},{5,3},{10,12},{11,13},{12,10},{13,11},{18,20},{1... | collective-permute-start | bytes 786440 | tf_op jit(solution)/shard_map/ppermute | solution.py:615
  76.4 10.7 %collective-permute-start.24 = (bf16[512,256]{1,0:T(8,128)(2,1)S(1)}, bf16[512,256]{1,0:T(8,128)(2,1)S(1)}, u32[]{:S(2)}, u32[]{:S(2)}) collective-permute-start(bf16[512,256]{1,0:T(8,128)(2,1)S(1)} %get-tuple-element.92), channel_id=1, source_target_pairs={{0,2},{1,3},{2,0},{3,1},{4,6},{5,7},{6,4},{7,5},{8,10},{9,11},{10,... | collective-permute-start | bytes 786440 | tf_op jit(solution)/shard_map/ppermute | solution.py:618
  81.0 5.2 %collective-permute-start.23 = (f32[136,256]{1,0:T(8,128)S(1)}, f32[136,256]{1,0:T(8,128)S(1)}, u32[]{:S(2)}, u32[]{:S(2)}) collective-permute-start(f32[136,256]{1,0:T(8,128)S(1)} %add.26), channel_id=1, source_target_pairs={{0,16},{8,24},{16,0},{24,8},{1,17},{9,25},{17,1},{25,9},{2,18},{10... | collective-permute-start | bytes 417800 | tf_op jit(solution)/shard_map/ppermute | solution.py:560
  81.7 15.2 %collective-permute-start.27 = (bf16[512,256]{1,0:T(8,128)(2,1)S(1)}, bf16[512,256]{1,0:T(8,128)(2,1)S(1)}, u32[]{:S(2)}, u32[]{:S(2)}) collective-permute-start(bf16[512,256]{1,0:T(8,128)(2,1)S(1)} %triple_sum.1), channel_id=1, source_target_pairs={{0,4},{1,5},{4,0},{5,1},{2,6},{3,7},{6,2},{7,3},{8,12},{9,13},{12,... | collective-permute-start | bytes 786440 | tf_op jit(solution)/shard_map/ppermute | solution.py:625
  87.1 1.4 %collective-permute-start.28 = (f32[136,256]{1,0:T(8,128)S(1)}, f32[136,256]{1,0:T(8,128)S(1)}, u32[]{:S(2)}, u32[]{:S(2)}) collective-permute-start(f32[136,256]{1,0:T(8,128)S(1)} %add.27.mine_ref), channel_id=1, source_target_pairs={{0,1},{1,0},{2,3},{3,2},{4,5},{5,4},{6,7},{7,6},{8,9},{9,8},{10,11... | collective-permute-start | bytes 417800 | tf_op jit(solution)/shard_map/ppermute | solution.py:702
  (2 other events, 1.4 us)
